TPU v7x, 32 devices: a whole 2x2x4 slice. The times are simulated.
32 devices in a mesh: gx: 8 (over y, x, core), gy: 4 (over z).
Axes of the slice: x: 2, y: 2, z: 4, core: 2. Of those that a mesh axis runs over, the one named last changes fastest.
Arguments:
- checkpoint: float32 [19, 32, 64, 256], P(None, 'gx', 'gy'), may hold values from 0 to 1, as said below
- adjoint_end: float32 [19, 32, 64, 256], P(None, 'gx', 'gy'), may hold values from -6 to 6
- resistance: float32 [32, 64, 256], P('gx', 'gy'), may hold values from 0 to 0.4
- solid_mask: int32 [32, 64, 256], P('gx', 'gy'), may hold values 0 or 1
- flags: int32 [32, 64, 256], P('gx', 'gy'), may hold values from 0 to 2
Outputs:
- adjoint_start: float32 [19, 32, 64, 256], P(None, 'gx', 'gy')
- sensitivity: float32 [32, 64, 256], P('gx', 'gy')
Inputs may be any that keep to these rules, and one draw needn't show every extreme that they name: `checkpoint`: every population is positive.
All inputs are finite; a program needn't handle non-finite values. No bound on the sum of `solid_mask` on one device may be relied on, other than what follows from the above.
Results may differ from a plain program's by a relative error of at most 0.0003.
Values sent between devices are 32-bit elements; how exact they have to be, the bound alone decides.
No kernel may reach another device: no remote copies, remote signals or barrier semaphores. Data moves between devices by JAX's collectives and lax.ppermute only.
A program may use at most 128 MiB of HBM per device.

v0:
```python
import jax
import jax.numpy as jnp
from jax import lax
from jax.experimental import pallas as pl
from jax.experimental.pallas import tpu as pltpu
from jax.sharding import PartitionSpec as P

VELOCITY = (
    (0, 0, 0),
    (1, 0, 0),
    (-1, 0, 0),
    (0, 1, 0),
    (0, -1, 0),
    (0, 0, 1),
    (0, 0, -1),
    (1, 1, 0),
    (-1, -1, 0),
    (1, -1, 0),
    (-1, 1, 0),
    (1, 0, 1),
    (-1, 0, -1),
    (1, 0, -1),
    (-1, 0, 1),
    (0, 1, 1),
    (0, -1, -1),
    (0, 1, -1),
    (0, -1, 1),
)


def pair_sums(f):
    even = [f[2 * k + 1] + f[2 * k + 2] for k in range(9)]
    odd = [f[2 * k + 1] - f[2 * k + 2] for k in range(9)]
    return even, odd


def grouped(f):
    even, odd = pair_sums(f)
    faces = even[:3]
    planes = [even[7] + even[8], even[5] + even[6], even[3] + even[4]]
    shears = [even[7] - even[8], even[5] - even[6], even[3] - even[4]]
    axes = [
        (odd[0], odd[3] + odd[4], odd[5] + odd[6]),
        (odd[1], odd[3] - odd[4], odd[7] + odd[8]),
        (odd[2], odd[5] - odd[6], odd[7] - odd[8]),
    ]
    return faces, planes, shears, axes, odd


def half_pairs(faces, planes, shears, axes):
    even = [0.5 * v for v in faces]
    for a in (2, 1, 0):
        even += [0.25 * (planes[a] + shears[a]), 0.25 * (planes[a] - shears[a])]
    odd = [0.5 * axes[a][0] for a in range(3)]
    for one, two in ((axes[0][1], axes[1][1]), (axes[0][2], axes[2][1]), (axes[1][2], axes[2][2])):
        odd += [0.25 * (one + two), 0.25 * (one - two)]
    return even, odd


def finish(rest, f, odd_sums, even, odd, grey, free):
    out = [f[0] - free * rest]
    for k in range(9):
        e = free * even[k]
        o = free * odd[k] + grey * odd_sums[k]
        out += [f[2 * k + 1] - (e + o), f[2 * k + 2] - (e - o)]
    return out


def collide_tile(f, grey, rate):
    faces, planes, shears, axes, odd_sums = grouped(f)
    total = faces[0] + faces[1] + faces[2]
    edges = planes[0] + planes[1] + planes[2]
    momentum = [d + a + b for d, a, b in axes]
    inverse = 1.0 / (f[0] + total + edges)
    u = [m * inverse for m in momentum]
    q = [m * v for m, v in zip(momentum, u)]
    q_all = q[0] + q[1] + q[2]
    energy = (1.19 * 19.0 / 2394.0) * (edges - f[0] - q_all)
    square = (1.4 / 252.0) * (9.0 * f[0] - 7.0 * total - 2.0 * edges + 5.5 * q_all)
    rest = 12.0 * square - 30.0 * energy
    d_total = -22.0 * energy - 8.0 * square
    d_edges = 32.0 * energy + 4.0 * square
    d_faces, d_planes = [], []
    for a in range(3):
        x = 3.0 * faces[a] - total
        y = edges - 3.0 * planes[a]
        eq = 3.0 * q[a] - q_all
        stress = rate * (x + y - eq)
        other = 1.4 * (y - 2.0 * x + 0.5 * eq)
        d_faces.append(d_total + (1.0 / 9.0) * (stress - other))
        d_planes.append(d_edges - (1.0 / 9.0) * (2.0 * stress + other))
    d_shears = [
        rate * (shears[0] - momentum[1] * u[2]),
        rate * (shears[1] - momentum[0] * u[2]),
        rate * (shears[2] - momentum[0] * u[1]),
    ]
    d_axes = []
    for d, a, b in axes:
        t = 0.2 * (a + b - 2.0 * d)
        v = 0.99 * (a - b)
        d_axes.append((-2.0 * t, t + v, t - v))
    even, odd = half_pairs(d_faces, d_planes, d_shears, d_axes)
    return finish(rest, f, odd_sums, even, odd, grey, 1.0 - grey)


def adjoint_tile(lam, f, grey, rate):
    f_faces, f_planes, f_shears, f_axes, _ = grouped(f)
    momentum = [d + a + b for d, a, b in f_axes]
    density = f[0] + (f_faces[0] + f_faces[1] + f_faces[2]) + (f_planes[0] + f_planes[1] + f_planes[2])
    inverse = 1.0 / density
    u = [m * inverse for m in momentum]
    faces, planes, shears, axes, odd_sums = grouped(lam)
    total = faces[0] + faces[1] + faces[2]
    edges = planes[0] + planes[1] + planes[2]
    energy = (1.19 / 2394.0) * (8.0 * edges - 11.0 * total - 30.0 * lam[0])
    square = (1.4 / 252.0) * (edges - 4.0 * total + 12.0 * lam[0])
    bulk = 19.0 * energy - 5.5 * square
    weights, w_faces, w_planes, slopes, w_axes = [], [], [], [], []
    w_total = -22.0 * energy - 8.0 * square
    w_edges = 32.0 * energy + 4.0 * square
    for a in range(3):
        x = 3.0 * faces[a] - total
        y = edges - 3.0 * planes[a]
        stress = rate * (x + y)
        other = 1.4 * (y - 2.0 * x)
        w_faces.append(w_total + (1.0 / 9.0) * (stress - other))
        w_planes.append(w_edges - (1.0 / 9.0) * (2.0 * stress + other))
        weights.append(2.0 * bulk + (1.0 / 9.0) * stress - (1.0 / 36.0) * other)
    w_shears = [rate * v for v in shears]
    cross = [0.25 * v for v in w_shears]
    pull = [
        weights[0] * u[0] + cross[2] * u[1] + cross[1] * u[2],
        weights[1] * u[1] + cross[2] * u[0] + cross[0] * u[2],
        weights[2] * u[2] + cross[1] * u[0] + cross[0] * u[1],
    ]
    by_density = 3.0 * square - 11.0 * energy - 0.5 * (u[0] * pull[0] + u[1] * pull[1] + u[2] * pull[2])
    for a in range(3):
        d, p, r = axes[a]
        flux = p + r - 4.0 * d
        v = 0.99 * (p - r)
        slope = pull[a] - 0.02 * flux
        t = 0.12 * flux - 4.0 * slope
        w_axes.append((-0.24 * flux - 2.0 * slope, t + v, t - v))
    rest = 12.0 * square - 30.0 * energy - by_density
    w_faces = [v - 2.0 * by_density for v in w_faces]
    w_planes = [v - 4.0 * by_density for v in w_planes]
    even, odd = half_pairs(w_faces, w_planes, w_shears, w_axes)
    out = finish(rest, lam, odd_sums, even, odd, grey, 1.0 - grey)
    near = rest * f[0]
    far = 0.0
    for a in range(3):
        near += 0.5 * (w_faces[a] * f_faces[a])
        far += w_planes[a] * f_planes[a] + w_shears[a] * f_shears[a]
        (wd, wa, wb), (d, p, r), (ld, lp, lr) = w_axes[a], f_axes[a], axes[a]
        near += (0.5 * wd - ld) * d
        far += (wa - 2.0 * lp) * p + (wb - 2.0 * lr) * r
    return out, near + 0.25 * far


def greyness(resistance, solid):
    return jnp.where(solid == 1, 1.0, resistance)


def shear_rate(flags):
    return jnp.where(flags == 0, 1.25, jnp.where(flags == 1, 0.9, 1.7))


def moving(sign, dim, step):
    return [i for i in range(19) if sign * VELOCITY[i][dim] == step]


def near_plane(field, step, i):
    sign = 1 - 2 * field
    return 19 * field + (moving(sign, 1, 0) + moving(sign, 1, step)).index(i)


def edge_plane(field, step, i):
    return 19 * field + 14 + moving(1 - 2 * field, 1, step).index(i)


def shifted_y(block, step, below, above):
    rows = block.shape[0]
    if step == 0:
        return block
    row = lax.broadcasted_iota(jnp.int32, block.shape, 0)
    if step == 1:
        return jnp.where(row == 0, below, pltpu.roll(block, 1, 0))
    return jnp.where(row == rows - 1, above, pltpu.roll(block, rows - 1, 0))


def shifted_z(block, step):
    return pltpu.roll(block, step % block.shape[1], 1) if step else block


def post_kernel(state, adjoint, resistance, solid, flags, post, up, down):
    nx, ny, nz = resistance.shape
    tiles = ny // 8

    def step(n, carry):
        x, rows = n // tiles, pl.ds(pl.multiple_of(n % tiles * 8, 8), 8)
        for half in range(nz // 128):
            at = (x, rows, pl.ds(half * 128, 128))
            out = collide_tile(
                [state[(i, *at)] for i in range(19)],
                greyness(resistance[at], solid[at]),
                shear_rate(flags[at]),
            )
            for i in range(19):
                post[(i, *at)] = out[i]
        return carry

    lax.fori_loop(0, nx * tiles, step, 0)
    for message, way, last, second in ((up, 1, ny - 1, ny - 2), (down, -1, 0, 1)):
        for field, source in ((0, post), (1, adjoint)):
            sign = 1 - 2 * field
            for i in moving(sign, 1, 0):
                message[near_plane(field, way, i)] = source[i, :, last, :]
            for i in moving(sign, 1, way):
                message[near_plane(field, way, i)] = source[i, :, second, :]
                message[edge_plane(field, way, i)] = source[i, :, last, :]
        message[38] = greyness(resistance[:, last, :], solid[:, last, :])
        message[39] = shear_rate(flags[:, last, :])


def halo_rows(source, below, above, field, i, side):
    step = (1 - 2 * field) * VELOCITY[i][1]
    if side == 0:
        if step == -1:
            return source[i, :, 0, :]
        return below[near_plane(field, 1, i)]
    if step == 1:
        return source[i, :, source.shape[2] - 1, :]
    return above[near_plane(field, -1, i)]


def column(source, below, above, field, i, x):
    step = (1 - 2 * field) * VELOCITY[i][1]
    if step == 0:
        return source[i, x]
    low = below[edge_plane(field, 1, i), pl.ds(x, 1), :] if step == 1 else None
    high = above[edge_plane(field, -1, i), pl.ds(x, 1), :] if step == -1 else None
    return shifted_y(source[i, x], step, low, high)


def pack_kernel(post, adjoint, below, above, right, left):
    nx, ny = post.shape[1:3]
    for message, way, x in ((right, 1, nx - 1), (left, -1, 0)):
        for field, source in ((0, post), (1, adjoint)):
            sign = 1 - 2 * field
            for k, i in enumerate(moving(sign, 0, way)):
                at = 5 * field + k
                message[at] = column(source, below, above, field, i, x)
                for side in range(2):
                    step = sign * VELOCITY[i][1]
                    if (side, step) == (0, -1):
                        line = source[i, x, pl.ds(0, 1), :]
                    elif (side, step) == (1, 1):
                        line = source[i, x, pl.ds(ny - 1, 1), :]
                    else:
                        halo, to = ((below, 1), (above, -1))[side]
                        line = halo[near_plane(field, to, i), pl.ds(x, 1), :]
                    message[10 + side, pl.ds(at, 1), :] = line


def middle_kernel(
    post, adjoint, resistance, solid, flags, below, above, from_left, from_right,
    pulled, sensitivity, right, left, middle, cotangent, out, grey, rate, sens,
):
    nx, ny, nz = resistance.shape
    tiles = ny // 8
    halo = nx * tiles

    for field, source, target in ((0, post, middle), (1, adjoint, cotangent)):
        sign = 1 - 2 * field
        for i in range(19):
            vx, _, vz = (sign * v for v in VELOCITY[i])
            outer = {1: from_left, -1: from_right}.get(vx)
            at = 5 * field + moving(sign, 0, vx).index(i) if vx else None
            for x in range(nx):
                if 0 <= x - vx < nx:
                    block = column(source, below, above, field, i, x - vx)
                else:
                    block = outer[at]
                block = shifted_z(block, vz)
                for t in range(tiles):
                    target[i, x * tiles + t] = block[8 * t : 8 * t + 8]
            for side in range(2):
                rows = halo_rows(source, below, above, field, i, side)
                base = side * nx
                if vx == 0:
                    target[i, halo, base : base + nx, :] = rows
                else:
                    first = 0 if vx == 1 else nx - 1
                    keep = rows[: nx - 1] if vx == 1 else rows[1:]
                    to = base + (1 if vx == 1 else 0)
                    target[i, halo, to : to + nx - 1, :] = keep
                    target[i, halo, base + first : base + first + 1, :] = outer[10 + side, at : at + 1, :]
            if vz:
                target[i, halo] = shifted_z(target[i, halo], vz)
    for x in range(nx):
        for t in range(tiles):
            at = (x, slice(8 * t, 8 * t + 8), slice(None))
            grey[x * tiles + t] = greyness(resistance[at], solid[at])
            rate[x * tiles + t] = shear_rate(flags[at])
    for side, line in enumerate((below, above)):
        grey[halo, side * nx : side * nx + nx, :] = line[38]
        rate[halo, side * nx : side * nx + nx, :] = line[39]

    def step(t, carry):
        for half in range(nz // 128):
            at = (t, slice(None), pl.ds(half * 128, 128))
            new, sens[at] = adjoint_tile(
                [cotangent[(i, *at)] for i in range(19)],
                [middle[(i, *at)] for i in range(19)],
                grey[at],
                rate[at],
            )
            for i in range(19):
                out[(i, *at)] = new[i]
        return carry

    lax.fori_loop(0, halo + 1, step, 0)
    for x in range(nx):
        for t in range(tiles):
            at = (x, slice(8 * t, 8 * t + 8), slice(None))
            sensitivity[at] = jnp.where(solid[at] == 1, 0.0, sens[x * tiles + t])
        for i in range(19):
            vx, vy, vz = (-v for v in VELOCITY[i])
            block = out[i, x * tiles : x * tiles + tiles].reshape(ny, nz)
            block = shifted_y(
                block, vy, out[i, halo, x : x + 1, :], out[i, halo, nx + x : nx + x + 1, :]
            )
            block = shifted_z(block, vz)
            pulled[i, x] = block
            if vx == 1 and x == nx - 1:
                right[moving(-1, 0, 1).index(i)] = block
            if vx == -1 and x == 0:
                left[moving(-1, 0, -1).index(i)] = block


def start_kernel(state, pulled, resistance, solid, flags, partial, from_left, from_right, start, sensitivity):
    nx, ny, nz = resistance.shape

    for x in range(nx):

        def step(t, carry, x=x):
            rows = pl.ds(pl.multiple_of(t * 8, 8), 8)
            for half in range(nz // 128):
                lanes = pl.ds(half * 128, 128)
                at = (x, rows, lanes)
                cotangent = []
                for i in range(19):
                    source = x + VELOCITY[i][0]
                    if source < 0:
                        cotangent.append(from_left[moving(-1, 0, 1).index(i), rows, lanes])
                    elif source == nx:
                        cotangent.append(from_right[moving(-1, 0, -1).index(i), rows, lanes])
                    else:
                        cotangent.append(pulled[i, source, rows, lanes])
                new, sens = adjoint_tile(
                    cotangent,
                    [state[(i, *at)] for i in range(19)],
                    greyness(resistance[at], solid[at]),
                    shear_rate(flags[at]),
                )
                for i in range(19):
                    start[(i, *at)] = new[i]
                sensitivity[at] = partial[at] + jnp.where(solid[at] == 1, 0.0, sens)
            return carry

        lax.fori_loop(0, ny // 8, step, 0)


def call(kernel, outs, *args, scratch=()):
    whole = pl.BlockSpec(memory_space=pltpu.VMEM)
    return pl.pallas_call(
        kernel,
        out_shape=[jax.ShapeDtypeStruct(s, jnp.float32) for s in outs],
        in_specs=[whole] * len(args),
        out_specs=[whole] * len(outs),
        scratch_shapes=[pltpu.VMEM(s, jnp.float32) for s in scratch],
        compiler_params=pltpu.CompilerParams(vmem_limit_bytes=VMEM_LIMIT),
    )(*args)


VMEM_LIMIT = 40 * 1024 * 1024


def exchange(axis, onward, backward):
    count = lax.axis_size(axis)
    ahead = [(i, (i + 1) % count) for i in range(count)]
    behind = [(i, (i - 1) % count) for i in range(count)]
    return lax.ppermute(onward, axis, ahead), lax.ppermute(backward, axis, behind)


def body(checkpoint, adjoint_end, resistance, solid_mask, flags):
    nx, ny, nz = resistance.shape
    whole = checkpoint.shape
    cells = (resistance, solid_mask, flags)
    post, up, down = call(
        post_kernel, [whole, (40, nx, nz), (40, nx, nz)], checkpoint, adjoint_end, *cells
    )
    below, above = exchange("gy", up, down)
    right, left = call(
        pack_kernel, [(12, ny, nz)] * 2, post, adjoint_end, below, above
    )
    from_left, from_right = exchange("gx", right, left)
    tiled = (nx * ny // 8 + 1, 8, nz)
    pulled, partial, right, left = call(
        middle_kernel,
        [whole, (nx, ny, nz), (5, ny, nz), (5, ny, nz)],
        post, adjoint_end, *cells, below, above, from_left, from_right,
        scratch=[(19, *tiled)] * 3 + [tiled] * 3,
    )
    from_left, from_right = exchange("gx", right, left)
    start, sensitivity = call(
        start_kernel,
        [whole, (nx, ny, nz)],
        checkpoint, pulled, *cells, partial, from_left, from_right,
    )
    return start, sensitivity


def solution(mesh):
    state, cell = P(None, "gx", "gy", None), P("gx", "gy", None)
    return jax.shard_map(
        body,
        mesh=mesh,
        in_specs=(state, state, cell, cell, cell),
        out_specs=(state, cell),
        check_vma=False,
    )
```

profile of v0, /device:TPU:3, one launch (start us, length us, event | category | flops | bytes accessed | tf_op | source)
XLA Modules:
  0.0 35.4 jit_solution(4175736390409572565)
XLA Ops:
  0.6 0.0 copy-start
  0.6 1.3 %copy-done = f32[19,4,16,256]{3,2,1,0:T(8,128)S(1)} copy-done((f32[19,4,16,256]{3,2,1,0:T(8,128)S(1)}, f32[19,4,16,256]{3,2,1,0:T(8,128)}, u32[]{:S(2)}) %copy-start) | copy-done | bytes 1245208
  1.9 0.0 copy-start.2
  1.9 1.3 %copy-done.2 = f32[19,4,16,256]{3,2,1,0:T(8,128)S(1)} copy-done((f32[19,4,16,256]{3,2,1,0:T(8,128)S(1)}, f32[19,4,16,256]{3,2,1,0:T(8,128)}, u32[]{:S(2)}) %copy-start.2) | copy-done | bytes 1245208
  3.2 0.0 copy-start.3
  3.2 0.8 %copy-done.3 = f32[4,16,256]{2,1,0:T(8,128)S(1)} copy-done((f32[4,16,256]{2,1,0:T(8,128)S(1)}, f32[4,16,256]{2,1,0:T(8,128)}, u32[]{:S(2)}) %copy-start.3) | copy-done | bytes 65560
  4.1 0.0 copy-start.5
  4.1 0.8 %copy-done.5 = s32[4,16,256]{2,1,0:T(8,128)S(1)} copy-done((s32[4,16,256]{2,1,0:T(8,128)S(1)}, s32[4,16,256]{2,1,0:T(8,128)}, u32[]{:S(2)}) %copy-start.5) | copy-done | bytes 65560
  4.9 0.0 copy-start.7
  4.9 0.8 %copy-done.7 = s32[4,16,256]{2,1,0:T(8,128)S(1)} copy-done((s32[4,16,256]{2,1,0:T(8,128)S(1)}, s32[4,16,256]{2,1,0:T(8,128)}, u32[]{:S(2)}) %copy-start.7) | copy-done | bytes 65560
  5.7 0.0 copy-start.1
  5.7 0.9 %shard_map.68 = (f32[19,4,16,256]{3,2,1,0:T(8,128)S(1)}, f32[40,4,256]{2,1,0:T(4,128)S(1)}, f32[40,4,256]{2,1,0:T(4,128)S(1)}) custom-call(f32[19,4,16,256]{3,2,1,0:T(8,128)S(1)} %copy-done.2, f32[19,4,16,256]{3,2,1,0:T(8,128)S(1)} %copy-done, f32[4,16,256]{2,1,0:T(8,128)S(1)} %copy-done.3, s32[4,16,256]{2,1,0:T(8,128)S(1)} %copy-done.5, ...), custom_call_target="tpu_custom_call" | custom-call | tf_op jit(solution)/shard_map/pallas_call | solution.py:376
  6.6 1.3 %collective-permute-start = (f32[40,4,256]{2,1,0:T(4,128)S(1)}, f32[40,4,256]{2,1,0:T(4,128)S(1)}, u32[]{:S(2)}, u32[]{:S(2)}) collective-permute-start(f32[40,4,256]{2,1,0:T(4,128)S(1)} %get-tuple-element.12), channel_id=1, source_target_pairs={{0,1},{1,2},{2,3},{3,0},{4,5},{5,6},{6,7},{7,4},{8,9},{9,10},{10,1... | collective-permute-start | bytes 491528 | tf_op jit(solution)/shard_map/ppermute | solution.py:393
  8.0 2.1 %collective-permute-start.1 = (f32[40,4,256]{2,1,0:T(4,128)S(1)}, f32[40,4,256]{2,1,0:T(4,128)S(1)}, u32[]{:S(2)}, u32[]{:S(2)}) collective-permute-start(f32[40,4,256]{2,1,0:T(4,128)S(1)} %get-tuple-element.13), channel_id=1, source_target_pairs={{0,3},{1,0},{2,1},{3,2},{4,7},{5,4},{6,5},{7,6},{8,11},{9,8},{10,9... | collective-permute-start | bytes 491528 | tf_op jit(solution)/shard_map/ppermute | solution.py:393
  10.1 3.7 %collective-permute-done.below = f32[40,4,256]{2,1,0:T(4,128)S(1)} collective-permute-done((f32[40,4,256]{2,1,0:T(4,128)S(1)}, f32[40,4,256]{2,1,0:T(4,128)S(1)}, u32[]{:S(2)}, u32[]{:S(2)}) %collective-permute-start) | collective-permute-done | bytes 163872 | tf_op jit(solution)/shard_map/ppermute | solution.py:393
  13.7 3.3 %collective-permute-done.1.above = f32[40,4,256]{2,1,0:T(4,128)S(1)} collective-permute-done((f32[40,4,256]{2,1,0:T(4,128)S(1)}, f32[40,4,256]{2,1,0:T(4,128)S(1)}, u32[]{:S(2)}, u32[]{:S(2)}) %collective-permute-start.1) | collective-permute-done | bytes 163872 | tf_op jit(solution)/shard_map/ppermute | solution.py:393
  17.0 0.0 copy-done.1
  17.0 0.0 copy-start.4
  17.0 0.0 copy-start.6
  17.0 2.3 %collective-permute-start.2 = (f32[12,16,256]{2,1,0:T(8,128)S(1)}, f32[12,16,256]{2,1,0:T(8,128)S(1)}, u32[]{:S(2)}, u32[]{:S(2)}) collective-permute-start(f32[12,16,256]{2,1,0:T(8,128)S(1)} %get-tuple-element.14), channel_id=1, source_target_pairs={{0,4},{4,8},{8,12},{12,16},{16,20},{20,24},{24,28},{28,0},{1,5},{5... | collective-permute-start | bytes 589832 | tf_op jit(solution)/shard_map/ppermute | solution.py:393
  19.3 0.0 collective-permute-start.3
  19.3 3.9 %collective-permute-done.2.from_left = f32[12,16,256]{2,1,0:T(8,128)S(1)} collective-permute-done((f32[12,16,256]{2,1,0:T(8,128)S(1)}, f32[12,16,256]{2,1,0:T(8,128)S(1)}, u32[]{:S(2)}, u32[]{:S(2)}) %collective-permute-start.2) | collective-permute-done | bytes 196640 | tf_op jit(solution)/shard_map/ppermute | solution.py:393
  23.2 2.5 %collective-permute-done.3.from_right = f32[12,16,256]{2,1,0:T(8,128)S(1)} collective-permute-done((f32[12,16,256]{2,1,0:T(8,128)S(1)}, f32[12,16,256]{2,1,0:T(8,128)S(1)}, u32[]{:S(2)}, u32[]{:S(2)}) %collective-permute-start.3) | collective-permute-done | bytes 196640 | tf_op jit(solution)/shard_map/ppermute | solution.py:393
  25.7 0.0 copy-done.4
  25.7 0.0 copy-done.6
  25.7 1.8 %shard_map.70 = (f32[19,4,16,256]{3,2,1,0:T(8,128)S(1)}, f32[4,16,256]{2,1,0:T(8,128)S(1)}, f32[5,16,256]{2,1,0:T(8,128)S(1)}, f32[5,16,256]{2,1,0:T(8,128)S(1)}) custom-call(f32[19,4,16,256]{3,2,1,0:T(8,128)S(1)} %get-tuple-element.11.post, f32[19,4,16,256]{3,2,1,0:T(8,128)S(1)} %copy-done.1, f32[4,16,256]{2,1,0:T(8,128)S(1)} %copy-done.4, ...), custom_call_target="tpu_custom_call" | custom-call | tf_op jit(solution)/shard_map/pallas_call | solution.py:376
  27.5 1.0 %collective-permute-start.4 = (f32[5,16,256]{2,1,0:T(8,128)S(1)}, f32[5,16,256]{2,1,0:T(8,128)S(1)}, u32[]{:S(2)}, u32[]{:S(2)}) collective-permute-start(f32[5,16,256]{2,1,0:T(8,128)S(1)} %get-tuple-element.18), channel_id=1, source_target_pairs={{0,4},{4,8},{8,12},{12,16},{16,20},{20,24},{24,28},{28,0},{1,5},{5... | collective-permute-start | bytes 245768 | tf_op jit(solution)/shard_map/ppermute | solution.py:393
  28.5 0.0 collective-permute-start.5
  28.5 2.3 %collective-permute-done.4.from_left = f32[5,16,256]{2,1,0:T(8,128)S(1)} collective-permute-done((f32[5,16,256]{2,1,0:T(8,128)S(1)}, f32[5,16,256]{2,1,0:T(8,128)S(1)}, u32[]{:S(2)}, u32[]{:S(2)}) %collective-permute-start.4) | collective-permute-done | bytes 81952 | tf_op jit(solution)/shard_map/ppermute | solution.py:393
  30.8 2.5 %collective-permute-done.5.from_right = f32[5,16,256]{2,1,0:T(8,128)S(1)} collective-permute-done((f32[5,16,256]{2,1,0:T(8,128)S(1)}, f32[5,16,256]{2,1,0:T(8,128)S(1)}, u32[]{:S(2)}, u32[]{:S(2)}) %collective-permute-start.5) | collective-permute-done | bytes 81952 | tf_op jit(solution)/shard_map/ppermute | solution.py:393
  33.3 2.2 %shard_map.71 = (f32[19,4,16,256]{3,2,1,0:T(8,128)}, f32[4,16,256]{2,1,0:T(8,128)}) custom-call(f32[19,4,16,256]{3,2,1,0:T(8,128)S(1)} %copy-done.2, f32[19,4,16,256]{3,2,1,0:T(8,128)S(1)} %get-tuple-element.16.pulled, f32[4,16,256]{2,1,0:T(8,128)S(1)} %copy-done.4, s32[4,16,256]{2,1,0:T(8,128)S(1)} %copy-done.6, s32[4,16,256]{2,1,0:T(8,128)S(1)} %copy-done.7, ...), custom_call_target="tpu_custom_call" | custom-call | tf_op jit(solution)/shard_map/pallas_call | solution.py:376
  (1 shorter events, 0.0 us)
Async XLA Ops:
  0.6 1.3 %copy-start = (f32[19,4,16,256]{3,2,1,0:T(8,128)S(1)}, f32[19,4,16,256]{3,2,1,0:T(8,128)}, u32[]{:S(2)}) copy-start(f32[19,4,16,256]{3,2,1,0:T(8,128)} %adjoint.5) | copy-start | bytes 3735556
  1.9 1.3 %copy-start.2 = (f32[19,4,16,256]{3,2,1,0:T(8,128)S(1)}, f32[19,4,16,256]{3,2,1,0:T(8,128)}, u32[]{:S(2)}) copy-start(f32[19,4,16,256]{3,2,1,0:T(8,128)} %state.3) | copy-start | bytes 3735556
  3.2 0.8 %copy-start.3 = (f32[4,16,256]{2,1,0:T(8,128)S(1)}, f32[4,16,256]{2,1,0:T(8,128)}, u32[]{:S(2)}) copy-start(f32[4,16,256]{2,1,0:T(8,128)} %resistance.5) | copy-start | bytes 196612
  4.1 0.8 %copy-start.5 = (s32[4,16,256]{2,1,0:T(8,128)S(1)}, s32[4,16,256]{2,1,0:T(8,128)}, u32[]{:S(2)}) copy-start(s32[4,16,256]{2,1,0:T(8,128)} %solid.5) | copy-start | bytes 196612
  4.9 0.8 %copy-start.7 = (s32[4,16,256]{2,1,0:T(8,128)S(1)}, s32[4,16,256]{2,1,0:T(8,128)}, u32[]{:S(2)}) copy-start(s32[4,16,256]{2,1,0:T(8,128)} %flags.5) | copy-start | bytes 196612
  5.7 11.3 %copy-start.1 = (f32[19,4,16,256]{3,2,1,0:T(8,128)S(1)}, f32[19,4,16,256]{3,2,1,0:T(8,128)}, u32[]{:S(2)}) copy-start(f32[19,4,16,256]{3,2,1,0:T(8,128)} %adjoint.5) | copy-start | bytes 3735556
  6.6 7.1 %collective-permute-start = (f32[40,4,256]{2,1,0:T(4,128)S(1)}, f32[40,4,256]{2,1,0:T(4,128)S(1)}, u32[]{:S(2)}, u32[]{:S(2)}) collective-permute-start(f32[40,4,256]{2,1,0:T(4,128)S(1)} %get-tuple-element.12), channel_id=1, source_target_pairs={{0,1},{1,2},{2,3},{3,0},{4,5},{5,6},{6,7},{7,4},{8,9},{9,10},{10,1... | collective-permute-start | bytes 491528 | tf_op jit(solution)/shard_map/ppermute | solution.py:393
  8.0 9.0 %collective-permute-start.1 = (f32[40,4,256]{2,1,0:T(4,128)S(1)}, f32[40,4,256]{2,1,0:T(4,128)S(1)}, u32[]{:S(2)}, u32[]{:S(2)}) collective-permute-start(f32[40,4,256]{2,1,0:T(4,128)S(1)} %get-tuple-element.13), channel_id=1, source_target_pairs={{0,3},{1,0},{2,1},{3,2},{4,7},{5,4},{6,5},{7,6},{8,11},{9,8},{10,9... | collective-permute-start | bytes 491528 | tf_op jit(solution)/shard_map/ppermute | solution.py:393
  17.0 8.7 %copy-start.4 = (f32[4,16,256]{2,1,0:T(8,128)S(1)}, f32[4,16,256]{2,1,0:T(8,128)}, u32[]{:S(2)}) copy-start(f32[4,16,256]{2,1,0:T(8,128)} %resistance.5) | copy-start | bytes 196612
  17.0 8.7 %copy-start.6 = (s32[4,16,256]{2,1,0:T(8,128)S(1)}, s32[4,16,256]{2,1,0:T(8,128)}, u32[]{:S(2)}) copy-start(s32[4,16,256]{2,1,0:T(8,128)} %solid.5) | copy-start | bytes 196612
  17.0 6.2 %collective-permute-start.2 = (f32[12,16,256]{2,1,0:T(8,128)S(1)}, f32[12,16,256]{2,1,0:T(8,128)S(1)}, u32[]{:S(2)}, u32[]{:S(2)}) collective-permute-start(f32[12,16,256]{2,1,0:T(8,128)S(1)} %get-tuple-element.14), channel_id=1, source_target_pairs={{0,4},{4,8},{8,12},{12,16},{16,20},{20,24},{24,28},{28,0},{1,5},{5... | collective-permute-start | bytes 589832 | tf_op jit(solution)/shard_map/ppermute | solution.py:393
  19.3 6.4 %collective-permute-start.3 = (f32[12,16,256]{2,1,0:T(8,128)S(1)}, f32[12,16,256]{2,1,0:T(8,128)S(1)}, u32[]{:S(2)}, u32[]{:S(2)}) collective-permute-start(f32[12,16,256]{2,1,0:T(8,128)S(1)} %get-tuple-element.15), channel_id=1, source_target_pairs={{0,28},{4,0},{8,4},{12,8},{16,12},{20,16},{24,20},{28,24},{1,29},{... | collective-permute-start | bytes 589832 | tf_op jit(solution)/shard_map/ppermute | solution.py:393
  27.5 3.2 %collective-permute-start.4 = (f32[5,16,256]{2,1,0:T(8,128)S(1)}, f32[5,16,256]{2,1,0:T(8,128)S(1)}, u32[]{:S(2)}, u32[]{:S(2)}) collective-permute-start(f32[5,16,256]{2,1,0:T(8,128)S(1)} %get-tuple-element.18), channel_id=1, source_target_pairs={{0,4},{4,8},{8,12},{12,16},{16,20},{20,24},{24,28},{28,0},{1,5},{5... | collective-permute-start | bytes 245768 | tf_op jit(solution)/shard_map/ppermute | solution.py:393
  28.5 4.8 %collective-permute-start.5 = (f32[5,16,256]{2,1,0:T(8,128)S(1)}, f32[5,16,256]{2,1,0:T(8,128)S(1)}, u32[]{:S(2)}, u32[]{:S(2)}) collective-permute-start(f32[5,16,256]{2,1,0:T(8,128)S(1)} %get-tuple-element.19), channel_id=1, source_target_pairs={{0,28},{4,0},{8,4},{12,8},{16,12},{20,16},{24,20},{28,24},{1,29},{... | collective-permute-start | bytes 245768 | tf_op jit(solution)/shard_map/ppermute | solution.py:393
where the time goes:
time: 35.8 us; the launch traced here: 35.4 us
  waiting for transfers between devices  18.1 us (51%)
  starting transfers between devices  6.69 us (19%)
  local copies, waits for them, and re-layouts  5.11 us (14%)
  Pallas kernels  4.93 us (14%)
  between operations  0.67 us (2%)
    ppermute x3, waiting for transfers between devices, exchange(): lax.ppermute(onward, axis, ahead)  9.83 us
    ppermute x3, waiting for transfers between devices, exchange(): lax.ppermute(backward, axis, behind)  8.22 us
    unnamed x16, local copies, waits for them, and re-layouts  5.11 us
    pallas_call x4, Pallas kernels, call(): pl.pallas_call(kernel, out_shape=[jax.ShapeDtypeStruct(s, jnp.float32) fo...  4.93 us
    ppermute x3, starting transfers between devices, exchange(): lax.ppermute(onward, axis, ahead)  4.59 us
    ppermute x3, starting transfers between devices, exchange(): lax.ppermute(backward, axis, behind)  2.1 us
  transfers between devices with their start and end apart: 6, of which 6 were waited for; matrix products, arithmetic and copies ran while one was open for 0% of the time, Pallas kernels for 0%

commit v1 on v0

--- a/solution.py
+++ b/solution.py
@@ -192,24 +192,40 @@
     return pltpu.roll(block, step % block.shape[1], 1) if step else block
 
 
-def post_kernel(state, adjoint, resistance, solid, flags, post, up, down):
+def post_kernel(
+    far_state, far_adjoint, far_resistance, far_solid, far_flags, post, up, down,
+    state, adjoint, resistance, solid, flags, done,
+):
     nx, ny, nz = resistance.shape
     tiles = ny // 8
-
-    def step(n, carry):
-        x, rows = n // tiles, pl.ds(pl.multiple_of(n % tiles * 8, 8), 8)
-        for half in range(nz // 128):
-            at = (x, rows, pl.ds(half * 128, 128))
-            out = collide_tile(
-                [state[(i, *at)] for i in range(19)],
-                greyness(resistance[at], solid[at]),
-                shear_rate(flags[at]),
-            )
-            for i in range(19):
-                post[(i, *at)] = out[i]
-        return carry
-
-    lax.fori_loop(0, nx * tiles, step, 0)
+    cells = ((far_resistance, resistance), (far_solid, solid), (far_flags, flags))
+    copies = [pltpu.make_async_copy(*pair, done.at[k]) for k, pair in enumerate(cells)]
+    for x in range(nx):
+        copies.append(pltpu.make_async_copy(far_state.at[:, x], state.at[:, x], done.at[3 + x]))
+    copies.append(pltpu.make_async_copy(far_adjoint, adjoint, done.at[3 + nx]))
+    for copy in copies:
+        copy.start()
+    for copy in copies[:3]:
+        copy.wait()
+
+    for x in range(nx):
+        copies[3 + x].wait()
+
+        def step(t, carry, x=x):
+            rows = pl.ds(pl.multiple_of(t * 8, 8), 8)
+            for half in range(nz // 128):
+                at = (x, rows, pl.ds(half * 128, 128))
+                out = collide_tile(
+                    [state[(i, *at)] for i in range(19)],
+                    greyness(resistance[at], solid[at]),
+                    shear_rate(flags[at]),
+                )
+                for i in range(19):
+                    post[(i, *at)] = out[i]
+            return carry
+
+        lax.fori_loop(0, tiles, step, 0)
+    copies[3 + nx].wait()
     for message, way, last, second in ((up, 1, ny - 1, ny - 2), (down, -1, 0, 1)):
         for field, source in ((0, post), (1, adjoint)):
             sign = 1 - 2 * field
@@ -371,14 +387,14 @@
         lax.fori_loop(0, ny // 8, step, 0)
 
 
-def call(kernel, outs, *args, scratch=()):
+def call(kernel, outs, *args, scratch=(), far=0):
     whole = pl.BlockSpec(memory_space=pltpu.VMEM)
     return pl.pallas_call(
         kernel,
         out_shape=[jax.ShapeDtypeStruct(s, jnp.float32) for s in outs],
-        in_specs=[whole] * len(args),
+        in_specs=[pl.BlockSpec(memory_space=pltpu.HBM)] * far + [whole] * (len(args) - far),
         out_specs=[whole] * len(outs),
-        scratch_shapes=[pltpu.VMEM(s, jnp.float32) for s in scratch],
+        scratch_shapes=[pltpu.VMEM(s, jnp.float32) if isinstance(s, tuple) else s for s in scratch],
         compiler_params=pltpu.CompilerParams(vmem_limit_bytes=VMEM_LIMIT),
     )(*args)
 
@@ -398,7 +414,9 @@
     whole = checkpoint.shape
     cells = (resistance, solid_mask, flags)
     post, up, down = call(
-        post_kernel, [whole, (40, nx, nz), (40, nx, nz)], checkpoint, adjoint_end, *cells
+        post_kernel, [whole, (40, nx, nz), (40, nx, nz)],
+        *(pltpu.with_memory_space_constraint(v, pltpu.HBM) for v in (checkpoint, adjoint_end, *cells)), far=5,
+        scratch=[whole, whole, (nx, ny, nz), *[pltpu.VMEM((nx, ny, nz), jnp.int32)] * 2, pltpu.SemaphoreType.DMA((nx + 4,))],
     )
     below, above = exchange("gy", up, down)
     right, left = call(

time: 35.8 us -> 31.7 us (0.89)
  local copies, waits for them, and re-layouts: 5.11 us -> 0.02 us
  Pallas kernels: 4.93 us -> 6.13 us
    unnamed x16 -> x10, local copies, waits for them, and re-layouts: 5.11 us -> 0.02 us
    pallas_call x4, Pallas kernels: 4.93 us -> 6.13 us  [call(): pl.pallas_call(kernel, out_shape=[jax.ShapeDtypeStruct(s, jnp.float32) fo...]
where the time goes in v1:
time: 31.7 us; the launch traced here: 31.6 us
  waiting for transfers between devices  18 us (57%)
  starting transfers between devices  6.69 us (21%)
  Pallas kernels  6.13 us (19%)
  between operations  0.68 us (2%)
    ppermute x3, waiting for transfers between devices, exchange(): lax.ppermute(onward, axis, ahead)  9.82 us
    ppermute x3, waiting for transfers between devices, exchange(): lax.ppermute(backward, axis, behind)  8.23 us
    pallas_call x4, Pallas kernels, call(): pl.pallas_call(kernel, out_shape=[jax.ShapeDtypeStruct(s, jnp.float32) fo...  6.13 us
    ppermute x3, starting transfers between devices, exchange(): lax.ppermute(onward, axis, ahead)  4.6 us
    ppermute x3, starting transfers between devices, exchange(): lax.ppermute(backward, axis, behind)  2.1 us
  transfers between devices with their start and end apart: 6, of which 6 were waited for; matrix products, arithmetic and copies ran while one was open for 0% of the time, Pallas kernels for 0%

profile of v1, /device:TPU:3, one launch (start us, length us, event | category | flops | bytes accessed | tf_op | source)
XLA Modules:
  0.0 31.6 jit_solution(1922819019565121657)
XLA Ops:
  0.6 0.0 copy-start
  0.6 2.1 %shard_map.68 = (f32[19,4,16,256]{3,2,1,0:T(8,128)S(1)}, f32[40,4,256]{2,1,0:T(4,128)S(1)}, f32[40,4,256]{2,1,0:T(4,128)S(1)}) custom-call(f32[19,4,16,256]{3,2,1,0:T(8,128)} %state.1, f32[19,4,16,256]{3,2,1,0:T(8,128)} %adjoint.3, f32[4,16,256]{2,1,0:T(8,128)} %resistance.3, s32[4,16,256]{2,1,0:T(8,128)} %solid.3, s32[4,16,256]{2,1,0:T(8,128)} %flags.3), custom_call_target="tpu_custom_call" | custom-call | tf_op jit(solution)/shard_map/pallas_call | solution.py:392
  2.7 1.3 %collective-permute-start = (f32[40,4,256]{2,1,0:T(4,128)S(1)}, f32[40,4,256]{2,1,0:T(4,128)S(1)}, u32[]{:S(2)}, u32[]{:S(2)}) collective-permute-start(f32[40,4,256]{2,1,0:T(4,128)S(1)} %get-tuple-element.12), channel_id=1, source_target_pairs={{0,1},{1,2},{2,3},{3,0},{4,5},{5,6},{6,7},{7,4},{8,9},{9,10},{10,1... | collective-permute-start | bytes 491528 | tf_op jit(solution)/shard_map/ppermute | solution.py:409
  4.1 2.1 %collective-permute-start.1 = (f32[40,4,256]{2,1,0:T(4,128)S(1)}, f32[40,4,256]{2,1,0:T(4,128)S(1)}, u32[]{:S(2)}, u32[]{:S(2)}) collective-permute-start(f32[40,4,256]{2,1,0:T(4,128)S(1)} %get-tuple-element.13), channel_id=1, source_target_pairs={{0,3},{1,0},{2,1},{3,2},{4,7},{5,4},{6,5},{7,6},{8,11},{9,8},{10,9... | collective-permute-start | bytes 491528 | tf_op jit(solution)/shard_map/ppermute | solution.py:409
  6.2 3.7 %collective-permute-done.below = f32[40,4,256]{2,1,0:T(4,128)S(1)} collective-permute-done((f32[40,4,256]{2,1,0:T(4,128)S(1)}, f32[40,4,256]{2,1,0:T(4,128)S(1)}, u32[]{:S(2)}, u32[]{:S(2)}) %collective-permute-start) | collective-permute-done | bytes 163872 | tf_op jit(solution)/shard_map/ppermute | solution.py:409
  9.8 3.3 %collective-permute-done.1.above = f32[40,4,256]{2,1,0:T(4,128)S(1)} collective-permute-done((f32[40,4,256]{2,1,0:T(4,128)S(1)}, f32[40,4,256]{2,1,0:T(4,128)S(1)}, u32[]{:S(2)}, u32[]{:S(2)}) %collective-permute-start.1) | collective-permute-done | bytes 163872 | tf_op jit(solution)/shard_map/ppermute | solution.py:409
  13.1 0.0 copy-done
  13.1 0.0 copy-start.2
  13.1 0.0 copy-start.3
  13.1 0.0 copy-start.4
  13.2 2.3 %collective-permute-start.2 = (f32[12,16,256]{2,1,0:T(8,128)S(1)}, f32[12,16,256]{2,1,0:T(8,128)S(1)}, u32[]{:S(2)}, u32[]{:S(2)}) collective-permute-start(f32[12,16,256]{2,1,0:T(8,128)S(1)} %get-tuple-element.14), channel_id=1, source_target_pairs={{0,4},{4,8},{8,12},{12,16},{16,20},{20,24},{24,28},{28,0},{1,5},{5... | collective-permute-start | bytes 589832 | tf_op jit(solution)/shard_map/ppermute | solution.py:409
  15.4 0.0 copy-start.1
  15.4 0.0 collective-permute-start.3
  15.4 3.9 %collective-permute-done.2.from_left = f32[12,16,256]{2,1,0:T(8,128)S(1)} collective-permute-done((f32[12,16,256]{2,1,0:T(8,128)S(1)}, f32[12,16,256]{2,1,0:T(8,128)S(1)}, u32[]{:S(2)}, u32[]{:S(2)}) %collective-permute-start.2) | collective-permute-done | bytes 196640 | tf_op jit(solution)/shard_map/ppermute | solution.py:409
  19.3 2.5 %collective-permute-done.3.from_right = f32[12,16,256]{2,1,0:T(8,128)S(1)} collective-permute-done((f32[12,16,256]{2,1,0:T(8,128)S(1)}, f32[12,16,256]{2,1,0:T(8,128)S(1)}, u32[]{:S(2)}, u32[]{:S(2)}) %collective-permute-start.3) | collective-permute-done | bytes 196640 | tf_op jit(solution)/shard_map/ppermute | solution.py:409
  21.8 0.0 copy-done.2
  21.8 0.0 copy-done.3
  21.8 0.0 copy-done.4
  21.8 1.8 %shard_map.70 = (f32[19,4,16,256]{3,2,1,0:T(8,128)S(1)}, f32[4,16,256]{2,1,0:T(8,128)S(1)}, f32[5,16,256]{2,1,0:T(8,128)S(1)}, f32[5,16,256]{2,1,0:T(8,128)S(1)}) custom-call(f32[19,4,16,256]{3,2,1,0:T(8,128)S(1)} %get-tuple-element.11.post, f32[19,4,16,256]{3,2,1,0:T(8,128)S(1)} %copy-done, f32[4,16,256]{2,1,0:T(8,128)S(1)} %copy-done.2, ...), custom_call_target="tpu_custom_call" | custom-call | tf_op jit(solution)/shard_map/pallas_call | solution.py:392
  23.7 1.0 %collective-permute-start.4 = (f32[5,16,256]{2,1,0:T(8,128)S(1)}, f32[5,16,256]{2,1,0:T(8,128)S(1)}, u32[]{:S(2)}, u32[]{:S(2)}) collective-permute-start(f32[5,16,256]{2,1,0:T(8,128)S(1)} %get-tuple-element.18), channel_id=1, source_target_pairs={{0,4},{4,8},{8,12},{12,16},{16,20},{20,24},{24,28},{28,0},{1,5},{5... | collective-permute-start | bytes 245768 | tf_op jit(solution)/shard_map/ppermute | solution.py:409
  24.6 0.0 collective-permute-start.5
  24.6 2.3 %collective-permute-done.4.from_left = f32[5,16,256]{2,1,0:T(8,128)S(1)} collective-permute-done((f32[5,16,256]{2,1,0:T(8,128)S(1)}, f32[5,16,256]{2,1,0:T(8,128)S(1)}, u32[]{:S(2)}, u32[]{:S(2)}) %collective-permute-start.4) | collective-permute-done | bytes 81952 | tf_op jit(solution)/shard_map/ppermute | solution.py:409
  26.9 2.5 %collective-permute-done.5.from_right = f32[5,16,256]{2,1,0:T(8,128)S(1)} collective-permute-done((f32[5,16,256]{2,1,0:T(8,128)S(1)}, f32[5,16,256]{2,1,0:T(8,128)S(1)}, u32[]{:S(2)}, u32[]{:S(2)}) %collective-permute-start.5) | collective-permute-done | bytes 81952 | tf_op jit(solution)/shard_map/ppermute | solution.py:409
  29.4 0.0 copy-done.1
  29.4 2.2 %shard_map.71 = (f32[19,4,16,256]{3,2,1,0:T(8,128)}, f32[4,16,256]{2,1,0:T(8,128)}) custom-call(f32[19,4,16,256]{3,2,1,0:T(8,128)S(1)} %copy-done.1, f32[19,4,16,256]{3,2,1,0:T(8,128)S(1)} %get-tuple-element.16.pulled, f32[4,16,256]{2,1,0:T(8,128)S(1)} %copy-done.2, s32[4,16,256]{2,1,0:T(8,128)S(1)} %copy-done.3, s32[4,16,256]{2,1,0:T(8,128)S(1)} %copy-done.4, ...), custom_call_target="tpu_custom_call" | custom-call | tf_op jit(solution)/shard_map/pallas_call | solution.py:392
  (1 shorter events, 0.0 us)
Async XLA Ops:
  0.6 12.5 %copy-start = (f32[19,4,16,256]{3,2,1,0:T(8,128)S(1)}, f32[19,4,16,256]{3,2,1,0:T(8,128)}, u32[]{:S(2)}) copy-start(f32[19,4,16,256]{3,2,1,0:T(8,128)} %adjoint.3) | copy-start | bytes 3735556
  2.7 7.1 %collective-permute-start = (f32[40,4,256]{2,1,0:T(4,128)S(1)}, f32[40,4,256]{2,1,0:T(4,128)S(1)}, u32[]{:S(2)}, u32[]{:S(2)}) collective-permute-start(f32[40,4,256]{2,1,0:T(4,128)S(1)} %get-tuple-element.12), channel_id=1, source_target_pairs={{0,1},{1,2},{2,3},{3,0},{4,5},{5,6},{6,7},{7,4},{8,9},{9,10},{10,1... | collective-permute-start | bytes 491528 | tf_op jit(solution)/shard_map/ppermute | solution.py:409
  4.1 9.0 %collective-permute-start.1 = (f32[40,4,256]{2,1,0:T(4,128)S(1)}, f32[40,4,256]{2,1,0:T(4,128)S(1)}, u32[]{:S(2)}, u32[]{:S(2)}) collective-permute-start(f32[40,4,256]{2,1,0:T(4,128)S(1)} %get-tuple-element.13), channel_id=1, source_target_pairs={{0,3},{1,0},{2,1},{3,2},{4,7},{5,4},{6,5},{7,6},{8,11},{9,8},{10,9... | collective-permute-start | bytes 491528 | tf_op jit(solution)/shard_map/ppermute | solution.py:409
  13.1 8.7 %copy-start.2 = (f32[4,16,256]{2,1,0:T(8,128)S(1)}, f32[4,16,256]{2,1,0:T(8,128)}, u32[]{:S(2)}) copy-start(f32[4,16,256]{2,1,0:T(8,128)} %resistance.3) | copy-start | bytes 196612
  13.1 8.7 %copy-start.3 = (s32[4,16,256]{2,1,0:T(8,128)S(1)}, s32[4,16,256]{2,1,0:T(8,128)}, u32[]{:S(2)}) copy-start(s32[4,16,256]{2,1,0:T(8,128)} %solid.3) | copy-start | bytes 196612
  13.1 8.7 %copy-start.4 = (s32[4,16,256]{2,1,0:T(8,128)S(1)}, s32[4,16,256]{2,1,0:T(8,128)}, u32[]{:S(2)}) copy-start(s32[4,16,256]{2,1,0:T(8,128)} %flags.3) | copy-start | bytes 196612
  13.2 6.2 %collective-permute-start.2 = (f32[12,16,256]{2,1,0:T(8,128)S(1)}, f32[12,16,256]{2,1,0:T(8,128)S(1)}, u32[]{:S(2)}, u32[]{:S(2)}) collective-permute-start(f32[12,16,256]{2,1,0:T(8,128)S(1)} %get-tuple-element.14), channel_id=1, source_target_pairs={{0,4},{4,8},{8,12},{12,16},{16,20},{20,24},{24,28},{28,0},{1,5},{5... | collective-permute-start | bytes 589832 | tf_op jit(solution)/shard_map/ppermute | solution.py:409
  15.4 14.0 %copy-start.1 = (f32[19,4,16,256]{3,2,1,0:T(8,128)S(1)}, f32[19,4,16,256]{3,2,1,0:T(8,128)}, u32[]{:S(2)}) copy-start(f32[19,4,16,256]{3,2,1,0:T(8,128)} %state.1) | copy-start | bytes 3735556
  15.4 6.4 %collective-permute-start.3 = (f32[12,16,256]{2,1,0:T(8,128)S(1)}, f32[12,16,256]{2,1,0:T(8,128)S(1)}, u32[]{:S(2)}, u32[]{:S(2)}) collective-permute-start(f32[12,16,256]{2,1,0:T(8,128)S(1)} %get-tuple-element.15), channel_id=1, source_target_pairs={{0,28},{4,0},{8,4},{12,8},{16,12},{20,16},{24,20},{28,24},{1,29},{... | collective-permute-start | bytes 589832 | tf_op jit(solution)/shard_map/ppermute | solution.py:409
  23.7 3.2 %collective-permute-start.4 = (f32[5,16,256]{2,1,0:T(8,128)S(1)}, f32[5,16,256]{2,1,0:T(8,128)S(1)}, u32[]{:S(2)}, u32[]{:S(2)}) collective-permute-start(f32[5,16,256]{2,1,0:T(8,128)S(1)} %get-tuple-element.18), channel_id=1, source_target_pairs={{0,4},{4,8},{8,12},{12,16},{16,20},{20,24},{24,28},{28,0},{1,5},{5... | collective-permute-start | bytes 245768 | tf_op jit(solution)/shard_map/ppermute | solution.py:409
  24.6 4.8 %collective-permute-start.5 = (f32[5,16,256]{2,1,0:T(8,128)S(1)}, f32[5,16,256]{2,1,0:T(8,128)S(1)}, u32[]{:S(2)}, u32[]{:S(2)}) collective-permute-start(f32[5,16,256]{2,1,0:T(8,128)S(1)} %get-tuple-element.19), channel_id=1, source_target_pairs={{0,28},{4,0},{8,4},{12,8},{16,12},{20,16},{24,20},{28,24},{1,29},{... | collective-permute-start | bytes 245768 | tf_op jit(solution)/shard_map/ppermute | solution.py:409

commit v2 on v0

v2 whole, which is shorter than its diff:
```python
import jax
import jax.numpy as jnp
from jax import lax
from jax.experimental import pallas as pl
from jax.experimental.pallas import tpu as pltpu
from jax.sharding import PartitionSpec as P

VELOCITY = (
    (0, 0, 0),
    (1, 0, 0),
    (-1, 0, 0),
    (0, 1, 0),
    (0, -1, 0),
    (0, 0, 1),
    (0, 0, -1),
    (1, 1, 0),
    (-1, -1, 0),
    (1, -1, 0),
    (-1, 1, 0),
    (1, 0, 1),
    (-1, 0, -1),
    (1, 0, -1),
    (-1, 0, 1),
    (0, 1, 1),
    (0, -1, -1),
    (0, 1, -1),
    (0, -1, 1),
)


def pair_sums(f):
    even = [f[2 * k + 1] + f[2 * k + 2] for k in range(9)]
    odd = [f[2 * k + 1] - f[2 * k + 2] for k in range(9)]
    return even, odd


def grouped(f):
    even, odd = pair_sums(f)
    faces = even[:3]
    planes = [even[7] + even[8], even[5] + even[6], even[3] + even[4]]
    shears = [even[7] - even[8], even[5] - even[6], even[3] - even[4]]
    axes = [
        (odd[0], odd[3] + odd[4], odd[5] + odd[6]),
        (odd[1], odd[3] - odd[4], odd[7] + odd[8]),
        (odd[2], odd[5] - odd[6], odd[7] - odd[8]),
    ]
    return faces, planes, shears, axes, odd


def half_pairs(faces, planes, shears, axes):
    even = [0.5 * v for v in faces]
    for a in (2, 1, 0):
        even += [0.25 * (planes[a] + shears[a]), 0.25 * (planes[a] - shears[a])]
    odd = [0.5 * axes[a][0] for a in range(3)]
    for one, two in ((axes[0][1], axes[1][1]), (axes[0][2], axes[2][1]), (axes[1][2], axes[2][2])):
        odd += [0.25 * (one + two), 0.25 * (one - two)]
    return even, odd


def finish(rest, f, odd_sums, even, odd, grey, free):
    out = [f[0] - free * rest]
    for k in range(9):
        e = free * even[k]
        o = free * odd[k] + grey * odd_sums[k]
        out += [f[2 * k + 1] - (e + o), f[2 * k + 2] - (e - o)]
    return out


def collide_tile(f, grey, rate):
    faces, planes, shears, axes, odd_sums = grouped(f)
    total = faces[0] + faces[1] + faces[2]
    edges = planes[0] + planes[1] + planes[2]
    momentum = [d + a + b for d, a, b in axes]
    inverse = 1.0 / (f[0] + total + edges)
    u = [m * inverse for m in momentum]
    q = [m * v for m, v in zip(momentum, u)]
    q_all = q[0] + q[1] + q[2]
    energy = (1.19 * 19.0 / 2394.0) * (edges - f[0] - q_all)
    square = (1.4 / 252.0) * (9.0 * f[0] - 7.0 * total - 2.0 * edges + 5.5 * q_all)
    rest = 12.0 * square - 30.0 * energy
    d_total = -22.0 * energy - 8.0 * square
    d_edges = 32.0 * energy + 4.0 * square
    d_faces, d_planes = [], []
    for a in range(3):
        x = 3.0 * faces[a] - total
        y = edges - 3.0 * planes[a]
        eq = 3.0 * q[a] - q_all
        stress = rate * (x + y - eq)
        other = 1.4 * (y - 2.0 * x + 0.5 * eq)
        d_faces.append(d_total + (1.0 / 9.0) * (stress - other))
        d_planes.append(d_edges - (1.0 / 9.0) * (2.0 * stress + other))
    d_shears = [
        rate * (shears[0] - momentum[1] * u[2]),
        rate * (shears[1] - momentum[0] * u[2]),
        rate * (shears[2] - momentum[0] * u[1]),
    ]
    d_axes = []
    for d, a, b in axes:
        t = 0.2 * (a + b - 2.0 * d)
        v = 0.99 * (a - b)
        d_axes.append((-2.0 * t, t + v, t - v))
    even, odd = half_pairs(d_faces, d_planes, d_shears, d_axes)
    return finish(rest, f, odd_sums, even, odd, grey, 1.0 - grey)


def adjoint_at(lam, density, momentum, grey, rate):
    inverse = 1.0 / density
    u = [m * inverse for m in momentum]
    faces, planes, shears, axes, odd_sums = grouped(lam)
    total = faces[0] + faces[1] + faces[2]
    edges = planes[0] + planes[1] + planes[2]
    energy = (1.19 / 2394.0) * (8.0 * edges - 11.0 * total - 30.0 * lam[0])
    square = (1.4 / 252.0) * (edges - 4.0 * total + 12.0 * lam[0])
    bulk = 19.0 * energy - 5.5 * square
    weights, w_faces, w_planes, slopes, w_axes = [], [], [], [], []
    w_total = -22.0 * energy - 8.0 * square
    w_edges = 32.0 * energy + 4.0 * square
    for a in range(3):
        x = 3.0 * faces[a] - total
        y = edges - 3.0 * planes[a]
        stress = rate * (x + y)
        other = 1.4 * (y - 2.0 * x)
        w_faces.append(w_total + (1.0 / 9.0) * (stress - other))
        w_planes.append(w_edges - (1.0 / 9.0) * (2.0 * stress + other))
        weights.append(2.0 * bulk + (1.0 / 9.0) * stress - (1.0 / 36.0) * other)
    w_shears = [rate * v for v in shears]
    cross = [0.25 * v for v in w_shears]
    pull = [
        weights[0] * u[0] + cross[2] * u[1] + cross[1] * u[2],
        weights[1] * u[1] + cross[2] * u[0] + cross[0] * u[2],
        weights[2] * u[2] + cross[1] * u[0] + cross[0] * u[1],
    ]
    by_density = 3.0 * square - 11.0 * energy - 0.5 * (u[0] * pull[0] + u[1] * pull[1] + u[2] * pull[2])
    for a in range(3):
        d, p, r = axes[a]
        flux = p + r - 4.0 * d
        v = 0.99 * (p - r)
        slope = pull[a] - 0.02 * flux
        t = 0.12 * flux - 4.0 * slope
        w_axes.append((-0.24 * flux - 2.0 * slope, t + v, t - v))
    rest = 12.0 * square - 30.0 * energy - by_density
    w_faces = [v - 2.0 * by_density for v in w_faces]
    w_planes = [v - 4.0 * by_density for v in w_planes]
    even, odd = half_pairs(w_faces, w_planes, w_shears, w_axes)
    out = finish(rest, lam, odd_sums, even, odd, grey, 1.0 - grey)
    for a in range(3):
        (wd, wa, wb), (ld, lp, lr) = w_axes[a], axes[a]
        w_axes[a] = (wd - 2.0 * ld, wa - 2.0 * lp, wb - 2.0 * lr)
    return out, (rest, w_faces, w_planes, w_shears, w_axes)


def adjoint_tile(lam, f, grey, rate):
    faces, planes, shears, axes, _ = grouped(f)
    momentum = [d + a + b for d, a, b in axes]
    density = f[0] + (faces[0] + faces[1] + faces[2]) + (planes[0] + planes[1] + planes[2])
    out, (rest, w_faces, w_planes, w_shears, w_axes) = adjoint_at(lam, density, momentum, grey, rate)
    near, far = 0.0, 0.0
    for a in range(3):
        (wd, wa, wb), (d, p, r) = w_axes[a], axes[a]
        near = near + w_faces[a] * faces[a] + wd * d
        far = far + w_planes[a] * planes[a] + w_shears[a] * shears[a] + wa * p + wb * r
    return out, rest * f[0] + 0.5 * near + 0.25 * far


def greyness(resistance, solid):
    return jnp.where(solid == 1, 1.0, resistance)


def shear_rate(flags):
    return jnp.where(flags == 0, 1.25, jnp.where(flags == 1, 0.9, 1.7))


def moving(sign, dim, step):
    return [i for i in range(19) if sign * VELOCITY[i][dim] == step]


NEAR, FAR_EDGE, GREY, RATE = 9, 23, 28, 29


def edge_plane(field, way, i):
    return (4, FAR_EDGE)[field] + moving(1 - 2 * field, 1, way).index(i)


def near_plane(way, i):
    return NEAR + (moving(-1, 1, 0) + moving(-1, 1, way)).index(i)


def x_plane(field, i):
    return 5 * field + moving(1 - 2 * field, 0, (1 - 2 * field) * VELOCITY[i][0]).index(i)


def velocity(field, i):
    return tuple((1 - 2 * field) * v for v in VELOCITY[i])


def rolled_y(block, step):
    return pltpu.roll(block, step % block.shape[0], 0) if step else block


def shifted_y(block, step, below, above):
    if step == 0:
        return block
    row = lax.broadcasted_iota(jnp.int32, block.shape, 0)
    if step == 1:
        return jnp.where(row == 0, below, rolled_y(block, 1))
    return jnp.where(row == block.shape[0] - 1, above, rolled_y(block, -1))


def shifted_z(block, step):
    return pltpu.roll(block, step % block.shape[1], 1) if step else block


def face_kernel(
    far_state, far_adjoint, far_resistance, far_solid, far_flags, right, left,
    state, resistance, solid, flags, done,
):
    nx, ny, nz = far_resistance.shape
    sides = ((right, 1, nx - 1), (left, -1, 0))
    copies, first = [], []
    for side, (message, way, x) in enumerate(sides):
        pairs = [
            (far_state.at[:, x], state.at[side]),
            (far_resistance.at[x], resistance.at[side]),
            (far_solid.at[x], solid.at[side]),
            (far_flags.at[x], flags.at[side]),
        ]
        pairs += [(far_adjoint.at[i, x], message.at[x_plane(1, i)]) for i in moving(-1, 0, way)]
        first.append(len(copies))
        for source, target in pairs:
            copies.append(pltpu.make_async_copy(source, target, done.at[len(copies)]))
    for copy in copies:
        copy.start()
    for side, (message, way, _) in enumerate(sides):
        for copy in copies[first[side] : first[side] + 4]:
            copy.wait()

        def step(t, carry, side=side, message=message, way=way):
            rows = pl.ds(pl.multiple_of(t * 8, 8), 8)
            for half in range(nz // 128):
                at = (rows, pl.ds(half * 128, 128))
                out = collide_tile(
                    [state[(side, i, *at)] for i in range(19)],
                    greyness(resistance[(side, *at)], solid[(side, *at)]),
                    shear_rate(flags[(side, *at)]),
                )
                for i in moving(1, 0, way):
                    message[(x_plane(0, i), *at)] = out[i]
            return carry

        lax.fori_loop(0, ny // 8, step, 0)
    for side in range(2):
        for copy in copies[first[side] + 4 : first[side] + 9]:
            copy.wait()


def post_kernel(state, resistance, solid, flags, post):
    nx, ny, nz = resistance.shape
    tiles = ny // 8

    def step(n, carry):
        x, rows = n // tiles, pl.ds(pl.multiple_of(n % tiles * 8, 8), 8)
        for half in range(nz // 128):
            at = (x, rows, pl.ds(half * 128, 128))
            out = collide_tile(
                [state[(i, *at)] for i in range(19)],
                greyness(resistance[at], solid[at]),
                shear_rate(flags[at]),
            )
            for i in range(19):
                post[(i, *at)] = out[i]
        return carry

    lax.fori_loop(0, nx * tiles, step, 0)


def rim_kernel(post, adjoint, resistance, solid, flags, from_left, from_right, up, down, work):
    nx, ny, nz = resistance.shape
    shares = {1: [0.0] * 4, -1: [0.0] * 4}
    for field, source in ((0, post), (1, adjoint)):
        for i in range(19):
            vx, vy, vz = velocity(field, i)
            picks = {0: (ny - 1, 0), 1: (ny - 2, ny - 1), -1: (1, 0)}[vy]
            tile = work.at[19 * field + i]
            for half, row in enumerate(picks):
                base = half * nx
                if vx == 0:
                    tile[base : base + nx, :] = source[i, :, row, :]
                    continue
                outer = from_left if vx == 1 else from_right
                edge = outer[x_plane(field, i), pl.ds(row, 1), :]
                lines = source[i, :, row, :]
                if vx == 1:
                    tile[base + 1 : base + nx, :] = lines[: nx - 1]
                    tile[base : base + 1, :] = edge
                else:
                    tile[base : base + nx - 1, :] = lines[1:]
                    tile[base + nx - 1 : base + nx, :] = edge
            if vz:
                tile[...] = shifted_z(tile[...], vz)
            for half in range(2):
                value = tile[half * nx : half * nx + nx, :]
                way = vy if vy else 1 - 2 * half
                message = up if way == 1 else down
                if vy and half == 1:
                    message[edge_plane(field, way, i)] = value
                elif field == 1:
                    message[near_plane(way, i)] = value
                else:
                    share = shares[way]
                    for k, factor in enumerate((1, vx, vy, vz)):
                        if factor:
                            share[k] = share[k] + factor * value
    for way, message, row in ((1, up, ny - 1), (-1, down, 0)):
        for k in range(4):
            message[k] = shares[way][k]
        message[GREY] = greyness(resistance[:, row, :], solid[:, row, :])
        message[RATE] = shear_rate(flags[:, row, :])


def middle_kernel(
    post, adjoint, resistance, solid, flags, from_left, from_right,
    out, sensitivity, rim_middle, rim_cotangent, middle, cotangent,
):
    nx, ny, nz = resistance.shape
    tiles = ny // 8
    for field, source, target, rim in (
        (0, post, middle, rim_middle),
        (1, adjoint, cotangent, rim_cotangent),
    ):
        for i in range(19):
            vx, vy, vz = velocity(field, i)
            for x in range(nx):
                if 0 <= x - vx < nx:
                    block = source[i, x - vx]
                else:
                    block = (from_left if vx == 1 else from_right)[x_plane(field, i)]
                block = rolled_y(shifted_z(block, vz), vy)
                target[i, x] = block
                rim[i, x : x + 1, :] = block[:1]
                rim[i, nx + x : nx + x + 1, :] = block[ny - 1 :]

    def step(n, carry):
        x, rows = n // tiles, pl.ds(pl.multiple_of(n % tiles * 8, 8), 8)
        for half in range(nz // 128):
            at = (x, rows, pl.ds(half * 128, 128))
            state = [middle[(i, *at)] for i in range(19)]
            new, sens = adjoint_tile(
                [cotangent[(i, *at)] for i in range(19)],
                state,
                greyness(resistance[at], solid[at]),
                shear_rate(flags[at]),
            )
            sensitivity[at] = jnp.where(solid[at] == 1, 0.0, sens)
            for i in range(19):
                out[(i, *at)] = new[i]
        return carry

    lax.fori_loop(0, nx * tiles, step, 0)


def pulled_block(out, outer_rows, halo_rows, i, x):
    nx, ny = out.shape[1:3]
    _, vy, vz = velocity(1, i)
    block = out[i, x]
    row = lax.broadcasted_iota(jnp.int32, block.shape, 0)
    block = jnp.where(row == 0, outer_rows[i, pl.ds(x, 1), :], block)
    block = jnp.where(row == ny - 1, outer_rows[i, pl.ds(nx + x, 1), :], block)
    low = halo_rows[i, pl.ds(x, 1), :] if vy == 1 else None
    high = halo_rows[i, pl.ds(nx + x, 1), :] if vy == -1 else None
    return shifted_z(shifted_y(block, vy, low, high), vz)


def edge_kernel(
    out, resistance, solid, flags, rim_middle, rim_cotangent, up, down, below, above,
    outer_rows, halo_rows, outer_sens, right, left, middle, cotangent, halo, cells,
):
    nx, ny, nz = resistance.shape
    low, high = slice(0, nx), slice(nx, 2 * nx)
    for field, rim, target in ((0, rim_middle, middle), (1, rim_cotangent, cotangent)):
        for i in range(19):
            vy = velocity(field, i)[1]
            target[i] = rim[i]
            if vy == 1:
                target[i, low, :] = below[edge_plane(field, 1, i)]
            if vy == -1:
                target[i, high, :] = above[edge_plane(field, -1, i)]
    for i in range(19):
        vy = velocity(1, i)[1]
        halo[i, low, :] = down[edge_plane(1, -1, i)] if vy == -1 else below[near_plane(1, i)]
        halo[i, high, :] = up[edge_plane(1, 1, i)] if vy == 1 else above[near_plane(-1, i)]
    for rows, way, received, sent in ((low, -1, below, down), (high, 1, above, up)):
        share = [received[k] for k in range(4)]
        for i in moving(1, 1, way):
            value = sent[edge_plane(0, way, i)]
            for k, factor in enumerate((1, *VELOCITY[i])):
                if factor:
                    share[k] = share[k] + factor * value
        for k in range(4):
            cells[k, rows, :] = share[k]
        cells[4, rows, :] = received[GREY]
        cells[5, rows, :] = received[RATE]
        row = 0 if way == -1 else ny - 1
        blocked = solid[:, row, :]
        cells[6, rows, :] = greyness(resistance[:, row, :], blocked)
        cells[7, rows, :] = shear_rate(flags[:, row, :])
        cells[8, rows, :] = jnp.where(blocked == 1, 0.0, 1.0)
    for part in range(nz // 128):
        at = (slice(None), pl.ds(part * 128, 128))
        state = [middle[(i, *at)] for i in range(19)]
        new, sens = adjoint_tile(
            [cotangent[(i, *at)] for i in range(19)], state, cells[(6, *at)], cells[(7, *at)]
        )
        outer_sens[at] = jnp.where(cells[(8, *at)] == 0.0, 0.0, sens)
        for i in range(19):
            outer_rows[(i, *at)] = new[i]
        lam = [halo[(i, *at)] for i in range(19)]
        density, *momentum = [cells[(k, *at)] for k in range(4)]
        new, _ = adjoint_at(lam, density, momentum, cells[(4, *at)], cells[(5, *at)])
        for i in range(19):
            halo_rows[(i, *at)] = new[i]
    for message, way, x in ((right, 1, nx - 1), (left, -1, 0)):
        for k, i in enumerate(moving(-1, 0, way)):
            message[k] = pulled_block(out, outer_rows, halo_rows, i, x)


def start_columns(columns, state, pulled, resistance, solid, flags, partial, from_left, from_right, start, total):
    nx, ny, nz = resistance.shape
    for slot, x in enumerate(columns):

        def step(t, carry, x=x, slot=slot):
            rows = pl.ds(pl.multiple_of(t * 8, 8), 8)
            for half in range(nz // 128):
                lanes = pl.ds(half * 128, 128)
                at = (x, rows, lanes)
                cotangent = []
                for i in range(19):
                    source = x + VELOCITY[i][0]
                    if source < 0:
                        cotangent.append(from_left[moving(-1, 0, 1).index(i), rows, lanes])
                    elif source == nx:
                        cotangent.append(from_right[moving(-1, 0, -1).index(i), rows, lanes])
                    else:
                        cotangent.append(pulled[i, source, rows, lanes])
                new, sens = adjoint_tile(
                    cotangent,
                    [state[(i, *at)] for i in range(19)],
                    greyness(resistance[at], solid[at]),
                    shear_rate(flags[at]),
                )
                for i in range(19):
                    start[slot, i, rows, lanes] = new[i]
                total[at] = partial[at] + jnp.where(solid[at] == 1, 0.0, sens)
            return carry

        lax.fori_loop(0, ny // 8, step, 0)
        yield slot, x


def inner_kernel(
    out, outer_rows, halo_rows, sens, outer_sens, state, resistance, solid, flags,
    far_start, pulled, partial, start, done,
):
    nx, ny = resistance.shape[:2]
    for x in range(nx):
        for i in range(19):
            pulled[i, x] = pulled_block(out, outer_rows, halo_rows, i, x)
        block = sens[x]
        row = lax.broadcasted_iota(jnp.int32, block.shape, 0)
        block = jnp.where(row == 0, outer_sens[pl.ds(x, 1), :], block)
        partial[x] = jnp.where(row == ny - 1, outer_sens[pl.ds(nx + x, 1), :], block)
    copies = []
    for slot, x in start_columns(
        range(1, nx - 1), state, pulled, resistance, solid, flags, partial, None, None, start, partial
    ):
        copies.append(pltpu.make_async_copy(start.at[slot], far_start.at[:, x], done.at[slot]))
        copies[-1].start()
    for copy in copies:
        copy.wait()


def outer_kernel(
    far_inner, state, pulled, resistance, solid, flags, partial, from_left, from_right,
    far_start, total, start, done,
):
    del far_inner
    nx = resistance.shape[0]
    copies = []
    total[...] = partial[...]
    for slot, x in start_columns(
        (0, nx - 1), state, pulled, resistance, solid, flags, partial, from_left, from_right, start, total
    ):
        copies.append(pltpu.make_async_copy(start.at[slot], far_start.at[:, x], done.at[slot]))
        copies[-1].start()
    for copy in copies:
        copy.wait()


VMEM_LIMIT = 40 * 1024 * 1024
VMEM, HBM = (pl.BlockSpec(memory_space=m) for m in (pltpu.VMEM, pltpu.HBM))


def call(kernel, outs, *args, scratch=(), far=(), far_out=(), aliases=None):
    return pl.pallas_call(
        kernel,
        out_shape=[jax.ShapeDtypeStruct(s, jnp.float32) for s in outs],
        in_specs=[HBM if k in far else VMEM for k in range(len(args))],
        out_specs=[HBM if k in far_out else VMEM for k in range(len(outs))],
        scratch_shapes=[pltpu.VMEM(s, jnp.float32) if isinstance(s, tuple) else s for s in scratch],
        input_output_aliases=aliases or {},
        compiler_params=pltpu.CompilerParams(vmem_limit_bytes=VMEM_LIMIT),
    )(*args)


def in_hbm(*arrays):
    return [pltpu.with_memory_space_constraint(v, pltpu.HBM) for v in arrays]


def exchange(axis, onward, backward):
    count = lax.axis_size(axis)
    ahead = [(i, (i + 1) % count) for i in range(count)]
    behind = [(i, (i - 1) % count) for i in range(count)]
    return lax.ppermute(onward, axis, ahead), lax.ppermute(backward, axis, behind)


def body(checkpoint, adjoint_end, resistance, solid_mask, flags):
    nx, ny, nz = resistance.shape
    whole, voxels, rim = checkpoint.shape, resistance.shape, (19, 2 * nx, nz)
    cells = (resistance, solid_mask, flags)
    pair = [pltpu.VMEM((2, ny, nz), jnp.int32)] * 2
    right, left = call(
        face_kernel, [(10, ny, nz)] * 2, *in_hbm(checkpoint, adjoint_end, *cells), far=range(5),
        scratch=[(2, 19, ny, nz), (2, ny, nz), *pair, pltpu.SemaphoreType.DMA((18,))],
    )
    sides = exchange("gx", right, left)
    (post,) = call(post_kernel, [whole], checkpoint, *cells)
    up, down = call(
        rim_kernel, [(30, nx, nz)] * 2, post, adjoint_end, *cells, *sides,
        scratch=[(38, 2 * nx, nz)],
    )
    below, above = exchange("gy", up, down)
    out, sens, *rims = call(
        middle_kernel, [whole, voxels, rim, rim], post, adjoint_end, *cells, *sides,
        scratch=[whole, whole],
    )
    outer_rows, halo_rows, outer_sens, right, left = call(
        edge_kernel, [rim, rim, rim[1:], (5, ny, nz), (5, ny, nz)],
        out, *cells, *rims, up, down, below, above,
        scratch=[rim, rim, rim, (9, *rim[1:])],
    )
    sides = exchange("gx", right, left)
    start, pulled, partial = call(
        inner_kernel, [whole, whole, voxels],
        out, outer_rows, halo_rows, sens, outer_sens, checkpoint, *cells, far_out=(0,),
        scratch=[(nx - 2, 19, ny, nz), pltpu.SemaphoreType.DMA((nx - 2,))],
    )
    start, sensitivity = call(
        outer_kernel, [whole, voxels],
        *in_hbm(start), checkpoint, pulled, *cells, partial, *sides, far=(0,), far_out=(0,), aliases={0: 0},
        scratch=[(2, 19, ny, nz), pltpu.SemaphoreType.DMA((2,))],
    )
    return start, sensitivity


def solution(mesh):
    state, cell = P(None, "gx", "gy", None), P("gx", "gy", None)
    return jax.shard_map(
        body,
        mesh=mesh,
        in_specs=(state, state, cell, cell, cell),
        out_specs=(state, cell),
        check_vma=False,
    )
```

time: 35.8 us -> 27.4 us (0.77)
  waiting for transfers between devices: 18.1 us -> 11.5 us
  local copies, waits for them, and re-layouts: 5.11 us -> 0.02 us
  Pallas kernels: 4.93 us -> 8.02 us
    ppermute x3, waiting for transfers between devices: 9.83 us -> 4.37 us  [exchange(): lax.ppermute(onward, axis, ahead)]
    unnamed x16 -> x10, local copies, waits for them, and re-layouts: 5.11 us -> 0.02 us
    pallas_call x4 -> x7, Pallas kernels: 4.93 us -> 8.02 us  [call(): pl.pallas_call(kernel, out_shape=[jax.ShapeDtypeStruct(s, jnp.float32) fo...]
    ppermute x3, waiting for transfers between devices: 8.22 us -> 7.09 us  [exchange(): lax.ppermute(backward, axis, behind)]
  transfers between devices with their start and end apart: 6 -> 6, of which waited for: 6 -> 6; matrix products, arithmetic and copies ran while one was open for 0% -> 0% of each run, Pallas kernels for 0% -> 15%
where the time goes in v2:
time: 27.4 us; the launch traced here: 27.2 us
  waiting for transfers between devices  11.5 us (42%)
  Pallas kernels  8.02 us (29%)
  starting transfers between devices  7 us (26%)
  between operations  0.72 us (3%)
    pallas_call x7, Pallas kernels, call(): pl.pallas_call(kernel, out_shape=[jax.ShapeDtypeStruct(s, jnp.float32) fo...  8.02 us
    ppermute x3, waiting for transfers between devices, exchange(): lax.ppermute(backward, axis, behind)  7.09 us
    ppermute x3, starting transfers between devices, exchange(): lax.ppermute(onward, axis, ahead)  4.9 us
    ppermute x3, waiting for transfers between devices, exchange(): lax.ppermute(onward, axis, ahead)  4.37 us
    ppermute x3, starting transfers between devices, exchange(): lax.ppermute(backward, axis, behind)  2.1 us
  transfers between devices with their start and end apart: 6, of which 6 were waited for; matrix products, arithmetic and copies ran while one was open for 0% of the time, Pallas kernels for 15%

profile of v2, /device:TPU:3, one launch (start us, length us, event | category | flops | bytes accessed | tf_op | source)
XLA Modules:
  0.0 27.2 jit_solution(15510112089003559880)
XLA Ops:
  0.6 0.0 copy-start.4
  0.6 0.0 copy-start.3
  0.7 0.0 copy-start.2
  0.7 0.0 copy-start
  0.7 1.6 %shard_map.69 = (f32[10,16,256]{2,1,0:T(8,128)S(1)}, f32[10,16,256]{2,1,0:T(8,128)S(1)}) custom-call(f32[19,4,16,256]{3,2,1,0:T(8,128)} %state.5, f32[19,4,16,256]{3,2,1,0:T(8,128)} %adjoint.3, f32[4,16,256]{2,1,0:T(8,128)} %resistance.11, s32[4,16,256]{2,1,0:T(8,128)} %solid.11, s32[4,16,256]{2,1,0:T(8,128)} %flags.11), custom_call_target="tpu_custom_call" | custom-call | tf_op jit(solution)/shard_map/pallas_call | solution.py:503
  2.2 1.8 %collective-permute-start = (f32[10,16,256]{2,1,0:T(8,128)S(1)}, f32[10,16,256]{2,1,0:T(8,128)S(1)}, u32[]{:S(2)}, u32[]{:S(2)}) collective-permute-start(f32[10,16,256]{2,1,0:T(8,128)S(1)} %get-tuple-element.18), channel_id=1, source_target_pairs={{0,4},{4,8},{8,12},{12,16},{16,20},{20,24},{24,28},{28,0},{1,5},{5... | collective-permute-start | bytes 491528 | tf_op jit(solution)/shard_map/ppermute | solution.py:522
  4.1 0.0 copy-start.1
  4.1 0.0 collective-permute-start.1
  4.1 0.0 copy-done.4
  4.1 0.0 copy-done.3
  4.1 0.0 copy-done.2
  4.1 0.0 copy-done
  4.1 0.8 %shard_map.68.post = f32[19,4,16,256]{3,2,1,0:T(8,128)S(1)} custom-call(f32[19,4,16,256]{3,2,1,0:T(8,128)S(1)} %copy-done, f32[4,16,256]{2,1,0:T(8,128)S(1)} %copy-done.2, s32[4,16,256]{2,1,0:T(8,128)S(1)} %copy-done.3, s32[4,16,256]{2,1,0:T(8,128)S(1)} %copy-done.4), custom_call_target="tpu_custom_call" | custom-call | tf_op jit(solution)/shard_map/pallas_call | solution.py:503
  4.9 2.4 %collective-permute-done.from_left = f32[10,16,256]{2,1,0:T(8,128)S(1)} collective-permute-done((f32[10,16,256]{2,1,0:T(8,128)S(1)}, f32[10,16,256]{2,1,0:T(8,128)S(1)}, u32[]{:S(2)}, u32[]{:S(2)}) %collective-permute-start) | collective-permute-done | bytes 163872 | tf_op jit(solution)/shard_map/ppermute | solution.py:522
  7.3 2.5 %collective-permute-done.1.from_right = f32[10,16,256]{2,1,0:T(8,128)S(1)} collective-permute-done((f32[10,16,256]{2,1,0:T(8,128)S(1)}, f32[10,16,256]{2,1,0:T(8,128)S(1)}, u32[]{:S(2)}, u32[]{:S(2)}) %collective-permute-start.1) | collective-permute-done | bytes 163872 | tf_op jit(solution)/shard_map/ppermute | solution.py:522
  9.7 0.0 copy-done.1
  9.7 0.2 shard_map.71
  10.0 1.3 %collective-permute-start.2 = (f32[30,4,256]{2,1,0:T(4,128)S(1)}, f32[30,4,256]{2,1,0:T(4,128)S(1)}, u32[]{:S(2)}, u32[]{:S(2)}) collective-permute-start(f32[30,4,256]{2,1,0:T(4,128)S(1)} %get-tuple-element.23.up), channel_id=1, source_target_pairs={{0,1},{1,2},{2,3},{3,0},{4,5},{5,6},{6,7},{7,4},{8,9},{9,10},{10,1... | collective-permute-start | bytes 368648 | tf_op jit(solution)/shard_map/ppermute | solution.py:522
  11.3 2.1 %collective-permute-start.3 = (f32[30,4,256]{2,1,0:T(4,128)S(1)}, f32[30,4,256]{2,1,0:T(4,128)S(1)}, u32[]{:S(2)}, u32[]{:S(2)}) collective-permute-start(f32[30,4,256]{2,1,0:T(4,128)S(1)} %get-tuple-element.24.down), channel_id=1, source_target_pairs={{0,3},{1,0},{2,1},{3,2},{4,7},{5,4},{6,5},{7,6},{8,11},{9,8},{10,9... | collective-permute-start | bytes 368648 | tf_op jit(solution)/shard_map/ppermute | solution.py:522
  13.4 1.6 %shard_map.70 = (f32[19,4,16,256]{3,2,1,0:T(8,128)S(1)}, f32[4,16,256]{2,1,0:T(8,128)S(1)}, f32[19,8,256]{2,1,0:T(8,128)S(1)}, f32[19,8,256]{2,1,0:T(8,128)S(1)}) custom-call(f32[19,4,16,256]{3,2,1,0:T(8,128)S(1)} %shard_map.68.post, f32[19,4,16,256]{3,2,1,0:T(8,128)S(1)} %copy-done.1, f32[4,16,256]{2,1,0:T(8,128)S(1)} %copy-done.2, ...), custom_call_target="tpu_custom_call" | custom-call | tf_op jit(solution)/shard_map/pallas_call | solution.py:503
  15.0 1.9 %collective-permute-done.2.below = f32[30,4,256]{2,1,0:T(4,128)S(1)} collective-permute-done((f32[30,4,256]{2,1,0:T(4,128)S(1)}, f32[30,4,256]{2,1,0:T(4,128)S(1)}, u32[]{:S(2)}, u32[]{:S(2)}) %collective-permute-start.2) | collective-permute-done | bytes 122912 | tf_op jit(solution)/shard_map/ppermute | solution.py:522
  16.9 1.6 %collective-permute-done.3.above = f32[30,4,256]{2,1,0:T(4,128)S(1)} collective-permute-done((f32[30,4,256]{2,1,0:T(4,128)S(1)}, f32[30,4,256]{2,1,0:T(4,128)S(1)}, u32[]{:S(2)}, u32[]{:S(2)}) %collective-permute-start.3) | collective-permute-done | bytes 122912 | tf_op jit(solution)/shard_map/ppermute | solution.py:522
  18.5 0.3 %shard_map.72 = (f32[19,8,256]{2,1,0:T(8,128)S(1)}, f32[19,8,256]{2,1,0:T(8,128)S(1)}, f32[8,256]{1,0:T(8,128)S(1)}, f32[5,16,256]{2,1,0:T(8,128)S(1)}, f32[5,16,256]{2,1,0:T(8,128)S(1)}) custom-call(f32[19,4,16,256]{3,2,1,0:T(8,128)S(1)} %get-tuple-element.20.out, f32[4,16,256]{2,1,0:T(8,128)S(1)} %copy-done.2, s32[4,16,256]{2,1,0:T(8,128)S(1)} %copy-done.3, ...), custom_call_target="tpu_custom_call" | custom-call | tf_op jit(solution)/shard_map/pallas_call | solution.py:503
  18.8 1.7 %collective-permute-start.4 = (f32[5,16,256]{2,1,0:T(8,128)S(1)}, f32[5,16,256]{2,1,0:T(8,128)S(1)}, u32[]{:S(2)}, u32[]{:S(2)}) collective-permute-start(f32[5,16,256]{2,1,0:T(8,128)S(1)} %get-tuple-element.32), channel_id=1, source_target_pairs={{0,4},{4,8},{8,12},{12,16},{16,20},{20,24},{24,28},{28,0},{1,5},{5... | collective-permute-start | bytes 245768 | tf_op jit(solution)/shard_map/ppermute | solution.py:522
  20.5 0.0 collective-permute-start.5
  20.5 1.6 %shard_map.73 = (f32[19,4,16,256]{3,2,1,0:T(8,128)}, f32[19,4,16,256]{3,2,1,0:T(8,128)S(1)}, f32[4,16,256]{2,1,0:T(8,128)S(1)}) custom-call(f32[19,4,16,256]{3,2,1,0:T(8,128)S(1)} %get-tuple-element.20.out, f32[19,8,256]{2,1,0:T(8,128)S(1)} %get-tuple-element.25.outer_rows, f32[19,8,256]{2,1,0:T(8,128)S(1)} %get-tuple-element.26.halo_rows, ...), custom_call_target="tpu_custom_call" | custom-call | tf_op jit(solution)/shard_map/pallas_call | solution.py:503
  22.1 0.1 collective-permute-done.4.from_left
  22.2 3.1 %collective-permute-done.5.from_right = f32[5,16,256]{2,1,0:T(8,128)S(1)} collective-permute-done((f32[5,16,256]{2,1,0:T(8,128)S(1)}, f32[5,16,256]{2,1,0:T(8,128)S(1)}, u32[]{:S(2)}, u32[]{:S(2)}) %collective-permute-start.5) | collective-permute-done | bytes 81952 | tf_op jit(solution)/shard_map/ppermute | solution.py:522
  25.3 1.9 %shard_map.74 = (f32[19,4,16,256]{3,2,1,0:T(8,128)}, f32[4,16,256]{2,1,0:T(8,128)}) custom-call(f32[19,4,16,256]{3,2,1,0:T(8,128)} %get-tuple-element.29.far_inner, f32[19,4,16,256]{3,2,1,0:T(8,128)S(1)} %copy-done, f32[19,4,16,256]{3,2,1,0:T(8,128)S(1)} %get-tuple-element.30.pulled, f32[4,16,256]{2,1,0:T(8,128)S(1)} %copy-done.2, ...), custom_call_target="tpu_custom_call", output_to_operand_aliasing={{0}: (0, {})} | custom-call | tf_op jit(solution)/shard_map/pallas_call | solution.py:503
Async XLA Ops:
  0.6 3.4 %copy-start.4 = (s32[4,16,256]{2,1,0:T(8,128)S(1)}, s32[4,16,256]{2,1,0:T(8,128)}, u32[]{:S(2)}) copy-start(s32[4,16,256]{2,1,0:T(8,128)} %flags.11) | copy-start | bytes 196612
  0.6 3.4 %copy-start.3 = (s32[4,16,256]{2,1,0:T(8,128)S(1)}, s32[4,16,256]{2,1,0:T(8,128)}, u32[]{:S(2)}) copy-start(s32[4,16,256]{2,1,0:T(8,128)} %solid.11) | copy-start | bytes 196612
  0.7 3.4 %copy-start.2 = (f32[4,16,256]{2,1,0:T(8,128)S(1)}, f32[4,16,256]{2,1,0:T(8,128)}, u32[]{:S(2)}) copy-start(f32[4,16,256]{2,1,0:T(8,128)} %resistance.11) | copy-start | bytes 196612
  0.7 3.4 %copy-start = (f32[19,4,16,256]{3,2,1,0:T(8,128)S(1)}, f32[19,4,16,256]{3,2,1,0:T(8,128)}, u32[]{:S(2)}) copy-start(f32[19,4,16,256]{3,2,1,0:T(8,128)} %state.5) | copy-start | bytes 3735556
  2.2 5.0 %collective-permute-start = (f32[10,16,256]{2,1,0:T(8,128)S(1)}, f32[10,16,256]{2,1,0:T(8,128)S(1)}, u32[]{:S(2)}, u32[]{:S(2)}) collective-permute-start(f32[10,16,256]{2,1,0:T(8,128)S(1)} %get-tuple-element.18), channel_id=1, source_target_pairs={{0,4},{4,8},{8,12},{12,16},{16,20},{20,24},{24,28},{28,0},{1,5},{5... | collective-permute-start | bytes 491528 | tf_op jit(solution)/shard_map/ppermute | solution.py:522
  4.1 5.7 %copy-start.1 = (f32[19,4,16,256]{3,2,1,0:T(8,128)S(1)}, f32[19,4,16,256]{3,2,1,0:T(8,128)}, u32[]{:S(2)}) copy-start(f32[19,4,16,256]{3,2,1,0:T(8,128)} %adjoint.3) | copy-start | bytes 3735556
  4.1 5.7 %collective-permute-start.1 = (f32[10,16,256]{2,1,0:T(8,128)S(1)}, f32[10,16,256]{2,1,0:T(8,128)S(1)}, u32[]{:S(2)}, u32[]{:S(2)}) collective-permute-start(f32[10,16,256]{2,1,0:T(8,128)S(1)} %get-tuple-element.19), channel_id=1, source_target_pairs={{0,28},{4,0},{8,4},{12,8},{16,12},{20,16},{24,20},{28,24},{1,29},{... | collective-permute-start | bytes 491528 | tf_op jit(solution)/shard_map/ppermute | solution.py:522
  10.0 6.9 %collective-permute-start.2 = (f32[30,4,256]{2,1,0:T(4,128)S(1)}, f32[30,4,256]{2,1,0:T(4,128)S(1)}, u32[]{:S(2)}, u32[]{:S(2)}) collective-permute-start(f32[30,4,256]{2,1,0:T(4,128)S(1)} %get-tuple-element.23.up), channel_id=1, source_target_pairs={{0,1},{1,2},{2,3},{3,0},{4,5},{5,6},{6,7},{7,4},{8,9},{9,10},{10,1... | collective-permute-start | bytes 368648 | tf_op jit(solution)/shard_map/ppermute | solution.py:522
  11.3 7.2 %collective-permute-start.3 = (f32[30,4,256]{2,1,0:T(4,128)S(1)}, f32[30,4,256]{2,1,0:T(4,128)S(1)}, u32[]{:S(2)}, u32[]{:S(2)}) collective-permute-start(f32[30,4,256]{2,1,0:T(4,128)S(1)} %get-tuple-element.24.down), channel_id=1, source_target_pairs={{0,3},{1,0},{2,1},{3,2},{4,7},{5,4},{6,5},{7,6},{8,11},{9,8},{10,9... | collective-permute-start | bytes 368648 | tf_op jit(solution)/shard_map/ppermute | solution.py:522
  18.8 3.4 %collective-permute-start.4 = (f32[5,16,256]{2,1,0:T(8,128)S(1)}, f32[5,16,256]{2,1,0:T(8,128)S(1)}, u32[]{:S(2)}, u32[]{:S(2)}) collective-permute-start(f32[5,16,256]{2,1,0:T(8,128)S(1)} %get-tuple-element.32), channel_id=1, source_target_pairs={{0,4},{4,8},{8,12},{12,16},{16,20},{20,24},{24,28},{28,0},{1,5},{5... | collective-permute-start | bytes 245768 | tf_op jit(solution)/shard_map/ppermute | solution.py:522
  20.5 4.8 %collective-permute-start.5 = (f32[5,16,256]{2,1,0:T(8,128)S(1)}, f32[5,16,256]{2,1,0:T(8,128)S(1)}, u32[]{:S(2)}, u32[]{:S(2)}) collective-permute-start(f32[5,16,256]{2,1,0:T(8,128)S(1)} %get-tuple-element.33), channel_id=1, source_target_pairs={{0,28},{4,0},{8,4},{12,8},{16,12},{20,16},{24,20},{28,24},{1,29},{... | collective-permute-start | bytes 245768 | tf_op jit(solution)/shard_map/ppermute | solution.py:522

commit v3 on v2

--- a/solution.py
+++ b/solution.py
@@ -103,9 +103,15 @@
     return finish(rest, f, odd_sums, even, odd, grey, 1.0 - grey)
 
 
-def adjoint_at(lam, density, momentum, grey, rate):
-    inverse = 1.0 / density
-    u = [m * inverse for m in momentum]
+def by_velocity(weights, cross, u):
+    return [
+        weights[0] * u[0] + cross[2] * u[1] + cross[1] * u[2],
+        weights[1] * u[1] + cross[2] * u[0] + cross[0] * u[2],
+        weights[2] * u[2] + cross[1] * u[0] + cross[0] * u[1],
+    ]
+
+
+def adjoint_at(lam, u, grey, rate):
     faces, planes, shears, axes, odd_sums = grouped(lam)
     total = faces[0] + faces[1] + faces[2]
     edges = planes[0] + planes[1] + planes[2]
@@ -125,12 +131,10 @@
         weights.append(2.0 * bulk + (1.0 / 9.0) * stress - (1.0 / 36.0) * other)
     w_shears = [rate * v for v in shears]
     cross = [0.25 * v for v in w_shears]
-    pull = [
-        weights[0] * u[0] + cross[2] * u[1] + cross[1] * u[2],
-        weights[1] * u[1] + cross[2] * u[0] + cross[0] * u[2],
-        weights[2] * u[2] + cross[1] * u[0] + cross[0] * u[1],
-    ]
-    by_density = 3.0 * square - 11.0 * energy - 0.5 * (u[0] * pull[0] + u[1] * pull[1] + u[2] * pull[2])
+    pull = by_velocity(weights, cross, u) if u else [0.0] * 3
+    by_density = 3.0 * square - 11.0 * energy
+    if u:
+        by_density = by_density - 0.5 * (u[0] * pull[0] + u[1] * pull[1] + u[2] * pull[2])
     for a in range(3):
         d, p, r = axes[a]
         flux = p + r - 4.0 * d
@@ -146,14 +150,15 @@
     for a in range(3):
         (wd, wa, wb), (ld, lp, lr) = w_axes[a], axes[a]
         w_axes[a] = (wd - 2.0 * ld, wa - 2.0 * lp, wb - 2.0 * lr)
-    return out, (rest, w_faces, w_planes, w_shears, w_axes)
+    return out, (rest, w_faces, w_planes, w_shears, w_axes), (weights, cross)
 
 
 def adjoint_tile(lam, f, grey, rate):
     faces, planes, shears, axes, _ = grouped(f)
     momentum = [d + a + b for d, a, b in axes]
-    density = f[0] + (faces[0] + faces[1] + faces[2]) + (planes[0] + planes[1] + planes[2])
-    out, (rest, w_faces, w_planes, w_shears, w_axes) = adjoint_at(lam, density, momentum, grey, rate)
+    inverse = 1.0 / (f[0] + (faces[0] + faces[1] + faces[2]) + (planes[0] + planes[1] + planes[2]))
+    u = [m * inverse for m in momentum]
+    out, (rest, w_faces, w_planes, w_shears, w_axes), _ = adjoint_at(lam, u, grey, rate)
     near, far = 0.0, 0.0
     for a in range(3):
         (wd, wa, wb), (d, p, r) = w_axes[a], axes[a]
@@ -174,15 +179,17 @@
     return [i for i in range(19) if sign * VELOCITY[i][dim] == step]
 
 
-NEAR, FAR_EDGE, GREY, RATE = 9, 23, 28, 29
+SHARE, AT_REST, WEIGHTS, GREY, RATE, PLANES = 0, 9, 14, 25, 26, 27
 
 
 def edge_plane(field, way, i):
-    return (4, FAR_EDGE)[field] + moving(1 - 2 * field, 1, way).index(i)
-
-
-def near_plane(way, i):
-    return NEAR + (moving(-1, 1, 0) + moving(-1, 1, way)).index(i)
+    return (4, 20)[field] + moving(1 - 2 * field, 1, way).index(i)
+
+
+def halo_terms(lam, grey, rate):
+    out, _, (weights, cross) = adjoint_at(lam, None, grey, rate)
+    free = 1.0 - grey
+    return out, [free * v for v in (*weights, *cross)]
 
 
 def x_plane(field, i):
@@ -253,29 +260,44 @@
             copy.wait()
 
 
-def post_kernel(state, resistance, solid, flags, post):
+def post_kernel(
+    far_state, far_adjoint, far_resistance, far_solid, far_flags,
+    post, state, adjoint, resistance, solid, flags, done,
+):
     nx, ny, nz = resistance.shape
-    tiles = ny // 8
-
-    def step(n, carry):
-        x, rows = n // tiles, pl.ds(pl.multiple_of(n % tiles * 8, 8), 8)
-        for half in range(nz // 128):
-            at = (x, rows, pl.ds(half * 128, 128))
-            out = collide_tile(
-                [state[(i, *at)] for i in range(19)],
-                greyness(resistance[at], solid[at]),
-                shear_rate(flags[at]),
-            )
-            for i in range(19):
-                post[(i, *at)] = out[i]
-        return carry
-
-    lax.fori_loop(0, nx * tiles, step, 0)
-
-
-def rim_kernel(post, adjoint, resistance, solid, flags, from_left, from_right, up, down, work):
+    pairs = [(far_resistance, resistance), (far_solid, solid), (far_flags, flags)]
+    pairs += [(far_state.at[:, x], state.at[:, x]) for x in range(nx)] + [(far_adjoint, adjoint)]
+    copies = [pltpu.make_async_copy(*pair, done.at[k]) for k, pair in enumerate(pairs)]
+    for copy in copies:
+        copy.start()
+    for copy in copies[:3]:
+        copy.wait()
+    for x in range(nx):
+        copies[3 + x].wait()
+
+        def step(t, carry, x=x):
+            rows = pl.ds(pl.multiple_of(t * 8, 8), 8)
+            for half in range(nz // 128):
+                at = (x, rows, pl.ds(half * 128, 128))
+                out = collide_tile(
+                    [state[(i, *at)] for i in range(19)],
+                    greyness(resistance[at], solid[at]),
+                    shear_rate(flags[at]),
+                )
+                for i in range(19):
+                    post[(i, *at)] = out[i]
+            return carry
+
+        lax.fori_loop(0, ny // 8, step, 0)
+    copies[-1].wait()
+
+
+def rim_kernel(
+    post, adjoint, resistance, solid, flags, from_left, from_right, up, down, work, near, cells
+):
     nx, ny, nz = resistance.shape
     shares = {1: [0.0] * 4, -1: [0.0] * 4}
+    halves = (slice(0, nx), slice(nx, 2 * nx))
     for field, source in ((0, post), (1, adjoint)):
         for i in range(19):
             vx, vy, vz = velocity(field, i)
@@ -298,23 +320,37 @@
             if vz:
                 tile[...] = shifted_z(tile[...], vz)
             for half in range(2):
-                value = tile[half * nx : half * nx + nx, :]
+                value = tile[halves[half]]
                 way = vy if vy else 1 - 2 * half
                 message = up if way == 1 else down
                 if vy and half == 1:
                     message[edge_plane(field, way, i)] = value
                 elif field == 1:
-                    message[near_plane(way, i)] = value
+                    side = 0 if way == 1 else 1
+                    near[i, halves[side], :] = value
+                    if vy:
+                        near[i, halves[1 - side], :] = jnp.zeros_like(value)
                 else:
                     share = shares[way]
                     for k, factor in enumerate((1, vx, vy, vz)):
                         if factor:
                             share[k] = share[k] + factor * value
-    for way, message, row in ((1, up, ny - 1), (-1, down, 0)):
+    for way, message, row, half in ((1, up, ny - 1, halves[0]), (-1, down, 0, halves[1])):
         for k in range(4):
-            message[k] = shares[way][k]
-        message[GREY] = greyness(resistance[:, row, :], solid[:, row, :])
-        message[RATE] = shear_rate(flags[:, row, :])
+            message[SHARE + k] = shares[way][k]
+        cells[0, half, :] = message[GREY] = greyness(resistance[:, row, :], solid[:, row, :])
+        cells[1, half, :] = message[RATE] = shear_rate(flags[:, row, :])
+    for part in range(nz // 128):
+        lanes = pl.ds(part * 128, 128)
+        at = (slice(None), lanes)
+        out, weights = halo_terms(
+            [near[(i, *at)] for i in range(19)], cells[(0, *at)], cells[(1, *at)]
+        )
+        for way, message, half in ((1, up, halves[0]), (-1, down, halves[1])):
+            for k, i in enumerate(moving(-1, 1, way)):
+                message[AT_REST + k, :, lanes] = out[i][half]
+            for k in range(6):
+                message[WEIGHTS + k, :, lanes] = weights[k][half]
 
 
 def middle_kernel(
@@ -372,7 +408,7 @@
 
 def edge_kernel(
     out, resistance, solid, flags, rim_middle, rim_cotangent, up, down, below, above,
-    outer_rows, halo_rows, outer_sens, right, left, middle, cotangent, halo, cells,
+    outer_rows, halo_rows, outer_sens, right, left, middle, cotangent, cells,
 ):
     nx, ny, nz = resistance.shape
     low, high = slice(0, nx), slice(nx, 2 * nx)
@@ -384,47 +420,52 @@
                 target[i, low, :] = below[edge_plane(field, 1, i)]
             if vy == -1:
                 target[i, high, :] = above[edge_plane(field, -1, i)]
-    for i in range(19):
-        vy = velocity(1, i)[1]
-        halo[i, low, :] = down[edge_plane(1, -1, i)] if vy == -1 else below[near_plane(1, i)]
-        halo[i, high, :] = up[edge_plane(1, 1, i)] if vy == 1 else above[near_plane(-1, i)]
-    for rows, way, received, sent in ((low, -1, below, down), (high, 1, above, up)):
-        share = [received[k] for k in range(4)]
-        for i in moving(1, 1, way):
-            value = sent[edge_plane(0, way, i)]
+    for rows, way, received, sent in ((low, 1, below, down), (high, -1, above, up)):
+        share = [received[SHARE + k] for k in range(4)]
+        for i in moving(1, 1, -way):
+            value = sent[edge_plane(0, -way, i)]
             for k, factor in enumerate((1, *VELOCITY[i])):
                 if factor:
                     share[k] = share[k] + factor * value
-        for k in range(4):
-            cells[k, rows, :] = share[k]
-        cells[4, rows, :] = received[GREY]
-        cells[5, rows, :] = received[RATE]
-        row = 0 if way == -1 else ny - 1
+        u = [v / share[0] for v in share[1:]]
+        lam = [jnp.zeros_like(share[0])] * 19
+        for i in moving(-1, 1, -way):
+            lam[i] = sent[edge_plane(1, -way, i)]
+        own, weights = halo_terms(lam, received[GREY], received[RATE])
+        weights = [v + received[WEIGHTS + k] for k, v in enumerate(weights)]
+        pull = by_velocity(weights[:3], weights[3:], u)
+        scale = 0.5 * (u[0] * pull[0] + u[1] * pull[1] + u[2] * pull[2])
+        for k, i in enumerate(moving(-1, 1, way)):
+            value = own[i] + received[AT_REST + k] - scale
+            for a in range(3):
+                if VELOCITY[i][a]:
+                    value = value + VELOCITY[i][a] * pull[a]
+            halo_rows[i, rows, :] = value
+        row = 0 if way == 1 else ny - 1
         blocked = solid[:, row, :]
-        cells[6, rows, :] = greyness(resistance[:, row, :], blocked)
-        cells[7, rows, :] = shear_rate(flags[:, row, :])
-        cells[8, rows, :] = jnp.where(blocked == 1, 0.0, 1.0)
+        cells[0, rows, :] = greyness(resistance[:, row, :], blocked)
+        cells[1, rows, :] = shear_rate(flags[:, row, :])
+        cells[2, rows, :] = jnp.where(blocked == 1, 0.0, 1.0)
     for part in range(nz // 128):
         at = (slice(None), pl.ds(part * 128, 128))
         state = [middle[(i, *at)] for i in range(19)]
         new, sens = adjoint_tile(
-            [cotangent[(i, *at)] for i in range(19)], state, cells[(6, *at)], cells[(7, *at)]
+            [cotangent[(i, *at)] for i in range(19)], state, cells[(0, *at)], cells[(1, *at)]
         )
-        outer_sens[at] = jnp.where(cells[(8, *at)] == 0.0, 0.0, sens)
+        outer_sens[at] = jnp.where(cells[(2, *at)] == 0.0, 0.0, sens)
         for i in range(19):
             outer_rows[(i, *at)] = new[i]
-        lam = [halo[(i, *at)] for i in range(19)]
-        density, *momentum = [cells[(k, *at)] for k in range(4)]
-        new, _ = adjoint_at(lam, density, momentum, cells[(4, *at)], cells[(5, *at)])
-        for i in range(19):
-            halo_rows[(i, *at)] = new[i]
     for message, way, x in ((right, 1, nx - 1), (left, -1, 0)):
         for k, i in enumerate(moving(-1, 0, way)):
             message[k] = pulled_block(out, outer_rows, halo_rows, i, x)
 
 
-def start_columns(columns, state, pulled, resistance, solid, flags, partial, from_left, from_right, start, total):
+def start_columns(
+    columns, state, pulled, resistance, solid, flags, partial, from_left, from_right,
+    start, total, far_start, far_total, done,
+):
     nx, ny, nz = resistance.shape
+    copies = []
     for slot, x in enumerate(columns):
 
         def step(t, carry, x=x, slot=slot):
@@ -449,16 +490,21 @@
                 )
                 for i in range(19):
                     start[slot, i, rows, lanes] = new[i]
-                total[at] = partial[at] + jnp.where(solid[at] == 1, 0.0, sens)
+                total[slot, rows, lanes] = partial[at] + jnp.where(solid[at] == 1, 0.0, sens)
             return carry
 
         lax.fori_loop(0, ny // 8, step, 0)
-        yield slot, x
+        pairs = ((start.at[slot], far_start.at[:, x]), (total.at[slot], far_total.at[x]))
+        for k, pair in enumerate(pairs):
+            copies.append(pltpu.make_async_copy(*pair, done.at[2 * slot + k]))
+            copies[-1].start()
+    for copy in copies:
+        copy.wait()
 
 
 def inner_kernel(
     out, outer_rows, halo_rows, sens, outer_sens, state, resistance, solid, flags,
-    far_start, pulled, partial, start, done,
+    far_start, far_total, pulled, partial, start, total, done,
 ):
     nx, ny = resistance.shape[:2]
     for x in range(nx):
@@ -468,31 +514,21 @@
         row = lax.broadcasted_iota(jnp.int32, block.shape, 0)
         block = jnp.where(row == 0, outer_sens[pl.ds(x, 1), :], block)
         partial[x] = jnp.where(row == ny - 1, outer_sens[pl.ds(nx + x, 1), :], block)
-    copies = []
-    for slot, x in start_columns(
-        range(1, nx - 1), state, pulled, resistance, solid, flags, partial, None, None, start, partial
-    ):
-        copies.append(pltpu.make_async_copy(start.at[slot], far_start.at[:, x], done.at[slot]))
-        copies[-1].start()
-    for copy in copies:
-        copy.wait()
+    start_columns(
+        range(1, nx - 1), state, pulled, resistance, solid, flags, partial, None, None,
+        start, total, far_start, far_total, done,
+    )
 
 
 def outer_kernel(
-    far_inner, state, pulled, resistance, solid, flags, partial, from_left, from_right,
-    far_start, total, start, done,
-):
-    del far_inner
-    nx = resistance.shape[0]
-    copies = []
-    total[...] = partial[...]
-    for slot, x in start_columns(
-        (0, nx - 1), state, pulled, resistance, solid, flags, partial, from_left, from_right, start, total
-    ):
-        copies.append(pltpu.make_async_copy(start.at[slot], far_start.at[:, x], done.at[slot]))
-        copies[-1].start()
-    for copy in copies:
-        copy.wait()
+    inner_start, inner_total, state, pulled, resistance, solid, flags, partial, from_left, from_right,
+    far_start, far_total, start, total, done,
+):
+    del inner_start, inner_total
+    start_columns(
+        (0, resistance.shape[0] - 1), state, pulled, resistance, solid, flags, partial, from_left,
+        from_right, start, total, far_start, far_total, done,
+    )
 
 
 VMEM_LIMIT = 40 * 1024 * 1024
@@ -500,9 +536,10 @@
 
 
 def call(kernel, outs, *args, scratch=(), far=(), far_out=(), aliases=None):
+    made = [v if isinstance(v, jax.ShapeDtypeStruct) else jax.ShapeDtypeStruct(v, jnp.float32) for v in outs]
     return pl.pallas_call(
         kernel,
-        out_shape=[jax.ShapeDtypeStruct(s, jnp.float32) for s in outs],
+        out_shape=made,
         in_specs=[HBM if k in far else VMEM for k in range(len(args))],
         out_specs=[HBM if k in far_out else VMEM for k in range(len(outs))],
         scratch_shapes=[pltpu.VMEM(s, jnp.float32) if isinstance(s, tuple) else s for s in scratch],
@@ -525,17 +562,20 @@
 def body(checkpoint, adjoint_end, resistance, solid_mask, flags):
     nx, ny, nz = resistance.shape
     whole, voxels, rim = checkpoint.shape, resistance.shape, (19, 2 * nx, nz)
-    cells = (resistance, solid_mask, flags)
+    far = in_hbm(checkpoint, adjoint_end, resistance, solid_mask, flags)
     pair = [pltpu.VMEM((2, ny, nz), jnp.int32)] * 2
     right, left = call(
-        face_kernel, [(10, ny, nz)] * 2, *in_hbm(checkpoint, adjoint_end, *cells), far=range(5),
+        face_kernel, [(10, ny, nz)] * 2, *far, far=range(5),
         scratch=[(2, 19, ny, nz), (2, ny, nz), *pair, pltpu.SemaphoreType.DMA((18,))],
     )
     sides = exchange("gx", right, left)
-    (post,) = call(post_kernel, [whole], checkpoint, *cells)
+    post, checkpoint, adjoint_end, *cells = call(
+        post_kernel, [whole] + [jax.ShapeDtypeStruct(v.shape, v.dtype) for v in far],
+        *far, far=range(5), scratch=[pltpu.SemaphoreType.DMA((nx + 4,))],
+    )
     up, down = call(
-        rim_kernel, [(30, nx, nz)] * 2, post, adjoint_end, *cells, *sides,
-        scratch=[(38, 2 * nx, nz)],
+        rim_kernel, [(PLANES, nx, nz)] * 2, post, adjoint_end, *cells, *sides,
+        scratch=[(38, *rim[1:]), rim, (2, *rim[1:])],
     )
     below, above = exchange("gy", up, down)
     out, sens, *rims = call(
@@ -545,18 +585,19 @@
     outer_rows, halo_rows, outer_sens, right, left = call(
         edge_kernel, [rim, rim, rim[1:], (5, ny, nz), (5, ny, nz)],
         out, *cells, *rims, up, down, below, above,
-        scratch=[rim, rim, rim, (9, *rim[1:])],
+        scratch=[rim, rim, (3, *rim[1:])],
     )
     sides = exchange("gx", right, left)
-    start, pulled, partial = call(
-        inner_kernel, [whole, whole, voxels],
-        out, outer_rows, halo_rows, sens, outer_sens, checkpoint, *cells, far_out=(0,),
-        scratch=[(nx - 2, 19, ny, nz), pltpu.SemaphoreType.DMA((nx - 2,))],
+    *done, pulled, partial = call(
+        inner_kernel, [whole, voxels, whole, voxels],
+        out, outer_rows, halo_rows, sens, outer_sens, checkpoint, *cells, far_out=(0, 1),
+        scratch=[(nx - 2, 19, ny, nz), (nx - 2, ny, nz), pltpu.SemaphoreType.DMA((2 * nx - 4,))],
     )
     start, sensitivity = call(
         outer_kernel, [whole, voxels],
-        *in_hbm(start), checkpoint, pulled, *cells, partial, *sides, far=(0,), far_out=(0,), aliases={0: 0},
-        scratch=[(2, 19, ny, nz), pltpu.SemaphoreType.DMA((2,))],
+        *in_hbm(*done), checkpoint, pulled, *cells, partial, *sides,
+        far=(0, 1), far_out=(0, 1), aliases={0: 0, 1: 1},
+        scratch=[(2, 19, ny, nz), (2, ny, nz), pltpu.SemaphoreType.DMA((4,))],
     )
     return start, sensitivity
 

time: 27.4 us -> 26.2 us (0.956)
  waiting for transfers between devices: 11.5 us -> 9.84 us
  Pallas kernels: 8.02 us -> 8.5 us
    ppermute x3, waiting for transfers between devices: 4.37 us -> 2.74 us  [exchange(): lax.ppermute(onward, axis, ahead)]
    pallas_call x7, Pallas kernels: 8.02 us -> 8.5 us  [call(): pl.pallas_call(kernel, out_shape=made, in_specs=[HBM if k in far else VME...]
  transfers between devices with their start and end apart: 6 -> 6, of which waited for: 6 -> 6; matrix products, arithmetic and copies ran while one was open for 0% -> 0% of each run, Pallas kernels for 15% -> 20%
where the time goes in v3:
time: 26.2 us; the launch traced here: 26 us
  waiting for transfers between devices  9.84 us (38%)
  Pallas kernels  8.5 us (32%)
  starting transfers between devices  6.99 us (27%)
  between operations  0.67 us (3%)
    pallas_call x7, Pallas kernels, call(): pl.pallas_call(kernel, out_shape=made, in_specs=[HBM if k in far else VME...  8.5 us
    ppermute x3, waiting for transfers between devices, exchange(): lax.ppermute(backward, axis, behind)  7.1 us
    ppermute x3, starting transfers between devices, exchange(): lax.ppermute(onward, axis, ahead)  4.9 us
    ppermute x3, waiting for transfers between devices, exchange(): lax.ppermute(onward, axis, ahead)  2.74 us
    ppermute x3, starting transfers between devices, exchange(): lax.ppermute(backward, axis, behind)  2.1 us
  transfers between devices with their start and end apart: 6, of which 6 were waited for; matrix products, arithmetic and copies ran while one was open for 0% of the time, Pallas kernels for 20%

profile of v3, /device:TPU:3, one launch (start us, length us, event | category | flops | bytes accessed | tf_op | source)
XLA Modules:
  0.0 26.0 jit_solution(15434227408641298324)
XLA Ops:
  0.6 1.5 %shard_map.69 = (f32[10,16,256]{2,1,0:T(8,128)S(1)}, f32[10,16,256]{2,1,0:T(8,128)S(1)}) custom-call(f32[19,4,16,256]{3,2,1,0:T(8,128)} %far_state.3, f32[19,4,16,256]{3,2,1,0:T(8,128)} %far_adjoint.3, f32[4,16,256]{2,1,0:T(8,128)} %far_resistance.3, s32[4,16,256]{2,1,0:T(8,128)} %far_solid.3, s32[4,16,256]{2,1,0:T(8,128)} %far_flags.3), custom_call_target="tpu_custom_call" | custom-call | tf_op jit(solution)/shard_map/pallas_call | solution.py:540
  2.1 1.8 %collective-permute-start = (f32[10,16,256]{2,1,0:T(8,128)S(1)}, f32[10,16,256]{2,1,0:T(8,128)S(1)}, u32[]{:S(2)}, u32[]{:S(2)}) collective-permute-start(f32[10,16,256]{2,1,0:T(8,128)S(1)} %get-tuple-element.30), channel_id=1, source_target_pairs={{0,4},{4,8},{8,12},{12,16},{16,20},{20,24},{24,28},{28,0},{1,5},{5... | collective-permute-start | bytes 491528 | tf_op jit(solution)/shard_map/ppermute | solution.py:559
  4.0 0.0 collective-permute-start.1
  4.0 1.9 %shard_map.68 = (f32[19,4,16,256]{3,2,1,0:T(8,128)S(1)}, f32[19,4,16,256]{3,2,1,0:T(8,128)S(1)}, f32[19,4,16,256]{3,2,1,0:T(8,128)S(1)}, f32[4,16,256]{2,1,0:T(8...) custom-call(f32[19,4,16,256]{3,2,1,0:T(8,128)} %far_state.3, f32[19,4,16,256]{3,2,1,0:T(8,128)} %far_adjoint.3, ...), custom_call_target="tpu_custom_call" | custom-call | tf_op jit(solution)/shard_map/pallas_call | solution.py:540
  5.8 1.3 %collective-permute-done.from_left = f32[10,16,256]{2,1,0:T(8,128)S(1)} collective-permute-done((f32[10,16,256]{2,1,0:T(8,128)S(1)}, f32[10,16,256]{2,1,0:T(8,128)S(1)}, u32[]{:S(2)}, u32[]{:S(2)}) %collective-permute-start) | collective-permute-done | bytes 163872 | tf_op jit(solution)/shard_map/ppermute | solution.py:559
  7.2 2.5 %collective-permute-done.1.from_right = f32[10,16,256]{2,1,0:T(8,128)S(1)} collective-permute-done((f32[10,16,256]{2,1,0:T(8,128)S(1)}, f32[10,16,256]{2,1,0:T(8,128)S(1)}, u32[]{:S(2)}, u32[]{:S(2)}) %collective-permute-start.1) | collective-permute-done | bytes 163872 | tf_op jit(solution)/shard_map/ppermute | solution.py:559
  9.6 0.3 %shard_map.71 = (f32[27,4,256]{2,1,0:T(4,128)S(1)}, f32[27,4,256]{2,1,0:T(4,128)S(1)}) custom-call(f32[19,4,16,256]{3,2,1,0:T(8,128)S(1)} %get-tuple-element.25.post, f32[19,4,16,256]{3,2,1,0:T(8,128)S(1)} %get-tuple-element.26.adjoint, f32[4,16,256]{2,1,0:T(8,128)S(1)} %get-tuple-element.27.resistance, s32[4,16,256]{2,1,0:T(8,128)S(1)} %get-tuple-element.28.solid, ...), custom_call_target="tpu_custom_call" | custom-call | tf_op jit(solution)/shard_map/pallas_call | solution.py:540
  10.0 1.3 %collective-permute-start.2 = (f32[27,4,256]{2,1,0:T(4,128)S(1)}, f32[27,4,256]{2,1,0:T(4,128)S(1)}, u32[]{:S(2)}, u32[]{:S(2)}) collective-permute-start(f32[27,4,256]{2,1,0:T(4,128)S(1)} %get-tuple-element.35.up), channel_id=1, source_target_pairs={{0,1},{1,2},{2,3},{3,0},{4,5},{5,6},{6,7},{7,4},{8,9},{9,10},{10,1... | collective-permute-start | bytes 331784 | tf_op jit(solution)/shard_map/ppermute | solution.py:559
  11.3 2.1 %collective-permute-start.3 = (f32[27,4,256]{2,1,0:T(4,128)S(1)}, f32[27,4,256]{2,1,0:T(4,128)S(1)}, u32[]{:S(2)}, u32[]{:S(2)}) collective-permute-start(f32[27,4,256]{2,1,0:T(4,128)S(1)} %get-tuple-element.36.down), channel_id=1, source_target_pairs={{0,3},{1,0},{2,1},{3,2},{4,7},{5,4},{6,5},{7,6},{8,11},{9,8},{10,9... | collective-permute-start | bytes 331784 | tf_op jit(solution)/shard_map/ppermute | solution.py:559
  13.4 1.6 %shard_map.70 = (f32[19,4,16,256]{3,2,1,0:T(8,128)S(1)}, f32[4,16,256]{2,1,0:T(8,128)S(1)}, f32[19,8,256]{2,1,0:T(8,128)S(1)}, f32[19,8,256]{2,1,0:T(8,128)S(1)}) custom-call(f32[19,4,16,256]{3,2,1,0:T(8,128)S(1)} %get-tuple-element.25.post, f32[19,4,16,256]{3,2,1,0:T(8,128)S(1)} %get-tuple-element.26.adjoint, ...), custom_call_target="tpu_custom_call" | custom-call | tf_op jit(solution)/shard_map/pallas_call | solution.py:540
  15.0 1.3 %collective-permute-done.2.below = f32[27,4,256]{2,1,0:T(4,128)S(1)} collective-permute-done((f32[27,4,256]{2,1,0:T(4,128)S(1)}, f32[27,4,256]{2,1,0:T(4,128)S(1)}, u32[]{:S(2)}, u32[]{:S(2)}) %collective-permute-start.2) | collective-permute-done | bytes 110624 | tf_op jit(solution)/shard_map/ppermute | solution.py:559
  16.4 1.6 %collective-permute-done.3.above = f32[27,4,256]{2,1,0:T(4,128)S(1)} collective-permute-done((f32[27,4,256]{2,1,0:T(4,128)S(1)}, f32[27,4,256]{2,1,0:T(4,128)S(1)}, u32[]{:S(2)}, u32[]{:S(2)}) %collective-permute-start.3) | collective-permute-done | bytes 110624 | tf_op jit(solution)/shard_map/ppermute | solution.py:559
  17.9 0.2 shard_map.72
  18.2 1.7 %collective-permute-start.4 = (f32[5,16,256]{2,1,0:T(8,128)S(1)}, f32[5,16,256]{2,1,0:T(8,128)S(1)}, u32[]{:S(2)}, u32[]{:S(2)}) collective-permute-start(f32[5,16,256]{2,1,0:T(8,128)S(1)} %get-tuple-element.46), channel_id=1, source_target_pairs={{0,4},{4,8},{8,12},{12,16},{16,20},{20,24},{24,28},{28,0},{1,5},{5... | collective-permute-start | bytes 245768 | tf_op jit(solution)/shard_map/ppermute | solution.py:559
  19.9 0.0 collective-permute-start.5
  19.9 1.6 %shard_map.73 = (f32[19,4,16,256]{3,2,1,0:T(8,128)}, f32[4,16,256]{2,1,0:T(8,128)}, f32[19,4,16,256]{3,2,1,0:T(8,128)S(1)}, f32[4,16,256]{2,1,0:T(8,128)S(1)}) custom-call(f32[19,4,16,256]{3,2,1,0:T(8,128)S(1)} %get-tuple-element.32.out, f32[19,8,256]{2,1,0:T(8,128)S(1)} %get-tuple-element.37.outer_rows, f32[19,8,256]{2,1,0:T(8,128)S(1)} %get-tuple-element.38.halo_rows, ...), custom_call_target="tpu_custom_call" | custom-call | tf_op jit(solution)/shard_map/pallas_call | solution.py:540
  21.6 0.1 collective-permute-done.4.from_left
  21.6 3.1 %collective-permute-done.5.from_right = f32[5,16,256]{2,1,0:T(8,128)S(1)} collective-permute-done((f32[5,16,256]{2,1,0:T(8,128)S(1)}, f32[5,16,256]{2,1,0:T(8,128)S(1)}, u32[]{:S(2)}, u32[]{:S(2)}) %collective-permute-start.5) | collective-permute-done | bytes 81952 | tf_op jit(solution)/shard_map/ppermute | solution.py:559
  24.7 1.3 %shard_map.74 = (f32[19,4,16,256]{3,2,1,0:T(8,128)}, f32[4,16,256]{2,1,0:T(8,128)}) custom-call(f32[19,4,16,256]{3,2,1,0:T(8,128)} %get-tuple-element.42.inner_start, f32[4,16,256]{2,1,0:T(8,128)} %get-tuple-element.43.inner_total, f32[19,4,16,256]{3,2,1,0:T(8,128)S(1)} %get-tuple-element.41.state, ...), custom_call_target="tpu_custom_call", output_to_operand_aliasing={{0}: (0, {}), {1}: (1, {})} | custom-call | tf_op jit(solution)/shard_map/pallas_call | solution.py:540
Async XLA Ops:
  2.1 5.0 %collective-permute-start = (f32[10,16,256]{2,1,0:T(8,128)S(1)}, f32[10,16,256]{2,1,0:T(8,128)S(1)}, u32[]{:S(2)}, u32[]{:S(2)}) collective-permute-start(f32[10,16,256]{2,1,0:T(8,128)S(1)} %get-tuple-element.30), channel_id=1, source_target_pairs={{0,4},{4,8},{8,12},{12,16},{16,20},{20,24},{24,28},{28,0},{1,5},{5... | collective-permute-start | bytes 491528 | tf_op jit(solution)/shard_map/ppermute | solution.py:559
  4.0 5.7 %collective-permute-start.1 = (f32[10,16,256]{2,1,0:T(8,128)S(1)}, f32[10,16,256]{2,1,0:T(8,128)S(1)}, u32[]{:S(2)}, u32[]{:S(2)}) collective-permute-start(f32[10,16,256]{2,1,0:T(8,128)S(1)} %get-tuple-element.31), channel_id=1, source_target_pairs={{0,28},{4,0},{8,4},{12,8},{16,12},{20,16},{24,20},{28,24},{1,29},{... | collective-permute-start | bytes 491528 | tf_op jit(solution)/shard_map/ppermute | solution.py:559
  10.0 6.4 %collective-permute-start.2 = (f32[27,4,256]{2,1,0:T(4,128)S(1)}, f32[27,4,256]{2,1,0:T(4,128)S(1)}, u32[]{:S(2)}, u32[]{:S(2)}) collective-permute-start(f32[27,4,256]{2,1,0:T(4,128)S(1)} %get-tuple-element.35.up), channel_id=1, source_target_pairs={{0,1},{1,2},{2,3},{3,0},{4,5},{5,6},{6,7},{7,4},{8,9},{9,10},{10,1... | collective-permute-start | bytes 331784 | tf_op jit(solution)/shard_map/ppermute | solution.py:559
  11.3 6.6 %collective-permute-start.3 = (f32[27,4,256]{2,1,0:T(4,128)S(1)}, f32[27,4,256]{2,1,0:T(4,128)S(1)}, u32[]{:S(2)}, u32[]{:S(2)}) collective-permute-start(f32[27,4,256]{2,1,0:T(4,128)S(1)} %get-tuple-element.36.down), channel_id=1, source_target_pairs={{0,3},{1,0},{2,1},{3,2},{4,7},{5,4},{6,5},{7,6},{8,11},{9,8},{10,9... | collective-permute-start | bytes 331784 | tf_op jit(solution)/shard_map/ppermute | solution.py:559
  18.2 3.4 %collective-permute-start.4 = (f32[5,16,256]{2,1,0:T(8,128)S(1)}, f32[5,16,256]{2,1,0:T(8,128)S(1)}, u32[]{:S(2)}, u32[]{:S(2)}) collective-permute-start(f32[5,16,256]{2,1,0:T(8,128)S(1)} %get-tuple-element.46), channel_id=1, source_target_pairs={{0,4},{4,8},{8,12},{12,16},{16,20},{20,24},{24,28},{28,0},{1,5},{5... | collective-permute-start | bytes 245768 | tf_op jit(solution)/shard_map/ppermute | solution.py:559
  19.9 4.8 %collective-permute-start.5 = (f32[5,16,256]{2,1,0:T(8,128)S(1)}, f32[5,16,256]{2,1,0:T(8,128)S(1)}, u32[]{:S(2)}, u32[]{:S(2)}) collective-permute-start(f32[5,16,256]{2,1,0:T(8,128)S(1)} %get-tuple-element.47), channel_id=1, source_target_pairs={{0,28},{4,0},{8,4},{12,8},{16,12},{20,16},{24,20},{28,24},{1,29},{... | collective-permute-start | bytes 245768 | tf_op jit(solution)/shard_map/ppermute | solution.py:559

commit v4 on v3

--- a/solution.py
+++ b/solution.py
@@ -292,9 +292,7 @@
     copies[-1].wait()
 
 
-def rim_kernel(
-    post, adjoint, resistance, solid, flags, from_left, from_right, up, down, work, near, cells
-):
+def rim_kernel(post, adjoint, resistance, solid, flags, up, down, work, near, cells):
     nx, ny, nz = resistance.shape
     shares = {1: [0.0] * 4, -1: [0.0] * 4}
     halves = (slice(0, nx), slice(nx, 2 * nx))
@@ -305,18 +303,15 @@
             tile = work.at[19 * field + i]
             for half, row in enumerate(picks):
                 base = half * nx
+                lines = source[i, :, row, :]
                 if vx == 0:
-                    tile[base : base + nx, :] = source[i, :, row, :]
-                    continue
-                outer = from_left if vx == 1 else from_right
-                edge = outer[x_plane(field, i), pl.ds(row, 1), :]
-                lines = source[i, :, row, :]
-                if vx == 1:
+                    tile[base : base + nx, :] = lines
+                elif vx == 1:
                     tile[base + 1 : base + nx, :] = lines[: nx - 1]
-                    tile[base : base + 1, :] = edge
+                    tile[base : base + 1, :] = jnp.zeros_like(lines[:1])
                 else:
                     tile[base : base + nx - 1, :] = lines[1:]
-                    tile[base + nx - 1 : base + nx, :] = edge
+                    tile[base + nx - 1 : base + nx, :] = jnp.zeros_like(lines[:1])
             if vz:
                 tile[...] = shifted_z(tile[...], vz)
             for half in range(2):
@@ -353,6 +348,64 @@
                 message[WEIGHTS + k, :, lanes] = weights[k][half]
 
 
+EXTRA = tuple(range(SHARE, SHARE + 4)) + tuple(range(AT_REST, AT_REST + 5)) + tuple(range(WEIGHTS, WEIGHTS + 6))
+
+
+def corner(field, vx, vy):
+    return next(i for i in range(19) if velocity(field, i) == (vx, vy, 0))
+
+
+def extra_kernel(resistance, solid, flags, from_left, from_right, up, down, near, cells):
+    nx, ny, nz = resistance.shape
+    near[...] = jnp.zeros(near.shape, jnp.float32)
+    for side, (outer, vx, x) in enumerate(((from_left, 1, 0), (from_right, -1, nx - 1))):
+        for half, (message, way, last, second) in enumerate(((up, 1, ny - 1, ny - 2), (down, -1, 0, 1))):
+            row = 2 * half + side
+            share = [0.0] * 4
+            for field in range(2):
+                for i in moving(1 - 2 * field, 0, vx):
+                    _, vy, vz = velocity(field, i)
+                    if vy == -way:
+                        continue
+                    pick = second if vy == way else last
+                    value = shifted_z(outer[x_plane(field, i), pl.ds(pick, 1), :], vz)
+                    if field == 1:
+                        near[i, row : row + 1, :] = value
+                        continue
+                    for k, factor in enumerate((1, vx, vy, vz)):
+                        if factor:
+                            share[k] = share[k] + factor * value
+                plane = x_plane(field, corner(field, vx, way))
+                message[15 + field, side : side + 1, :] = outer[plane, pl.ds(last, 1), :]
+            for k in range(4):
+                message[k, side : side + 1, :] = share[k]
+            at = (x, slice(last, last + 1), slice(None))
+            cells[0, row : row + 1, :] = greyness(resistance[at], solid[at])
+            cells[1, row : row + 1, :] = shear_rate(flags[at])
+    for part in range(nz // 128):
+        lanes = pl.ds(part * 128, 128)
+        at = (slice(None), lanes)
+        out, weights = halo_terms(
+            [near[(i, *at)] for i in range(19)], cells[(0, *at)], cells[(1, *at)]
+        )
+        for half, (message, way) in enumerate(((up, 1), (down, -1))):
+            rows = slice(2 * half, 2 * half + 2)
+            for k, i in enumerate(moving(-1, 1, way)):
+                message[4 + k, :, lanes] = out[i][rows]
+            for k in range(6):
+                message[9 + k, :, lanes] = weights[k][rows]
+
+
+def add_extra(total, message, extra, way, planes):
+    nx = total.shape[1]
+    total[...] = message[...]
+    for side, (vx, x) in enumerate(((1, 0), (-1, nx - 1))):
+        places = EXTRA + tuple(edge_plane(f, way, corner(f, vx, way)) for f in range(2))
+        for k in planes:
+            to = (places[k], slice(x, x + 1), slice(None))
+            total[to] = total[to] + extra[k, side : side + 1, :]
+
+
 def middle_kernel(
     post, adjoint, resistance, solid, flags, from_left, from_right,
     out, sensitivity, rim_middle, rim_cotangent, middle, cotangent,
@@ -407,9 +460,14 @@
 
 
 def edge_kernel(
-    out, resistance, solid, flags, rim_middle, rim_cotangent, up, down, below, above,
-    outer_rows, halo_rows, outer_sens, right, left, middle, cotangent, cells,
+    out, resistance, solid, flags, rim_middle, rim_cotangent, *refs
 ):
+    messages, extras, refs = refs[:4], refs[4:8], refs[8:]
+    outer_rows, halo_rows, outer_sens, right, left, middle, cotangent, cells, *totals = refs
+    for k, way in enumerate((1, -1, 1, -1)):
+        planes = (15, 16) if k < 2 else range(17)
+        add_extra(totals[k], messages[k], extras[k], way, planes)
+    up, down, below, above = totals
     nx, ny, nz = resistance.shape
     low, high = slice(0, nx), slice(nx, 2 * nx)
     for field, rim, target in ((0, rim_middle, middle), (1, rim_cotangent, cotangent)):
@@ -573,19 +631,24 @@
         post_kernel, [whole] + [jax.ShapeDtypeStruct(v.shape, v.dtype) for v in far],
         *far, far=range(5), scratch=[pltpu.SemaphoreType.DMA((nx + 4,))],
     )
-    up, down = call(
-        rim_kernel, [(PLANES, nx, nz)] * 2, post, adjoint_end, *cells, *sides,
+    rims_out = call(
+        rim_kernel, [(PLANES, nx, nz)] * 2, post, adjoint_end, *cells,
         scratch=[(38, *rim[1:]), rim, (2, *rim[1:])],
     )
-    below, above = exchange("gy", up, down)
+    rims_in = exchange("gy", *rims_out)
+    extra_out = call(
+        extra_kernel, [(17, 2, nz)] * 2, *cells, *sides,
+        scratch=[(19, 4, nz), (2, 4, nz)],
+    )
+    extra_in = exchange("gy", *extra_out)
     out, sens, *rims = call(
         middle_kernel, [whole, voxels, rim, rim], post, adjoint_end, *cells, *sides,
         scratch=[whole, whole],
     )
     outer_rows, halo_rows, outer_sens, right, left = call(
         edge_kernel, [rim, rim, rim[1:], (5, ny, nz), (5, ny, nz)],
-        out, *cells, *rims, up, down, below, above,
-        scratch=[rim, rim, (3, *rim[1:])],
+        out, *cells, *rims, *rims_out, *rims_in, *extra_out, *extra_in,
+        scratch=[rim, rim, (3, *rim[1:])] + [(PLANES, nx, nz)] * 4,
     )
     sides = exchange("gx", right, left)
     *done, pulled, partial = call(

time: 26.2 us -> 25.5 us (0.973)
  waiting for transfers between devices: 9.84 us -> 3.63 us
  starting transfers between devices: 6.99 us -> 12.1 us
    ppermute x3 -> x4, waiting for transfers between devices: 7.1 us -> 3.1 us  [exchange(): lax.ppermute(backward, axis, behind)]
    ppermute x3 -> x4, starting transfers between devices: 4.9 us -> 7.86 us  [exchange(): lax.ppermute(onward, axis, ahead)]
    ppermute x3 -> x4, waiting for transfers between devices: 2.74 us -> 0.54 us  [exchange(): lax.ppermute(onward, axis, ahead)]
    ppermute x3 -> x4, starting transfers between devices: 2.1 us -> 4.19 us  [exchange(): lax.ppermute(backward, axis, behind)]
    pallas_call x7 -> x8, Pallas kernels: 8.5 us -> 8.72 us  [call(): pl.pallas_call(kernel, out_shape=made, in_specs=[HBM if k in far else VME...]
  transfers between devices with their start and end apart: 6 -> 8, of which waited for: 6 -> 5; matrix products, arithmetic and copies ran while one was open for 0% -> 0% of each run, Pallas kernels for 20% -> 22%
where the time goes in v4:
time: 25.5 us; the launch traced here: 25.1 us
  starting transfers between devices  12.1 us (47%)
  Pallas kernels  8.72 us (34%)
  waiting for transfers between devices  3.63 us (14%)
  between operations  0.7 us (3%)
    pallas_call x8, Pallas kernels, call(): pl.pallas_call(kernel, out_shape=made, in_specs=[HBM if k in far else VME...  8.72 us
    ppermute x4, starting transfers between devices, exchange(): lax.ppermute(onward, axis, ahead)  7.86 us
    ppermute x4, starting transfers between devices, exchange(): lax.ppermute(backward, axis, behind)  4.19 us
    ppermute x4, waiting for transfers between devices, exchange(): lax.ppermute(backward, axis, behind)  3.1 us
    ppermute x4, waiting for transfers between devices, exchange(): lax.ppermute(onward, axis, ahead)  0.54 us
  transfers between devices with their start and end apart: 8, of which 5 were waited for; matrix products, arithmetic and copies ran while one was open for 0% of the time, Pallas kernels for 22%

profile of v4, /device:TPU:3, one launch (start us, length us, event | category | flops | bytes accessed | tf_op | source)
XLA Modules:
  0.0 25.1 jit_solution(975961804090966835)
XLA Ops:
  0.6 1.5 %shard_map.69 = (f32[10,16,256]{2,1,0:T(8,128)S(1)}, f32[10,16,256]{2,1,0:T(8,128)S(1)}) custom-call(f32[19,4,16,256]{3,2,1,0:T(8,128)} %far_state.3, f32[19,4,16,256]{3,2,1,0:T(8,128)} %far_adjoint.3, f32[4,16,256]{2,1,0:T(8,128)} %far_resistance.3, s32[4,16,256]{2,1,0:T(8,128)} %far_solid.3, s32[4,16,256]{2,1,0:T(8,128)} %far_flags.3), custom_call_target="tpu_custom_call" | custom-call | tf_op jit(solution)/shard_map/pallas_call | solution.py:598
  2.1 1.8 %collective-permute-start = (f32[10,16,256]{2,1,0:T(8,128)S(1)}, f32[10,16,256]{2,1,0:T(8,128)S(1)}, u32[]{:S(2)}, u32[]{:S(2)}) collective-permute-start(f32[10,16,256]{2,1,0:T(8,128)S(1)} %get-tuple-element.32), channel_id=1, source_target_pairs={{0,4},{4,8},{8,12},{12,16},{16,20},{20,24},{24,28},{28,0},{1,5},{5... | collective-permute-start | bytes 491528 | tf_op jit(solution)/shard_map/ppermute | solution.py:617
  4.0 0.0 collective-permute-start.1
  4.0 1.9 %shard_map.68 = (f32[19,4,16,256]{3,2,1,0:T(8,128)S(1)}, f32[19,4,16,256]{3,2,1,0:T(8,128)S(1)}, f32[19,4,16,256]{3,2,1,0:T(8,128)S(1)}, f32[4,16,256]{2,1,0:T(8...) custom-call(f32[19,4,16,256]{3,2,1,0:T(8,128)} %far_state.3, f32[19,4,16,256]{3,2,1,0:T(8,128)} %far_adjoint.3, ...), custom_call_target="tpu_custom_call" | custom-call | tf_op jit(solution)/shard_map/pallas_call | solution.py:598
  5.8 0.3 %shard_map.71 = (f32[27,4,256]{2,1,0:T(4,128)S(1)}, f32[27,4,256]{2,1,0:T(4,128)S(1)}) custom-call(f32[19,4,16,256]{3,2,1,0:T(8,128)S(1)} %get-tuple-element.27.post, f32[19,4,16,256]{3,2,1,0:T(8,128)S(1)} %get-tuple-element.28.adjoint, f32[4,16,256]{2,1,0:T(8,128)S(1)} %get-tuple-element.29.resistance, s32[4,16,256]{2,1,0:T(8,128)S(1)} %get-tuple-element.30.solid, ...), custom_call_target="tpu_custom_call" | custom-call | tf_op jit(solution)/shard_map/pallas_call | solution.py:598
  6.1 1.3 %collective-permute-start.2 = (f32[27,4,256]{2,1,0:T(4,128)S(1)}, f32[27,4,256]{2,1,0:T(4,128)S(1)}, u32[]{:S(2)}, u32[]{:S(2)}) collective-permute-start(f32[27,4,256]{2,1,0:T(4,128)S(1)} %get-tuple-element.37.refs_0_), channel_id=1, source_target_pairs={{0,1},{1,2},{2,3},{3,0},{4,5},{5,6},{6,7},{7,4},{8,9},{9,10},{10,1... | collective-permute-start | bytes 331784 | tf_op jit(solution)/shard_map/ppermute | solution.py:617
  7.5 2.1 %collective-permute-start.3 = (f32[27,4,256]{2,1,0:T(4,128)S(1)}, f32[27,4,256]{2,1,0:T(4,128)S(1)}, u32[]{:S(2)}, u32[]{:S(2)}) collective-permute-start(f32[27,4,256]{2,1,0:T(4,128)S(1)} %get-tuple-element.38.refs_1_), channel_id=1, source_target_pairs={{0,3},{1,0},{2,1},{3,2},{4,7},{5,4},{6,5},{7,6},{8,11},{9,8},{10,9... | collective-permute-start | bytes 331784 | tf_op jit(solution)/shard_map/ppermute | solution.py:617
  9.6 0.0 collective-permute-done.from_left
  9.6 0.1 collective-permute-done.1.from_right
  9.6 0.2 shard_map.72
  9.8 1.3 %collective-permute-start.4 = (f32[17,2,256]{2,1,0:T(2,128)S(1)}, f32[17,2,256]{2,1,0:T(2,128)S(1)}, u32[]{:S(2)}, u32[]{:S(2)}) collective-permute-start(f32[17,2,256]{2,1,0:T(2,128)S(1)} %get-tuple-element.39.refs_4_), channel_id=1, source_target_pairs={{0,1},{1,2},{2,3},{3,0},{4,5},{5,6},{6,7},{7,4},{8,9},{9,10},{10,1... | collective-permute-start | bytes 104456 | tf_op jit(solution)/shard_map/ppermute | solution.py:617
  11.1 2.1 %collective-permute-start.5 = (f32[17,2,256]{2,1,0:T(2,128)S(1)}, f32[17,2,256]{2,1,0:T(2,128)S(1)}, u32[]{:S(2)}, u32[]{:S(2)}) collective-permute-start(f32[17,2,256]{2,1,0:T(2,128)S(1)} %get-tuple-element.40.refs_5_), channel_id=1, source_target_pairs={{0,3},{1,0},{2,1},{3,2},{4,7},{5,4},{6,5},{7,6},{8,11},{9,8},{10,9... | collective-permute-start | bytes 104456 | tf_op jit(solution)/shard_map/ppermute | solution.py:617
  13.2 1.6 %shard_map.70 = (f32[19,4,16,256]{3,2,1,0:T(8,128)S(1)}, f32[4,16,256]{2,1,0:T(8,128)S(1)}, f32[19,8,256]{2,1,0:T(8,128)S(1)}, f32[19,8,256]{2,1,0:T(8,128)S(1)}) custom-call(f32[19,4,16,256]{3,2,1,0:T(8,128)S(1)} %get-tuple-element.27.post, f32[19,4,16,256]{3,2,1,0:T(8,128)S(1)} %get-tuple-element.28.adjoint, ...), custom_call_target="tpu_custom_call" | custom-call | tf_op jit(solution)/shard_map/pallas_call | solution.py:598
  14.9 0.0 collective-permute-done.2.refs_2_
  14.9 0.0 collective-permute-done.3.refs_3_
  14.9 0.2 collective-permute-done.4.refs_6_
  15.1 0.3 %collective-permute-done.5.refs_7_ = f32[17,2,256]{2,1,0:T(2,128)S(1)} collective-permute-done((f32[17,2,256]{2,1,0:T(2,128)S(1)}, f32[17,2,256]{2,1,0:T(2,128)S(1)}, u32[]{:S(2)}, u32[]{:S(2)}) %collective-permute-start.5) | collective-permute-done | bytes 34848 | tf_op jit(solution)/shard_map/ppermute | solution.py:617
  15.3 0.3 %shard_map.73 = (f32[19,8,256]{2,1,0:T(8,128)S(1)}, f32[19,8,256]{2,1,0:T(8,128)S(1)}, f32[8,256]{1,0:T(8,128)S(1)}, f32[5,16,256]{2,1,0:T(8,128)S(1)}, f32[5,16,256]{2,1,0:T(8,128)S(1)}) custom-call(f32[19,4,16,256]{3,2,1,0:T(8,128)S(1)} %get-tuple-element.34.out, f32[4,16,256]{2,1,0:T(8,128)S(1)} %get-tuple-element.29.resistance, ...), custom_call_target="tpu_custom_call" | custom-call | tf_op jit(solution)/shard_map/pallas_call | solution.py:598
  15.7 3.3 %collective-permute-start.6 = (f32[5,16,256]{2,1,0:T(8,128)S(1)}, f32[5,16,256]{2,1,0:T(8,128)S(1)}, u32[]{:S(2)}, u32[]{:S(2)}) collective-permute-start(f32[5,16,256]{2,1,0:T(8,128)S(1)} %get-tuple-element.50), channel_id=1, source_target_pairs={{0,4},{4,8},{8,12},{12,16},{16,20},{20,24},{24,28},{28,0},{1,5},{5... | collective-permute-start | bytes 245768 | tf_op jit(solution)/shard_map/ppermute | solution.py:617
  19.0 0.0 collective-permute-start.7
  19.0 1.6 %shard_map.74 = (f32[19,4,16,256]{3,2,1,0:T(8,128)}, f32[4,16,256]{2,1,0:T(8,128)}, f32[19,4,16,256]{3,2,1,0:T(8,128)S(1)}, f32[4,16,256]{2,1,0:T(8,128)S(1)}) custom-call(f32[19,4,16,256]{3,2,1,0:T(8,128)S(1)} %get-tuple-element.34.out, f32[19,8,256]{2,1,0:T(8,128)S(1)} %get-tuple-element.41.outer_rows, f32[19,8,256]{2,1,0:T(8,128)S(1)} %get-tuple-element.42.halo_rows, ...), custom_call_target="tpu_custom_call" | custom-call | tf_op jit(solution)/shard_map/pallas_call | solution.py:598
  20.6 0.4 %collective-permute-done.6.from_left = f32[5,16,256]{2,1,0:T(8,128)S(1)} collective-permute-done((f32[5,16,256]{2,1,0:T(8,128)S(1)}, f32[5,16,256]{2,1,0:T(8,128)S(1)}, u32[]{:S(2)}, u32[]{:S(2)}) %collective-permute-start.6) | collective-permute-done | bytes 81952 | tf_op jit(solution)/shard_map/ppermute | solution.py:617
  21.0 2.8 %collective-permute-done.7.from_right = f32[5,16,256]{2,1,0:T(8,128)S(1)} collective-permute-done((f32[5,16,256]{2,1,0:T(8,128)S(1)}, f32[5,16,256]{2,1,0:T(8,128)S(1)}, u32[]{:S(2)}, u32[]{:S(2)}) %collective-permute-start.7) | collective-permute-done | bytes 81952 | tf_op jit(solution)/shard_map/ppermute | solution.py:617
  23.8 1.3 %shard_map.75 = (f32[19,4,16,256]{3,2,1,0:T(8,128)}, f32[4,16,256]{2,1,0:T(8,128)}) custom-call(f32[19,4,16,256]{3,2,1,0:T(8,128)} %get-tuple-element.46.inner_start, f32[4,16,256]{2,1,0:T(8,128)} %get-tuple-element.47.inner_total, f32[19,4,16,256]{3,2,1,0:T(8,128)S(1)} %get-tuple-element.45.state, ...), custom_call_target="tpu_custom_call", output_to_operand_aliasing={{0}: (0, {}), {1}: (1, {})} | custom-call | tf_op jit(solution)/shard_map/pallas_call | solution.py:598
Async XLA Ops:
  2.1 7.4 %collective-permute-start = (f32[10,16,256]{2,1,0:T(8,128)S(1)}, f32[10,16,256]{2,1,0:T(8,128)S(1)}, u32[]{:S(2)}, u32[]{:S(2)}) collective-permute-start(f32[10,16,256]{2,1,0:T(8,128)S(1)} %get-tuple-element.32), channel_id=1, source_target_pairs={{0,4},{4,8},{8,12},{12,16},{16,20},{20,24},{24,28},{28,0},{1,5},{5... | collective-permute-start | bytes 491528 | tf_op jit(solution)/shard_map/ppermute | solution.py:617
  4.0 5.7 %collective-permute-start.1 = (f32[10,16,256]{2,1,0:T(8,128)S(1)}, f32[10,16,256]{2,1,0:T(8,128)S(1)}, u32[]{:S(2)}, u32[]{:S(2)}) collective-permute-start(f32[10,16,256]{2,1,0:T(8,128)S(1)} %get-tuple-element.33), channel_id=1, source_target_pairs={{0,28},{4,0},{8,4},{12,8},{16,12},{20,16},{24,20},{28,24},{1,29},{... | collective-permute-start | bytes 491528 | tf_op jit(solution)/shard_map/ppermute | solution.py:617
  6.1 8.7 %collective-permute-start.2 = (f32[27,4,256]{2,1,0:T(4,128)S(1)}, f32[27,4,256]{2,1,0:T(4,128)S(1)}, u32[]{:S(2)}, u32[]{:S(2)}) collective-permute-start(f32[27,4,256]{2,1,0:T(4,128)S(1)} %get-tuple-element.37.refs_0_), channel_id=1, source_target_pairs={{0,1},{1,2},{2,3},{3,0},{4,5},{5,6},{6,7},{7,4},{8,9},{9,10},{10,1... | collective-permute-start | bytes 331784 | tf_op jit(solution)/shard_map/ppermute | solution.py:617
  7.5 7.4 %collective-permute-start.3 = (f32[27,4,256]{2,1,0:T(4,128)S(1)}, f32[27,4,256]{2,1,0:T(4,128)S(1)}, u32[]{:S(2)}, u32[]{:S(2)}) collective-permute-start(f32[27,4,256]{2,1,0:T(4,128)S(1)} %get-tuple-element.38.refs_1_), channel_id=1, source_target_pairs={{0,3},{1,0},{2,1},{3,2},{4,7},{5,4},{6,5},{7,6},{8,11},{9,8},{10,9... | collective-permute-start | bytes 331784 | tf_op jit(solution)/shard_map/ppermute | solution.py:617
  9.8 5.3 %collective-permute-start.4 = (f32[17,2,256]{2,1,0:T(2,128)S(1)}, f32[17,2,256]{2,1,0:T(2,128)S(1)}, u32[]{:S(2)}, u32[]{:S(2)}) collective-permute-start(f32[17,2,256]{2,1,0:T(2,128)S(1)} %get-tuple-element.39.refs_4_), channel_id=1, source_target_pairs={{0,1},{1,2},{2,3},{3,0},{4,5},{5,6},{6,7},{7,4},{8,9},{9,10},{10,1... | collective-permute-start | bytes 104456 | tf_op jit(solution)/shard_map/ppermute | solution.py:617
  11.1 4.2 %collective-permute-start.5 = (f32[17,2,256]{2,1,0:T(2,128)S(1)}, f32[17,2,256]{2,1,0:T(2,128)S(1)}, u32[]{:S(2)}, u32[]{:S(2)}) collective-permute-start(f32[17,2,256]{2,1,0:T(2,128)S(1)} %get-tuple-element.40.refs_5_), channel_id=1, source_target_pairs={{0,3},{1,0},{2,1},{3,2},{4,7},{5,4},{6,5},{7,6},{8,11},{9,8},{10,9... | collective-permute-start | bytes 104456 | tf_op jit(solution)/shard_map/ppermute | solution.py:617
  15.7 5.3 %collective-permute-start.6 = (f32[5,16,256]{2,1,0:T(8,128)S(1)}, f32[5,16,256]{2,1,0:T(8,128)S(1)}, u32[]{:S(2)}, u32[]{:S(2)}) collective-permute-start(f32[5,16,256]{2,1,0:T(8,128)S(1)} %get-tuple-element.50), channel_id=1, source_target_pairs={{0,4},{4,8},{8,12},{12,16},{16,20},{20,24},{24,28},{28,0},{1,5},{5... | collective-permute-start | bytes 245768 | tf_op jit(solution)/shard_map/ppermute | solution.py:617
  19.0 4.8 %collective-permute-start.7 = (f32[5,16,256]{2,1,0:T(8,128)S(1)}, f32[5,16,256]{2,1,0:T(8,128)S(1)}, u32[]{:S(2)}, u32[]{:S(2)}) collective-permute-start(f32[5,16,256]{2,1,0:T(8,128)S(1)} %get-tuple-element.51), channel_id=1, source_target_pairs={{0,28},{4,0},{8,4},{12,8},{16,12},{20,16},{24,20},{28,24},{1,29},{... | collective-permute-start | bytes 245768 | tf_op jit(solution)/shard_map/ppermute | solution.py:617

commit v5 on v3

--- a/solution.py
+++ b/solution.py
@@ -260,41 +260,28 @@
             copy.wait()
 
 
-def post_kernel(
-    far_state, far_adjoint, far_resistance, far_solid, far_flags,
-    post, state, adjoint, resistance, solid, flags, done,
-):
+def post_kernel(state, adjoint, resistance, solid, flags, post):
+    del adjoint
     nx, ny, nz = resistance.shape
-    pairs = [(far_resistance, resistance), (far_solid, solid), (far_flags, flags)]
-    pairs += [(far_state.at[:, x], state.at[:, x]) for x in range(nx)] + [(far_adjoint, adjoint)]
-    copies = [pltpu.make_async_copy(*pair, done.at[k]) for k, pair in enumerate(pairs)]
-    for copy in copies:
-        copy.start()
-    for copy in copies[:3]:
-        copy.wait()
-    for x in range(nx):
-        copies[3 + x].wait()
-
-        def step(t, carry, x=x):
-            rows = pl.ds(pl.multiple_of(t * 8, 8), 8)
-            for half in range(nz // 128):
-                at = (x, rows, pl.ds(half * 128, 128))
-                out = collide_tile(
-                    [state[(i, *at)] for i in range(19)],
-                    greyness(resistance[at], solid[at]),
-                    shear_rate(flags[at]),
-                )
-                for i in range(19):
-                    post[(i, *at)] = out[i]
-            return carry
-
-        lax.fori_loop(0, ny // 8, step, 0)
-    copies[-1].wait()
-
-
-def rim_kernel(
-    post, adjoint, resistance, solid, flags, from_left, from_right, up, down, work, near, cells
-):
+    tiles = ny // 8
+
+    def step(n, carry):
+        x, rows = n // tiles, pl.ds(pl.multiple_of(n % tiles * 8, 8), 8)
+        for half in range(nz // 128):
+            at = (x, rows, pl.ds(half * 128, 128))
+            out = collide_tile(
+                [state[(i, *at)] for i in range(19)],
+                greyness(resistance[at], solid[at]),
+                shear_rate(flags[at]),
+            )
+            for i in range(19):
+                post[(i, *at)] = out[i]
+        return carry
+
+    lax.fori_loop(0, nx * tiles, step, 0)
+
+
+def rim_kernel(post, adjoint, resistance, solid, flags, up, down, work, near, cells):
     nx, ny, nz = resistance.shape
     shares = {1: [0.0] * 4, -1: [0.0] * 4}
     halves = (slice(0, nx), slice(nx, 2 * nx))
@@ -305,18 +292,15 @@
             tile = work.at[19 * field + i]
             for half, row in enumerate(picks):
                 base = half * nx
+                lines = source[i, :, row, :]
                 if vx == 0:
-                    tile[base : base + nx, :] = source[i, :, row, :]
-                    continue
-                outer = from_left if vx == 1 else from_right
-                edge = outer[x_plane(field, i), pl.ds(row, 1), :]
-                lines = source[i, :, row, :]
-                if vx == 1:
+                    tile[base : base + nx, :] = lines
+                elif vx == 1:
                     tile[base + 1 : base + nx, :] = lines[: nx - 1]
-                    tile[base : base + 1, :] = edge
+                    tile[base : base + 1, :] = jnp.zeros_like(lines[:1])
                 else:
                     tile[base : base + nx - 1, :] = lines[1:]
-                    tile[base + nx - 1 : base + nx, :] = edge
+                    tile[base + nx - 1 : base + nx, :] = jnp.zeros_like(lines[:1])
             if vz:
                 tile[...] = shifted_z(tile[...], vz)
             for half in range(2):
@@ -353,6 +337,51 @@
                 message[WEIGHTS + k, :, lanes] = weights[k][half]
 
 
+def beside(field, vx, way):
+    return [i for i in moving(1 - 2 * field, 0, vx) if velocity(field, i)[1] in (0, way)]
+
+
+def corner(field, vx, vy):
+    return next(i for i in range(19) if velocity(field, i) == (vx, vy, 0))
+
+
+def corner_kernel(from_left, from_right, up, down):
+    ny = from_left.shape[1]
+    for side, (outer, vx) in enumerate(((from_left, 1), (from_right, -1))):
+        for message, way, last, second in ((up, 1, ny - 1, ny - 2), (down, -1, 0, 1)):
+            for field in range(2):
+                for k, i in enumerate(beside(field, vx, way)):
+                    _, vy, vz = velocity(field, i)
+                    line = outer[x_plane(field, i), pl.ds(second if vy else last, 1), :]
+                    message[4 * field + k, side : side + 1, :] = shifted_z(line, vz)
+                plane = x_plane(field, corner(field, vx, way))
+                message[8 + field, side : side + 1, :] = outer[plane, pl.ds(last, 1), :]
+
+
+def add_corners(total, message, extra, way, halo):
+    nx = total.shape[1]
+    total[...] = message[...]
+    if halo is not None:
+        for i in moving(-1, 0, 1) + moving(-1, 0, -1):
+            halo[i] = jnp.zeros(halo.shape[1:], jnp.float32)
+    for side, (vx, x) in enumerate(((1, 0), (-1, nx - 1))):
+        at, own = slice(x, x + 1), slice(side, side + 1)
+        for field in range(2):
+            plane = edge_plane(field, way, corner(field, vx, way))
+            total[plane, at, :] = total[plane, at, :] + extra[8 + field, own, :]
+        if halo is None:
+            continue
+        share = [total[SHARE + k, at, :] for k in range(4)]
+        for k, i in enumerate(beside(0, vx, way)):
+            for m, factor in enumerate((1, *velocity(0, i))):
+                if factor:
+                    share[m] = share[m] + factor * extra[k, own, :]
+        for k in range(4):
+            total[SHARE + k, at, :] = share[k]
+        for k, i in enumerate(beside(1, vx, way)):
+            halo[i, at, :] = extra[4 + k, own, :]
+
+
 def middle_kernel(
     post, adjoint, resistance, solid, flags, from_left, from_right,
     out, sensitivity, rim_middle, rim_cotangent, middle, cotangent,
@@ -407,9 +436,14 @@
 
 
 def edge_kernel(
-    out, resistance, solid, flags, rim_middle, rim_cotangent, up, down, below, above,
-    outer_rows, halo_rows, outer_sens, right, left, middle, cotangent, cells,
+    out, resistance, solid, flags, rim_middle, rim_cotangent, *refs
 ):
+    messages, extras, refs = refs[:4], refs[4:8], refs[8:]
+    outer_rows, halo_rows, outer_sens, right, left, middle, cotangent, cells, *totals = refs
+    totals, halos = totals[:4], totals[4:]
+    for k, way in enumerate((1, -1, 1, -1)):
+        add_corners(totals[k], messages[k], extras[k], way, halos[k - 2] if k > 1 else None)
+    up, down, below, above = totals
     nx, ny, nz = resistance.shape
     low, high = slice(0, nx), slice(nx, 2 * nx)
     for field, rim, target in ((0, rim_middle, middle), (1, rim_cotangent, cotangent)):
@@ -429,6 +463,9 @@
                     share[k] = share[k] + factor * value
         u = [v / share[0] for v in share[1:]]
         lam = [jnp.zeros_like(share[0])] * 19
+        for vx in (1, -1):
+            for i in beside(1, vx, way):
+                lam[i] = halos[0 if way == 1 else 1][i]
         for i in moving(-1, 1, -way):
             lam[i] = sent[edge_plane(1, -way, i)]
         own, weights = halo_terms(lam, received[GREY], received[RATE])
@@ -569,23 +606,25 @@
         scratch=[(2, 19, ny, nz), (2, ny, nz), *pair, pltpu.SemaphoreType.DMA((18,))],
     )
     sides = exchange("gx", right, left)
-    post, checkpoint, adjoint_end, *cells = call(
-        post_kernel, [whole] + [jax.ShapeDtypeStruct(v.shape, v.dtype) for v in far],
-        *far, far=range(5), scratch=[pltpu.SemaphoreType.DMA((nx + 4,))],
-    )
-    up, down = call(
-        rim_kernel, [(PLANES, nx, nz)] * 2, post, adjoint_end, *cells, *sides,
+    cells = (resistance, solid_mask, flags)
+    (post,) = call(post_kernel, [whole], checkpoint, adjoint_end, *cells)
+    rims_out = call(
+        rim_kernel, [(PLANES, nx, nz)] * 2, post, adjoint_end, *cells,
         scratch=[(38, *rim[1:]), rim, (2, *rim[1:])],
     )
-    below, above = exchange("gy", up, down)
+    rims_in = exchange("gy", *rims_out)
+    corner_out = call(
+        corner_kernel, [(10, 2, nz)] * 2, *sides
+    )
+    corner_in = exchange("gy", *corner_out)
     out, sens, *rims = call(
         middle_kernel, [whole, voxels, rim, rim], post, adjoint_end, *cells, *sides,
         scratch=[whole, whole],
     )
     outer_rows, halo_rows, outer_sens, right, left = call(
         edge_kernel, [rim, rim, rim[1:], (5, ny, nz), (5, ny, nz)],
-        out, *cells, *rims, up, down, below, above,
-        scratch=[rim, rim, (3, *rim[1:])],
+        out, *cells, *rims, *rims_out, *rims_in, *corner_out, *corner_in,
+        scratch=[rim, rim, (3, *rim[1:])] + [(PLANES, nx, nz)] * 4 + [(19, nx, nz)] * 2,
     )
     sides = exchange("gx", right, left)
     *done, pulled, partial = call(

time: 26.2 us -> 24.3 us (0.927)
  waiting for transfers between devices: 9.84 us -> 4.25 us
  starting transfers between devices: 6.99 us -> 11.2 us
  Pallas kernels: 8.5 us -> 7.66 us
    ppermute x3 -> x4, waiting for transfers between devices: 7.1 us -> 3.62 us  [exchange(): lax.ppermute(backward, axis, behind)]
    ppermute x3 -> x4, starting transfers between devices: 4.9 us -> 7.05 us  [exchange(): lax.ppermute(onward, axis, ahead)]
    ppermute x3 -> x4, waiting for transfers between devices: 2.74 us -> 0.64 us  [exchange(): lax.ppermute(onward, axis, ahead)]
    ppermute x3 -> x4, starting transfers between devices: 2.1 us -> 4.19 us  [exchange(): lax.ppermute(backward, axis, behind)]
    pallas_call x7 -> x8, Pallas kernels: 8.5 us -> 7.66 us  [call(): pl.pallas_call(kernel, out_shape=made, in_specs=[HBM if k in far else VME...]
  transfers between devices with their start and end apart: 6 -> 8, of which waited for: 6 -> 3; matrix products, arithmetic and copies ran while one was open for 0% -> 0% of each run, Pallas kernels for 20% -> 18%
where the time goes in v5:
time: 24.3 us; the launch traced here: 23.9 us
  starting transfers between devices  11.2 us (46%)
  Pallas kernels  7.66 us (32%)
  waiting for transfers between devices  4.25 us (17%)
  between operations  0.78 us (3%)
    pallas_call x8, Pallas kernels, call(): pl.pallas_call(kernel, out_shape=made, in_specs=[HBM if k in far else VME...  7.66 us
    ppermute x4, starting transfers between devices, exchange(): lax.ppermute(onward, axis, ahead)  7.05 us
    ppermute x4, starting transfers between devices, exchange(): lax.ppermute(backward, axis, behind)  4.19 us
    ppermute x4, waiting for transfers between devices, exchange(): lax.ppermute(backward, axis, behind)  3.62 us
    ppermute x4, waiting for transfers between devices, exchange(): lax.ppermute(onward, axis, ahead)  0.64 us
  transfers between devices with their start and end apart: 8, of which 3 were waited for; matrix products, arithmetic and copies ran while one was open for 0% of the time, Pallas kernels for 18%

profile of v5, /device:TPU:3, one launch (start us, length us, event | category | flops | bytes accessed | tf_op | source)
XLA Modules:
  0.0 23.9 jit_solution(6286679875207151066)
XLA Ops:
  0.6 0.0 copy-start.4
  0.6 0.0 copy-start.3
  0.7 0.0 copy-start.2
  0.7 0.0 copy-start
  0.7 0.0 copy-start.1
  0.7 1.6 %shard_map.69 = (f32[10,16,256]{2,1,0:T(8,128)S(1)}, f32[10,16,256]{2,1,0:T(8,128)S(1)}) custom-call(f32[19,4,16,256]{3,2,1,0:T(8,128)} %state.5, f32[19,4,16,256]{3,2,1,0:T(8,128)} %adjoint.5, f32[4,16,256]{2,1,0:T(8,128)} %resistance.11, s32[4,16,256]{2,1,0:T(8,128)} %solid.11, s32[4,16,256]{2,1,0:T(8,128)} %flags.11), custom_call_target="tpu_custom_call" | custom-call | tf_op jit(solution)/shard_map/pallas_call | solution.py:577
  2.3 1.8 %collective-permute-start = (f32[10,16,256]{2,1,0:T(8,128)S(1)}, f32[10,16,256]{2,1,0:T(8,128)S(1)}, u32[]{:S(2)}, u32[]{:S(2)}) collective-permute-start(f32[10,16,256]{2,1,0:T(8,128)S(1)} %get-tuple-element.21), channel_id=1, source_target_pairs={{0,4},{4,8},{8,12},{12,16},{16,20},{20,24},{24,28},{28,0},{1,5},{5... | collective-permute-start | bytes 491528 | tf_op jit(solution)/shard_map/ppermute | solution.py:596
  4.1 0.0 collective-permute-start.1
  4.1 0.0 copy-done.4
  4.1 0.0 copy-done.3
  4.1 0.0 copy-done.2
  4.1 0.0 copy-done
  4.1 0.0 copy-done.1
  4.2 0.8 %shard_map.68.post = f32[19,4,16,256]{3,2,1,0:T(8,128)S(1)} custom-call(f32[19,4,16,256]{3,2,1,0:T(8,128)S(1)} %copy-done.1, f32[19,4,16,256]{3,2,1,0:T(8,128)S(1)} %copy-done, f32[4,16,256]{2,1,0:T(8,128)S(1)} %copy-done.2, s32[4,16,256]{2,1,0:T(8,128)S(1)} %copy-done.3, s32[4,16,256]{2,1,0:T(8,128)S(1)} %copy-done.4), custom_call_target="tpu_custom_call" | custom-call | tf_op jit(solution)/shard_map/pallas_call | solution.py:577
  4.9 0.3 %shard_map.71 = (f32[27,4,256]{2,1,0:T(4,128)S(1)}, f32[27,4,256]{2,1,0:T(4,128)S(1)}) custom-call(f32[19,4,16,256]{3,2,1,0:T(8,128)S(1)} %shard_map.68.post, f32[19,4,16,256]{3,2,1,0:T(8,128)S(1)} %copy-done, f32[4,16,256]{2,1,0:T(8,128)S(1)} %copy-done.2, s32[4,16,256]{2,1,0:T(8,128)S(1)} %copy-done.3, s32[4,16,256]{2,1,0:T(8,128)S(1)} %copy-done.4), custom_call_target="tpu_custom_call" | custom-call | tf_op jit(solution)/shard_map/pallas_call | solution.py:577
  5.2 1.3 %collective-permute-start.2 = (f32[27,4,256]{2,1,0:T(4,128)S(1)}, f32[27,4,256]{2,1,0:T(4,128)S(1)}, u32[]{:S(2)}, u32[]{:S(2)}) collective-permute-start(f32[27,4,256]{2,1,0:T(4,128)S(1)} %get-tuple-element.26.refs_0_), channel_id=1, source_target_pairs={{0,1},{1,2},{2,3},{3,0},{4,5},{5,6},{6,7},{7,4},{8,9},{9,10},{10,1... | collective-permute-start | bytes 331784 | tf_op jit(solution)/shard_map/ppermute | solution.py:596
  6.6 2.1 %collective-permute-start.3 = (f32[27,4,256]{2,1,0:T(4,128)S(1)}, f32[27,4,256]{2,1,0:T(4,128)S(1)}, u32[]{:S(2)}, u32[]{:S(2)}) collective-permute-start(f32[27,4,256]{2,1,0:T(4,128)S(1)} %get-tuple-element.27.refs_1_), channel_id=1, source_target_pairs={{0,3},{1,0},{2,1},{3,2},{4,7},{5,4},{6,5},{7,6},{8,11},{9,8},{10,9... | collective-permute-start | bytes 331784 | tf_op jit(solution)/shard_map/ppermute | solution.py:596
  8.7 0.0 collective-permute-done.from_left
  8.7 1.1 %collective-permute-done.1.from_right = f32[10,16,256]{2,1,0:T(8,128)S(1)} collective-permute-done((f32[10,16,256]{2,1,0:T(8,128)S(1)}, f32[10,16,256]{2,1,0:T(8,128)S(1)}, u32[]{:S(2)}, u32[]{:S(2)}) %collective-permute-start.1) | collective-permute-done | bytes 163872 | tf_op jit(solution)/shard_map/ppermute | solution.py:596
  9.8 0.1 shard_map.72
  9.9 1.3 %collective-permute-start.4 = (f32[10,2,256]{2,1,0:T(2,128)S(1)}, f32[10,2,256]{2,1,0:T(2,128)S(1)}, u32[]{:S(2)}, u32[]{:S(2)}) collective-permute-start(f32[10,2,256]{2,1,0:T(2,128)S(1)} %get-tuple-element.28.refs_4_), channel_id=1, source_target_pairs={{0,1},{1,2},{2,3},{3,0},{4,5},{5,6},{6,7},{7,4},{8,9},{9,10},{10,1... | collective-permute-start | bytes 61448 | tf_op jit(solution)/shard_map/ppermute | solution.py:596
  11.2 2.1 %collective-permute-start.5 = (f32[10,2,256]{2,1,0:T(2,128)S(1)}, f32[10,2,256]{2,1,0:T(2,128)S(1)}, u32[]{:S(2)}, u32[]{:S(2)}) collective-permute-start(f32[10,2,256]{2,1,0:T(2,128)S(1)} %get-tuple-element.29.refs_5_), channel_id=1, source_target_pairs={{0,3},{1,0},{2,1},{3,2},{4,7},{5,4},{6,5},{7,6},{8,11},{9,8},{10,9... | collective-permute-start | bytes 61448 | tf_op jit(solution)/shard_map/ppermute | solution.py:596
  13.3 1.6 %shard_map.70 = (f32[19,4,16,256]{3,2,1,0:T(8,128)S(1)}, f32[4,16,256]{2,1,0:T(8,128)S(1)}, f32[19,8,256]{2,1,0:T(8,128)S(1)}, f32[19,8,256]{2,1,0:T(8,128)S(1)}) custom-call(f32[19,4,16,256]{3,2,1,0:T(8,128)S(1)} %shard_map.68.post, f32[19,4,16,256]{3,2,1,0:T(8,128)S(1)} %copy-done, f32[4,16,256]{2,1,0:T(8,128)S(1)} %copy-done.2, ...), custom_call_target="tpu_custom_call" | custom-call | tf_op jit(solution)/shard_map/pallas_call | solution.py:577
  15.0 0.0 collective-permute-done.2.refs_2_
  15.0 0.0 collective-permute-done.3.refs_3_
  15.0 0.0 collective-permute-done.4.refs_6_
  15.0 0.0 collective-permute-done.5.refs_7_
  15.0 0.3 %shard_map.73 = (f32[19,8,256]{2,1,0:T(8,128)S(1)}, f32[19,8,256]{2,1,0:T(8,128)S(1)}, f32[8,256]{1,0:T(8,128)S(1)}, f32[5,16,256]{2,1,0:T(8,128)S(1)}, f32[5,16,256]{2,1,0:T(8,128)S(1)}) custom-call(f32[19,4,16,256]{3,2,1,0:T(8,128)S(1)} %get-tuple-element.23.out, f32[4,16,256]{2,1,0:T(8,128)S(1)} %copy-done.2, s32[4,16,256]{2,1,0:T(8,128)S(1)} %copy-done.3, ...), custom_call_target="tpu_custom_call" | custom-call | tf_op jit(solution)/shard_map/pallas_call | solution.py:577
  15.3 2.5 %collective-permute-start.6 = (f32[5,16,256]{2,1,0:T(8,128)S(1)}, f32[5,16,256]{2,1,0:T(8,128)S(1)}, u32[]{:S(2)}, u32[]{:S(2)}) collective-permute-start(f32[5,16,256]{2,1,0:T(8,128)S(1)} %get-tuple-element.38), channel_id=1, source_target_pairs={{0,4},{4,8},{8,12},{12,16},{16,20},{20,24},{24,28},{28,0},{1,5},{5... | collective-permute-start | bytes 245768 | tf_op jit(solution)/shard_map/ppermute | solution.py:596
  17.9 0.0 collective-permute-start.7
  17.9 1.6 %shard_map.74 = (f32[19,4,16,256]{3,2,1,0:T(8,128)}, f32[4,16,256]{2,1,0:T(8,128)}, f32[19,4,16,256]{3,2,1,0:T(8,128)S(1)}, f32[4,16,256]{2,1,0:T(8,128)S(1)}) custom-call(f32[19,4,16,256]{3,2,1,0:T(8,128)S(1)} %get-tuple-element.23.out, f32[19,8,256]{2,1,0:T(8,128)S(1)} %get-tuple-element.30.outer_rows, f32[19,8,256]{2,1,0:T(8,128)S(1)} %get-tuple-element.31.halo_rows, ...), custom_call_target="tpu_custom_call" | custom-call | tf_op jit(solution)/shard_map/pallas_call | solution.py:577
  19.5 0.6 %collective-permute-done.6.from_left = f32[5,16,256]{2,1,0:T(8,128)S(1)} collective-permute-done((f32[5,16,256]{2,1,0:T(8,128)S(1)}, f32[5,16,256]{2,1,0:T(8,128)S(1)}, u32[]{:S(2)}, u32[]{:S(2)}) %collective-permute-start.6) | collective-permute-done | bytes 81952 | tf_op jit(solution)/shard_map/ppermute | solution.py:596
  20.1 2.5 %collective-permute-done.7.from_right = f32[5,16,256]{2,1,0:T(8,128)S(1)} collective-permute-done((f32[5,16,256]{2,1,0:T(8,128)S(1)}, f32[5,16,256]{2,1,0:T(8,128)S(1)}, u32[]{:S(2)}, u32[]{:S(2)}) %collective-permute-start.7) | collective-permute-done | bytes 81952 | tf_op jit(solution)/shard_map/ppermute | solution.py:596
  22.6 1.3 %shard_map.75 = (f32[19,4,16,256]{3,2,1,0:T(8,128)}, f32[4,16,256]{2,1,0:T(8,128)}) custom-call(f32[19,4,16,256]{3,2,1,0:T(8,128)} %get-tuple-element.34.inner_start, f32[4,16,256]{2,1,0:T(8,128)} %get-tuple-element.35.inner_total, f32[19,4,16,256]{3,2,1,0:T(8,128)S(1)} %copy-done.1, ...), custom_call_target="tpu_custom_call", output_to_operand_aliasing={{0}: (0, {}), {1}: (1, {})} | custom-call | tf_op jit(solution)/shard_map/pallas_call | solution.py:577
Async XLA Ops:
  0.6 3.5 %copy-start.4 = (s32[4,16,256]{2,1,0:T(8,128)S(1)}, s32[4,16,256]{2,1,0:T(8,128)}, u32[]{:S(2)}) copy-start(s32[4,16,256]{2,1,0:T(8,128)} %flags.11) | copy-start | bytes 196612
  0.6 3.5 %copy-start.3 = (s32[4,16,256]{2,1,0:T(8,128)S(1)}, s32[4,16,256]{2,1,0:T(8,128)}, u32[]{:S(2)}) copy-start(s32[4,16,256]{2,1,0:T(8,128)} %solid.11) | copy-start | bytes 196612
  0.7 3.5 %copy-start.2 = (f32[4,16,256]{2,1,0:T(8,128)S(1)}, f32[4,16,256]{2,1,0:T(8,128)}, u32[]{:S(2)}) copy-start(f32[4,16,256]{2,1,0:T(8,128)} %resistance.11) | copy-start | bytes 196612
  0.7 3.5 %copy-start = (f32[19,4,16,256]{3,2,1,0:T(8,128)S(1)}, f32[19,4,16,256]{3,2,1,0:T(8,128)}, u32[]{:S(2)}) copy-start(f32[19,4,16,256]{3,2,1,0:T(8,128)} %adjoint.5) | copy-start | bytes 3735556
  0.7 3.5 %copy-start.1 = (f32[19,4,16,256]{3,2,1,0:T(8,128)S(1)}, f32[19,4,16,256]{3,2,1,0:T(8,128)}, u32[]{:S(2)}) copy-start(f32[19,4,16,256]{3,2,1,0:T(8,128)} %state.5) | copy-start | bytes 3735556
  2.3 6.4 %collective-permute-start = (f32[10,16,256]{2,1,0:T(8,128)S(1)}, f32[10,16,256]{2,1,0:T(8,128)S(1)}, u32[]{:S(2)}, u32[]{:S(2)}) collective-permute-start(f32[10,16,256]{2,1,0:T(8,128)S(1)} %get-tuple-element.21), channel_id=1, source_target_pairs={{0,4},{4,8},{8,12},{12,16},{16,20},{20,24},{24,28},{28,0},{1,5},{5... | collective-permute-start | bytes 491528 | tf_op jit(solution)/shard_map/ppermute | solution.py:596
  4.1 5.7 %collective-permute-start.1 = (f32[10,16,256]{2,1,0:T(8,128)S(1)}, f32[10,16,256]{2,1,0:T(8,128)S(1)}, u32[]{:S(2)}, u32[]{:S(2)}) collective-permute-start(f32[10,16,256]{2,1,0:T(8,128)S(1)} %get-tuple-element.22), channel_id=1, source_target_pairs={{0,28},{4,0},{8,4},{12,8},{16,12},{20,16},{24,20},{28,24},{1,29},{... | collective-permute-start | bytes 491528 | tf_op jit(solution)/shard_map/ppermute | solution.py:596
  5.2 9.7 %collective-permute-start.2 = (f32[27,4,256]{2,1,0:T(4,128)S(1)}, f32[27,4,256]{2,1,0:T(4,128)S(1)}, u32[]{:S(2)}, u32[]{:S(2)}) collective-permute-start(f32[27,4,256]{2,1,0:T(4,128)S(1)} %get-tuple-element.26.refs_0_), channel_id=1, source_target_pairs={{0,1},{1,2},{2,3},{3,0},{4,5},{5,6},{6,7},{7,4},{8,9},{9,10},{10,1... | collective-permute-start | bytes 331784 | tf_op jit(solution)/shard_map/ppermute | solution.py:596
  6.6 8.4 %collective-permute-start.3 = (f32[27,4,256]{2,1,0:T(4,128)S(1)}, f32[27,4,256]{2,1,0:T(4,128)S(1)}, u32[]{:S(2)}, u32[]{:S(2)}) collective-permute-start(f32[27,4,256]{2,1,0:T(4,128)S(1)} %get-tuple-element.27.refs_1_), channel_id=1, source_target_pairs={{0,3},{1,0},{2,1},{3,2},{4,7},{5,4},{6,5},{7,6},{8,11},{9,8},{10,9... | collective-permute-start | bytes 331784 | tf_op jit(solution)/shard_map/ppermute | solution.py:596
  9.9 5.1 %collective-permute-start.4 = (f32[10,2,256]{2,1,0:T(2,128)S(1)}, f32[10,2,256]{2,1,0:T(2,128)S(1)}, u32[]{:S(2)}, u32[]{:S(2)}) collective-permute-start(f32[10,2,256]{2,1,0:T(2,128)S(1)} %get-tuple-element.28.refs_4_), channel_id=1, source_target_pairs={{0,1},{1,2},{2,3},{3,0},{4,5},{5,6},{6,7},{7,4},{8,9},{9,10},{10,1... | collective-permute-start | bytes 61448 | tf_op jit(solution)/shard_map/ppermute | solution.py:596
  11.2 3.8 %collective-permute-start.5 = (f32[10,2,256]{2,1,0:T(2,128)S(1)}, f32[10,2,256]{2,1,0:T(2,128)S(1)}, u32[]{:S(2)}, u32[]{:S(2)}) collective-permute-start(f32[10,2,256]{2,1,0:T(2,128)S(1)} %get-tuple-element.29.refs_5_), channel_id=1, source_target_pairs={{0,3},{1,0},{2,1},{3,2},{4,7},{5,4},{6,5},{7,6},{8,11},{9,8},{10,9... | collective-permute-start | bytes 61448 | tf_op jit(solution)/shard_map/ppermute | solution.py:596
  15.3 4.8 %collective-permute-start.6 = (f32[5,16,256]{2,1,0:T(8,128)S(1)}, f32[5,16,256]{2,1,0:T(8,128)S(1)}, u32[]{:S(2)}, u32[]{:S(2)}) collective-permute-start(f32[5,16,256]{2,1,0:T(8,128)S(1)} %get-tuple-element.38), channel_id=1, source_target_pairs={{0,4},{4,8},{8,12},{12,16},{16,20},{20,24},{24,28},{28,0},{1,5},{5... | collective-permute-start | bytes 245768 | tf_op jit(solution)/shard_map/ppermute | solution.py:596
  17.9 4.8 %collective-permute-start.7 = (f32[5,16,256]{2,1,0:T(8,128)S(1)}, f32[5,16,256]{2,1,0:T(8,128)S(1)}, u32[]{:S(2)}, u32[]{:S(2)}) collective-permute-start(f32[5,16,256]{2,1,0:T(8,128)S(1)} %get-tuple-element.39), channel_id=1, source_target_pairs={{0,28},{4,0},{8,4},{12,8},{16,12},{20,16},{24,20},{28,24},{1,29},{... | collective-permute-start | bytes 245768 | tf_op jit(solution)/shard_map/ppermute | solution.py:596

commit v6 on v5

--- a/solution.py
+++ b/solution.py
@@ -223,22 +223,20 @@
 ):
     nx, ny, nz = far_resistance.shape
     sides = ((right, 1, nx - 1), (left, -1, 0))
-    copies, first = [], []
+    pairs, faces = [], []
     for side, (message, way, x) in enumerate(sides):
-        pairs = [
+        pairs += [
             (far_state.at[:, x], state.at[side]),
             (far_resistance.at[x], resistance.at[side]),
             (far_solid.at[x], solid.at[side]),
             (far_flags.at[x], flags.at[side]),
         ]
-        pairs += [(far_adjoint.at[i, x], message.at[x_plane(1, i)]) for i in moving(-1, 0, way)]
-        first.append(len(copies))
-        for source, target in pairs:
-            copies.append(pltpu.make_async_copy(source, target, done.at[len(copies)]))
+        faces += [(far_adjoint.at[i, x], message.at[x_plane(1, i)]) for i in moving(-1, 0, way)]
+    copies = [pltpu.make_async_copy(*pair, done.at[k]) for k, pair in enumerate(pairs + faces)]
     for copy in copies:
         copy.start()
     for side, (message, way, _) in enumerate(sides):
-        for copy in copies[first[side] : first[side] + 4]:
+        for copy in copies[4 * side : 4 * side + 4]:
             copy.wait()
 
         def step(t, carry, side=side, message=message, way=way):
@@ -255,9 +253,8 @@
             return carry
 
         lax.fori_loop(0, ny // 8, step, 0)
-    for side in range(2):
-        for copy in copies[first[side] + 4 : first[side] + 9]:
-            copy.wait()
+    for copy in copies[8:]:
+        copy.wait()
 
 
 def post_kernel(state, adjoint, resistance, solid, flags, post):
@@ -607,6 +604,7 @@
     )
     sides = exchange("gx", right, left)
     cells = (resistance, solid_mask, flags)
+    checkpoint, adjoint_end, right = lax.optimization_barrier((checkpoint, adjoint_end, right))
     (post,) = call(post_kernel, [whole], checkpoint, adjoint_end, *cells)
     rims_out = call(
         rim_kernel, [(PLANES, nx, nz)] * 2, post, adjoint_end, *cells,

time: 24.3 us -> 23.7 us (0.975)
  the two profiles are of different devices: /device:TPU:3 before, /device:TPU:0 now
where the time goes in v6:
time: 23.7 us; the launch traced here: 23.5 us
  starting transfers between devices  13.8 us (58%)
  Pallas kernels  7.63 us (32%)
  waiting for transfers between devices  1.25 us (5%)
  between operations  0.77 us (3%)
    ppermute x4, starting transfers between devices, exchange(): lax.ppermute(backward, axis, behind)  10.5 us
    pallas_call x8, Pallas kernels, call(): pl.pallas_call(kernel, out_shape=made, in_specs=[HBM if k in far else VME...  7.63 us
    ppermute x4, starting transfers between devices, exchange(): lax.ppermute(onward, axis, ahead)  3.32 us
    ppermute x4, waiting for transfers between devices, exchange(): lax.ppermute(onward, axis, ahead)  1.24 us
  transfers between devices with their start and end apart: 8, of which 3 were waited for; matrix products, arithmetic and copies ran while one was open for 0% of the time, Pallas kernels for 19%

profile of v6, /device:TPU:0, one launch (start us, length us, event | category | flops | bytes accessed | tf_op | source)
XLA Modules:
  0.0 23.5 jit_solution(6575339018149164916)
XLA Ops:
  0.6 0.0 copy-start.4
  0.6 0.0 copy-start.3
  0.7 0.0 copy-start.2
  0.7 0.0 copy-start
  0.7 0.0 copy-start.1
  0.7 1.6 %shard_map.68 = (f32[10,16,256]{2,1,0:T(8,128)S(1)}, f32[10,16,256]{2,1,0:T(8,128)S(1)}) custom-call(f32[19,4,16,256]{3,2,1,0:T(8,128)} %state.2, f32[19,4,16,256]{3,2,1,0:T(8,128)} %adjoint.2, f32[4,16,256]{2,1,0:T(8,128)} %resistance.11, s32[4,16,256]{2,1,0:T(8,128)} %solid.11, s32[4,16,256]{2,1,0:T(8,128)} %flags.11), custom_call_target="tpu_custom_call" | custom-call | tf_op jit(solution)/shard_map/pallas_call | solution.py:574
  2.3 3.4 %collective-permute-start.1 = (f32[10,16,256]{2,1,0:T(8,128)S(1)}, f32[10,16,256]{2,1,0:T(8,128)S(1)}, u32[]{:S(2)}, u32[]{:S(2)}) collective-permute-start(f32[10,16,256]{2,1,0:T(8,128)S(1)} %get-tuple-element.26), channel_id=1, source_target_pairs={{0,28},{4,0},{8,4},{12,8},{16,12},{20,16},{24,20},{28,24},{1,29},{... | collective-permute-start | bytes 491528 | tf_op jit(solution)/shard_map/ppermute | solution.py:593
  5.7 0.0 collective-permute-start
  5.7 0.0 copy-done.4
  5.7 0.0 copy-done.3
  5.7 0.0 copy-done.2
  5.7 0.0 copy-done
  5.7 0.0 copy-done.1
  5.7 0.8 %shard_map.69.post = f32[19,4,16,256]{3,2,1,0:T(8,128)S(1)} custom-call(f32[19,4,16,256]{3,2,1,0:T(8,128)S(1)} %copy-done.1, f32[19,4,16,256]{3,2,1,0:T(8,128)S(1)} %copy-done, f32[4,16,256]{2,1,0:T(8,128)S(1)} %copy-done.2, s32[4,16,256]{2,1,0:T(8,128)S(1)} %copy-done.3, s32[4,16,256]{2,1,0:T(8,128)S(1)} %copy-done.4), custom_call_target="tpu_custom_call" | custom-call | tf_op jit(solution)/shard_map/pallas_call | solution.py:574
  6.5 0.3 %shard_map.71 = (f32[27,4,256]{2,1,0:T(4,128)S(1)}, f32[27,4,256]{2,1,0:T(4,128)S(1)}) custom-call(f32[19,4,16,256]{3,2,1,0:T(8,128)S(1)} %shard_map.69.post, f32[19,4,16,256]{3,2,1,0:T(8,128)S(1)} %copy-done, f32[4,16,256]{2,1,0:T(8,128)S(1)} %copy-done.2, s32[4,16,256]{2,1,0:T(8,128)S(1)} %copy-done.3, s32[4,16,256]{2,1,0:T(8,128)S(1)} %copy-done.4), custom_call_target="tpu_custom_call" | custom-call | tf_op jit(solution)/shard_map/pallas_call | solution.py:574
  6.8 1.6 %collective-permute-start.2 = (f32[27,4,256]{2,1,0:T(4,128)S(1)}, f32[27,4,256]{2,1,0:T(4,128)S(1)}, u32[]{:S(2)}, u32[]{:S(2)}) collective-permute-start(f32[27,4,256]{2,1,0:T(4,128)S(1)} %get-tuple-element.30.refs_0_), channel_id=1, source_target_pairs={{0,1},{1,2},{2,3},{3,0},{4,5},{5,6},{6,7},{7,4},{8,9},{9,10},{10,1... | collective-permute-start | bytes 331784 | tf_op jit(solution)/shard_map/ppermute | solution.py:593
  8.4 2.2 %collective-permute-start.3 = (f32[27,4,256]{2,1,0:T(4,128)S(1)}, f32[27,4,256]{2,1,0:T(4,128)S(1)}, u32[]{:S(2)}, u32[]{:S(2)}) collective-permute-start(f32[27,4,256]{2,1,0:T(4,128)S(1)} %get-tuple-element.31.refs_1_), channel_id=1, source_target_pairs={{0,3},{1,0},{2,1},{3,2},{4,7},{5,4},{6,5},{7,6},{8,11},{9,8},{10,9... | collective-permute-start | bytes 331784 | tf_op jit(solution)/shard_map/ppermute | solution.py:593
  10.6 0.0 collective-permute-done.1.from_right
  10.6 0.6 %collective-permute-done.from_left = f32[10,16,256]{2,1,0:T(8,128)S(1)} collective-permute-done((f32[10,16,256]{2,1,0:T(8,128)S(1)}, f32[10,16,256]{2,1,0:T(8,128)S(1)}, u32[]{:S(2)}, u32[]{:S(2)}) %collective-permute-start) | collective-permute-done | bytes 163872 | tf_op jit(solution)/shard_map/ppermute | solution.py:593
  11.3 0.1 shard_map.72
  11.4 1.6 %collective-permute-start.4 = (f32[10,2,256]{2,1,0:T(2,128)S(1)}, f32[10,2,256]{2,1,0:T(2,128)S(1)}, u32[]{:S(2)}, u32[]{:S(2)}) collective-permute-start(f32[10,2,256]{2,1,0:T(2,128)S(1)} %get-tuple-element.32.refs_4_), channel_id=1, source_target_pairs={{0,1},{1,2},{2,3},{3,0},{4,5},{5,6},{6,7},{7,4},{8,9},{9,10},{10,1... | collective-permute-start | bytes 61448 | tf_op jit(solution)/shard_map/ppermute | solution.py:593
  13.0 2.2 %collective-permute-start.5 = (f32[10,2,256]{2,1,0:T(2,128)S(1)}, f32[10,2,256]{2,1,0:T(2,128)S(1)}, u32[]{:S(2)}, u32[]{:S(2)}) collective-permute-start(f32[10,2,256]{2,1,0:T(2,128)S(1)} %get-tuple-element.33.refs_5_), channel_id=1, source_target_pairs={{0,3},{1,0},{2,1},{3,2},{4,7},{5,4},{6,5},{7,6},{8,11},{9,8},{10,9... | collective-permute-start | bytes 61448 | tf_op jit(solution)/shard_map/ppermute | solution.py:593
  15.3 1.6 %shard_map.70 = (f32[19,4,16,256]{3,2,1,0:T(8,128)S(1)}, f32[4,16,256]{2,1,0:T(8,128)S(1)}, f32[19,8,256]{2,1,0:T(8,128)S(1)}, f32[19,8,256]{2,1,0:T(8,128)S(1)}) custom-call(f32[19,4,16,256]{3,2,1,0:T(8,128)S(1)} %shard_map.69.post, f32[19,4,16,256]{3,2,1,0:T(8,128)S(1)} %copy-done, f32[4,16,256]{2,1,0:T(8,128)S(1)} %copy-done.2, ...), custom_call_target="tpu_custom_call" | custom-call | tf_op jit(solution)/shard_map/pallas_call | solution.py:574
  16.9 0.0 collective-permute-done.2.refs_2_
  16.9 0.0 collective-permute-done.3.refs_3_
  16.9 0.1 collective-permute-done.4.refs_6_
  17.0 0.0 collective-permute-done.5.refs_7_
  17.0 0.3 %shard_map.73 = (f32[19,8,256]{2,1,0:T(8,128)S(1)}, f32[19,8,256]{2,1,0:T(8,128)S(1)}, f32[8,256]{1,0:T(8,128)S(1)}, f32[5,16,256]{2,1,0:T(8,128)S(1)}, f32[5,16,256]{2,1,0:T(8,128)S(1)}) custom-call(f32[19,4,16,256]{3,2,1,0:T(8,128)S(1)} %get-tuple-element.27.out, f32[4,16,256]{2,1,0:T(8,128)S(1)} %copy-done.2, s32[4,16,256]{2,1,0:T(8,128)S(1)} %copy-done.3, ...), custom_call_target="tpu_custom_call" | custom-call | tf_op jit(solution)/shard_map/pallas_call | solution.py:574
  17.4 0.1 collective-permute-start.6
  17.4 2.6 %collective-permute-start.7 = (f32[5,16,256]{2,1,0:T(8,128)S(1)}, f32[5,16,256]{2,1,0:T(8,128)S(1)}, u32[]{:S(2)}, u32[]{:S(2)}) collective-permute-start(f32[5,16,256]{2,1,0:T(8,128)S(1)} %get-tuple-element.43), channel_id=1, source_target_pairs={{0,28},{4,0},{8,4},{12,8},{16,12},{20,16},{24,20},{28,24},{1,29},{... | collective-permute-start | bytes 245768 | tf_op jit(solution)/shard_map/ppermute | solution.py:593
  20.1 1.6 %shard_map.74 = (f32[19,4,16,256]{3,2,1,0:T(8,128)}, f32[4,16,256]{2,1,0:T(8,128)}, f32[19,4,16,256]{3,2,1,0:T(8,128)S(1)}, f32[4,16,256]{2,1,0:T(8,128)S(1)}) custom-call(f32[19,4,16,256]{3,2,1,0:T(8,128)S(1)} %get-tuple-element.27.out, f32[19,8,256]{2,1,0:T(8,128)S(1)} %get-tuple-element.34.outer_rows, f32[19,8,256]{2,1,0:T(8,128)S(1)} %get-tuple-element.35.halo_rows, ...), custom_call_target="tpu_custom_call" | custom-call | tf_op jit(solution)/shard_map/pallas_call | solution.py:574
  21.7 0.5 %collective-permute-done.6.from_left = f32[5,16,256]{2,1,0:T(8,128)S(1)} collective-permute-done((f32[5,16,256]{2,1,0:T(8,128)S(1)}, f32[5,16,256]{2,1,0:T(8,128)S(1)}, u32[]{:S(2)}, u32[]{:S(2)}) %collective-permute-start.6) | collective-permute-done | bytes 81952 | tf_op jit(solution)/shard_map/ppermute | solution.py:593
  22.2 0.0 collective-permute-done.7.from_right
  22.2 1.3 %shard_map.75 = (f32[19,4,16,256]{3,2,1,0:T(8,128)}, f32[4,16,256]{2,1,0:T(8,128)}) custom-call(f32[19,4,16,256]{3,2,1,0:T(8,128)} %get-tuple-element.38.inner_start, f32[4,16,256]{2,1,0:T(8,128)} %get-tuple-element.39.inner_total, f32[19,4,16,256]{3,2,1,0:T(8,128)S(1)} %copy-done.1, ...), custom_call_target="tpu_custom_call", output_to_operand_aliasing={{0}: (0, {}), {1}: (1, {})} | custom-call | tf_op jit(solution)/shard_map/pallas_call | solution.py:574
Async XLA Ops:
  0.6 5.0 %copy-start.4 = (s32[4,16,256]{2,1,0:T(8,128)S(1)}, s32[4,16,256]{2,1,0:T(8,128)}, u32[]{:S(2)}) copy-start(s32[4,16,256]{2,1,0:T(8,128)} %flags.11) | copy-start | bytes 196612
  0.6 5.0 %copy-start.3 = (s32[4,16,256]{2,1,0:T(8,128)S(1)}, s32[4,16,256]{2,1,0:T(8,128)}, u32[]{:S(2)}) copy-start(s32[4,16,256]{2,1,0:T(8,128)} %solid.11) | copy-start | bytes 196612
  0.7 5.0 %copy-start.2 = (f32[4,16,256]{2,1,0:T(8,128)S(1)}, f32[4,16,256]{2,1,0:T(8,128)}, u32[]{:S(2)}) copy-start(f32[4,16,256]{2,1,0:T(8,128)} %resistance.11) | copy-start | bytes 196612
  0.7 5.0 %copy-start = (f32[19,4,16,256]{3,2,1,0:T(8,128)S(1)}, f32[19,4,16,256]{3,2,1,0:T(8,128)}, u32[]{:S(2)}) copy-start(f32[19,4,16,256]{3,2,1,0:T(8,128)} %adjoint.2) | copy-start | bytes 3735556
  0.7 5.0 %copy-start.1 = (f32[19,4,16,256]{3,2,1,0:T(8,128)S(1)}, f32[19,4,16,256]{3,2,1,0:T(8,128)}, u32[]{:S(2)}) copy-start(f32[19,4,16,256]{3,2,1,0:T(8,128)} %state.2) | copy-start | bytes 3735556
  2.3 8.4 %collective-permute-start.1 = (f32[10,16,256]{2,1,0:T(8,128)S(1)}, f32[10,16,256]{2,1,0:T(8,128)S(1)}, u32[]{:S(2)}, u32[]{:S(2)}) collective-permute-start(f32[10,16,256]{2,1,0:T(8,128)S(1)} %get-tuple-element.26), channel_id=1, source_target_pairs={{0,28},{4,0},{8,4},{12,8},{16,12},{20,16},{24,20},{28,24},{1,29},{... | collective-permute-start | bytes 491528 | tf_op jit(solution)/shard_map/ppermute | solution.py:593
  5.7 5.6 %collective-permute-start = (f32[10,16,256]{2,1,0:T(8,128)S(1)}, f32[10,16,256]{2,1,0:T(8,128)S(1)}, u32[]{:S(2)}, u32[]{:S(2)}) collective-permute-start(f32[10,16,256]{2,1,0:T(8,128)S(1)} %get-tuple-element.23), channel_id=1, source_target_pairs={{0,4},{4,8},{8,12},{12,16},{16,20},{20,24},{24,28},{28,0},{1,5},{5... | collective-permute-start | bytes 491528 | tf_op jit(solution)/shard_map/ppermute | solution.py:593
  6.8 10.1 %collective-permute-start.2 = (f32[27,4,256]{2,1,0:T(4,128)S(1)}, f32[27,4,256]{2,1,0:T(4,128)S(1)}, u32[]{:S(2)}, u32[]{:S(2)}) collective-permute-start(f32[27,4,256]{2,1,0:T(4,128)S(1)} %get-tuple-element.30.refs_0_), channel_id=1, source_target_pairs={{0,1},{1,2},{2,3},{3,0},{4,5},{5,6},{6,7},{7,4},{8,9},{9,10},{10,1... | collective-permute-start | bytes 331784 | tf_op jit(solution)/shard_map/ppermute | solution.py:593
  8.4 8.5 %collective-permute-start.3 = (f32[27,4,256]{2,1,0:T(4,128)S(1)}, f32[27,4,256]{2,1,0:T(4,128)S(1)}, u32[]{:S(2)}, u32[]{:S(2)}) collective-permute-start(f32[27,4,256]{2,1,0:T(4,128)S(1)} %get-tuple-element.31.refs_1_), channel_id=1, source_target_pairs={{0,3},{1,0},{2,1},{3,2},{4,7},{5,4},{6,5},{7,6},{8,11},{9,8},{10,9... | collective-permute-start | bytes 331784 | tf_op jit(solution)/shard_map/ppermute | solution.py:593
  11.4 5.6 %collective-permute-start.4 = (f32[10,2,256]{2,1,0:T(2,128)S(1)}, f32[10,2,256]{2,1,0:T(2,128)S(1)}, u32[]{:S(2)}, u32[]{:S(2)}) collective-permute-start(f32[10,2,256]{2,1,0:T(2,128)S(1)} %get-tuple-element.32.refs_4_), channel_id=1, source_target_pairs={{0,1},{1,2},{2,3},{3,0},{4,5},{5,6},{6,7},{7,4},{8,9},{9,10},{10,1... | collective-permute-start | bytes 61448 | tf_op jit(solution)/shard_map/ppermute | solution.py:593
  13.0 4.0 %collective-permute-start.5 = (f32[10,2,256]{2,1,0:T(2,128)S(1)}, f32[10,2,256]{2,1,0:T(2,128)S(1)}, u32[]{:S(2)}, u32[]{:S(2)}) collective-permute-start(f32[10,2,256]{2,1,0:T(2,128)S(1)} %get-tuple-element.33.refs_5_), channel_id=1, source_target_pairs={{0,3},{1,0},{2,1},{3,2},{4,7},{5,4},{6,5},{7,6},{8,11},{9,8},{10,9... | collective-permute-start | bytes 61448 | tf_op jit(solution)/shard_map/ppermute | solution.py:593
  17.4 4.8 %collective-permute-start.6 = (f32[5,16,256]{2,1,0:T(8,128)S(1)}, f32[5,16,256]{2,1,0:T(8,128)S(1)}, u32[]{:S(2)}, u32[]{:S(2)}) collective-permute-start(f32[5,16,256]{2,1,0:T(8,128)S(1)} %get-tuple-element.42), channel_id=1, source_target_pairs={{0,4},{4,8},{8,12},{12,16},{16,20},{20,24},{24,28},{28,0},{1,5},{5... | collective-permute-start | bytes 245768 | tf_op jit(solution)/shard_map/ppermute | solution.py:593
  17.4 4.8 %collective-permute-start.7 = (f32[5,16,256]{2,1,0:T(8,128)S(1)}, f32[5,16,256]{2,1,0:T(8,128)S(1)}, u32[]{:S(2)}, u32[]{:S(2)}) collective-permute-start(f32[5,16,256]{2,1,0:T(8,128)S(1)} %get-tuple-element.43), channel_id=1, source_target_pairs={{0,28},{4,0},{8,4},{12,8},{16,12},{20,16},{24,20},{28,24},{1,29},{... | collective-permute-start | bytes 245768 | tf_op jit(solution)/shard_map/ppermute | solution.py:593

commit v7 on v6

--- a/solution.py
+++ b/solution.py
@@ -252,7 +252,7 @@
                     message[(x_plane(0, i), *at)] = out[i]
             return carry
 
-        lax.fori_loop(0, ny // 8, step, 0)
+        lax.fori_loop(0, ny // 8, step, 0, unroll=True)
     for copy in copies[8:]:
         copy.wait()
 
@@ -275,7 +275,7 @@
                 post[(i, *at)] = out[i]
         return carry
 
-    lax.fori_loop(0, nx * tiles, step, 0)
+    lax.fori_loop(0, nx * tiles, step, 0, unroll=2)
 
 
 def rim_kernel(post, adjoint, resistance, solid, flags, up, down, work, near, cells):
@@ -417,7 +417,7 @@
                 out[(i, *at)] = new[i]
         return carry
 
-    lax.fori_loop(0, nx * tiles, step, 0)
+    lax.fori_loop(0, nx * tiles, step, 0, unroll=2)
 
 
 def pulled_block(out, outer_rows, halo_rows, i, x):
@@ -527,7 +527,7 @@
                 total[slot, rows, lanes] = partial[at] + jnp.where(solid[at] == 1, 0.0, sens)
             return carry
 
-        lax.fori_loop(0, ny // 8, step, 0)
+        lax.fori_loop(0, ny // 8, step, 0, unroll=True)
         pairs = ((start.at[slot], far_start.at[:, x]), (total.at[slot], far_total.at[x]))
         for k, pair in enumerate(pairs):
             copies.append(pltpu.make_async_copy(*pair, done.at[2 * slot + k]))

time: 23.7 us -> 23.6 us (level)
  Pallas kernels: 7.63 us -> 7.36 us
    pallas_call x8, Pallas kernels: 7.63 us -> 7.36 us  [call(): pl.pallas_call(kernel, out_shape=made, in_specs=[HBM if k in far else VME...]
  transfers between devices with their start and end apart: 8 -> 8, of which waited for: 3 -> 3; matrix products, arithmetic and copies ran while one was open for 0% -> 0% of each run, Pallas kernels for 19% -> 18%
where the time goes in v7:
time: 23.6 us; the launch traced here: 23.4 us
  starting transfers between devices  13.8 us (58%)
  Pallas kernels  7.36 us (31%)
  waiting for transfers between devices  1.44 us (6%)
  between operations  0.77 us (3%)
    ppermute x4, starting transfers between devices, exchange(): lax.ppermute(backward, axis, behind)  10.5 us
    pallas_call x8, Pallas kernels, call(): pl.pallas_call(kernel, out_shape=made, in_specs=[HBM if k in far else VME...  7.36 us
    ppermute x4, starting transfers between devices, exchange(): lax.ppermute(onward, axis, ahead)  3.32 us
    ppermute x4, waiting for transfers between devices, exchange(): lax.ppermute(onward, axis, ahead)  1.43 us
  transfers between devices with their start and end apart: 8, of which 3 were waited for; matrix products, arithmetic and copies ran while one was open for 0% of the time, Pallas kernels for 18%

profile of v7, /device:TPU:0, one launch (start us, length us, event | category | flops | bytes accessed | tf_op | source)
XLA Modules:
  0.0 23.4 jit_solution(3469496759812939270)
XLA Ops:
  0.6 0.0 copy-start.4
  0.6 0.0 copy-start.3
  0.7 0.0 copy-start.2
  0.7 0.0 copy-start
  0.7 0.0 copy-start.1
  0.7 1.6 %shard_map.68 = (f32[10,16,256]{2,1,0:T(8,128)S(1)}, f32[10,16,256]{2,1,0:T(8,128)S(1)}) custom-call(f32[19,4,16,256]{3,2,1,0:T(8,128)} %state.2, f32[19,4,16,256]{3,2,1,0:T(8,128)} %adjoint.2, f32[4,16,256]{2,1,0:T(8,128)} %resistance.11, s32[4,16,256]{2,1,0:T(8,128)} %solid.11, s32[4,16,256]{2,1,0:T(8,128)} %flags.11), custom_call_target="tpu_custom_call" | custom-call | tf_op jit(solution)/shard_map/pallas_call | solution.py:574
  2.2 3.4 %collective-permute-start.1 = (f32[10,16,256]{2,1,0:T(8,128)S(1)}, f32[10,16,256]{2,1,0:T(8,128)S(1)}, u32[]{:S(2)}, u32[]{:S(2)}) collective-permute-start(f32[10,16,256]{2,1,0:T(8,128)S(1)} %get-tuple-element.26), channel_id=1, source_target_pairs={{0,28},{4,0},{8,4},{12,8},{16,12},{20,16},{24,20},{28,24},{1,29},{... | collective-permute-start | bytes 491528 | tf_op jit(solution)/shard_map/ppermute | solution.py:593
  5.6 0.0 collective-permute-start
  5.6 0.0 copy-done.4
  5.6 0.0 copy-done.3
  5.6 0.0 copy-done.2
  5.7 0.0 copy-done
  5.7 0.0 copy-done.1
  5.7 0.7 %shard_map.69.post = f32[19,4,16,256]{3,2,1,0:T(8,128)S(1)} custom-call(f32[19,4,16,256]{3,2,1,0:T(8,128)S(1)} %copy-done.1, f32[19,4,16,256]{3,2,1,0:T(8,128)S(1)} %copy-done, f32[4,16,256]{2,1,0:T(8,128)S(1)} %copy-done.2, s32[4,16,256]{2,1,0:T(8,128)S(1)} %copy-done.3, s32[4,16,256]{2,1,0:T(8,128)S(1)} %copy-done.4), custom_call_target="tpu_custom_call" | custom-call | tf_op jit(solution)/shard_map/pallas_call | solution.py:574
  6.4 0.3 %shard_map.71 = (f32[27,4,256]{2,1,0:T(4,128)S(1)}, f32[27,4,256]{2,1,0:T(4,128)S(1)}) custom-call(f32[19,4,16,256]{3,2,1,0:T(8,128)S(1)} %shard_map.69.post, f32[19,4,16,256]{3,2,1,0:T(8,128)S(1)} %copy-done, f32[4,16,256]{2,1,0:T(8,128)S(1)} %copy-done.2, s32[4,16,256]{2,1,0:T(8,128)S(1)} %copy-done.3, s32[4,16,256]{2,1,0:T(8,128)S(1)} %copy-done.4), custom_call_target="tpu_custom_call" | custom-call | tf_op jit(solution)/shard_map/pallas_call | solution.py:574
  6.7 1.6 %collective-permute-start.2 = (f32[27,4,256]{2,1,0:T(4,128)S(1)}, f32[27,4,256]{2,1,0:T(4,128)S(1)}, u32[]{:S(2)}, u32[]{:S(2)}) collective-permute-start(f32[27,4,256]{2,1,0:T(4,128)S(1)} %get-tuple-element.30.refs_0_), channel_id=1, source_target_pairs={{0,1},{1,2},{2,3},{3,0},{4,5},{5,6},{6,7},{7,4},{8,9},{9,10},{10,1... | collective-permute-start | bytes 331784 | tf_op jit(solution)/shard_map/ppermute | solution.py:593
  8.4 2.2 %collective-permute-start.3 = (f32[27,4,256]{2,1,0:T(4,128)S(1)}, f32[27,4,256]{2,1,0:T(4,128)S(1)}, u32[]{:S(2)}, u32[]{:S(2)}) collective-permute-start(f32[27,4,256]{2,1,0:T(4,128)S(1)} %get-tuple-element.31.refs_1_), channel_id=1, source_target_pairs={{0,3},{1,0},{2,1},{3,2},{4,7},{5,4},{6,5},{7,6},{8,11},{9,8},{10,9... | collective-permute-start | bytes 331784 | tf_op jit(solution)/shard_map/ppermute | solution.py:593
  10.6 0.0 collective-permute-done.1.from_right
  10.6 0.7 %collective-permute-done.from_left = f32[10,16,256]{2,1,0:T(8,128)S(1)} collective-permute-done((f32[10,16,256]{2,1,0:T(8,128)S(1)}, f32[10,16,256]{2,1,0:T(8,128)S(1)}, u32[]{:S(2)}, u32[]{:S(2)}) %collective-permute-start) | collective-permute-done | bytes 163872 | tf_op jit(solution)/shard_map/ppermute | solution.py:593
  11.3 0.1 shard_map.72
  11.4 1.6 %collective-permute-start.4 = (f32[10,2,256]{2,1,0:T(2,128)S(1)}, f32[10,2,256]{2,1,0:T(2,128)S(1)}, u32[]{:S(2)}, u32[]{:S(2)}) collective-permute-start(f32[10,2,256]{2,1,0:T(2,128)S(1)} %get-tuple-element.32.refs_4_), channel_id=1, source_target_pairs={{0,1},{1,2},{2,3},{3,0},{4,5},{5,6},{6,7},{7,4},{8,9},{9,10},{10,1... | collective-permute-start | bytes 61448 | tf_op jit(solution)/shard_map/ppermute | solution.py:593
  13.0 2.2 %collective-permute-start.5 = (f32[10,2,256]{2,1,0:T(2,128)S(1)}, f32[10,2,256]{2,1,0:T(2,128)S(1)}, u32[]{:S(2)}, u32[]{:S(2)}) collective-permute-start(f32[10,2,256]{2,1,0:T(2,128)S(1)} %get-tuple-element.33.refs_5_), channel_id=1, source_target_pairs={{0,3},{1,0},{2,1},{3,2},{4,7},{5,4},{6,5},{7,6},{8,11},{9,8},{10,9... | collective-permute-start | bytes 61448 | tf_op jit(solution)/shard_map/ppermute | solution.py:593
  15.3 1.6 %shard_map.70 = (f32[19,4,16,256]{3,2,1,0:T(8,128)S(1)}, f32[4,16,256]{2,1,0:T(8,128)S(1)}, f32[19,8,256]{2,1,0:T(8,128)S(1)}, f32[19,8,256]{2,1,0:T(8,128)S(1)}) custom-call(f32[19,4,16,256]{3,2,1,0:T(8,128)S(1)} %shard_map.69.post, f32[19,4,16,256]{3,2,1,0:T(8,128)S(1)} %copy-done, f32[4,16,256]{2,1,0:T(8,128)S(1)} %copy-done.2, ...), custom_call_target="tpu_custom_call" | custom-call | tf_op jit(solution)/shard_map/pallas_call | solution.py:574
  16.9 0.0 collective-permute-done.2.refs_2_
  16.9 0.0 collective-permute-done.3.refs_3_
  16.9 0.1 collective-permute-done.4.refs_6_
  17.0 0.0 collective-permute-done.5.refs_7_
  17.0 0.3 %shard_map.73 = (f32[19,8,256]{2,1,0:T(8,128)S(1)}, f32[19,8,256]{2,1,0:T(8,128)S(1)}, f32[8,256]{1,0:T(8,128)S(1)}, f32[5,16,256]{2,1,0:T(8,128)S(1)}, f32[5,16,256]{2,1,0:T(8,128)S(1)}) custom-call(f32[19,4,16,256]{3,2,1,0:T(8,128)S(1)} %get-tuple-element.27.out, f32[4,16,256]{2,1,0:T(8,128)S(1)} %copy-done.2, s32[4,16,256]{2,1,0:T(8,128)S(1)} %copy-done.3, ...), custom_call_target="tpu_custom_call" | custom-call | tf_op jit(solution)/shard_map/pallas_call | solution.py:574
  17.3 0.1 collective-permute-start.6
  17.4 2.6 %collective-permute-start.7 = (f32[5,16,256]{2,1,0:T(8,128)S(1)}, f32[5,16,256]{2,1,0:T(8,128)S(1)}, u32[]{:S(2)}, u32[]{:S(2)}) collective-permute-start(f32[5,16,256]{2,1,0:T(8,128)S(1)} %get-tuple-element.43), channel_id=1, source_target_pairs={{0,28},{4,0},{8,4},{12,8},{16,12},{20,16},{24,20},{28,24},{1,29},{... | collective-permute-start | bytes 245768 | tf_op jit(solution)/shard_map/ppermute | solution.py:593
  20.0 1.5 %shard_map.74 = (f32[19,4,16,256]{3,2,1,0:T(8,128)}, f32[4,16,256]{2,1,0:T(8,128)}, f32[19,4,16,256]{3,2,1,0:T(8,128)S(1)}, f32[4,16,256]{2,1,0:T(8,128)S(1)}) custom-call(f32[19,4,16,256]{3,2,1,0:T(8,128)S(1)} %get-tuple-element.27.out, f32[19,8,256]{2,1,0:T(8,128)S(1)} %get-tuple-element.34.outer_rows, f32[19,8,256]{2,1,0:T(8,128)S(1)} %get-tuple-element.35.halo_rows, ...), custom_call_target="tpu_custom_call" | custom-call | tf_op jit(solution)/shard_map/pallas_call | solution.py:574
  21.5 0.6 %collective-permute-done.6.from_left = f32[5,16,256]{2,1,0:T(8,128)S(1)} collective-permute-done((f32[5,16,256]{2,1,0:T(8,128)S(1)}, f32[5,16,256]{2,1,0:T(8,128)S(1)}, u32[]{:S(2)}, u32[]{:S(2)}) %collective-permute-start.6) | collective-permute-done | bytes 81952 | tf_op jit(solution)/shard_map/ppermute | solution.py:593
  22.2 0.0 collective-permute-done.7.from_right
  22.2 1.3 %shard_map.75 = (f32[19,4,16,256]{3,2,1,0:T(8,128)}, f32[4,16,256]{2,1,0:T(8,128)}) custom-call(f32[19,4,16,256]{3,2,1,0:T(8,128)} %get-tuple-element.38.inner_start, f32[4,16,256]{2,1,0:T(8,128)} %get-tuple-element.39.inner_total, f32[19,4,16,256]{3,2,1,0:T(8,128)S(1)} %copy-done.1, ...), custom_call_target="tpu_custom_call", output_to_operand_aliasing={{0}: (0, {}), {1}: (1, {})} | custom-call | tf_op jit(solution)/shard_map/pallas_call | solution.py:574
Async XLA Ops:
  0.6 5.0 %copy-start.4 = (s32[4,16,256]{2,1,0:T(8,128)S(1)}, s32[4,16,256]{2,1,0:T(8,128)}, u32[]{:S(2)}) copy-start(s32[4,16,256]{2,1,0:T(8,128)} %flags.11) | copy-start | bytes 196612
  0.6 5.0 %copy-start.3 = (s32[4,16,256]{2,1,0:T(8,128)S(1)}, s32[4,16,256]{2,1,0:T(8,128)}, u32[]{:S(2)}) copy-start(s32[4,16,256]{2,1,0:T(8,128)} %solid.11) | copy-start | bytes 196612
  0.7 5.0 %copy-start.2 = (f32[4,16,256]{2,1,0:T(8,128)S(1)}, f32[4,16,256]{2,1,0:T(8,128)}, u32[]{:S(2)}) copy-start(f32[4,16,256]{2,1,0:T(8,128)} %resistance.11) | copy-start | bytes 196612
  0.7 5.0 %copy-start = (f32[19,4,16,256]{3,2,1,0:T(8,128)S(1)}, f32[19,4,16,256]{3,2,1,0:T(8,128)}, u32[]{:S(2)}) copy-start(f32[19,4,16,256]{3,2,1,0:T(8,128)} %adjoint.2) | copy-start | bytes 3735556
  0.7 5.0 %copy-start.1 = (f32[19,4,16,256]{3,2,1,0:T(8,128)S(1)}, f32[19,4,16,256]{3,2,1,0:T(8,128)}, u32[]{:S(2)}) copy-start(f32[19,4,16,256]{3,2,1,0:T(8,128)} %state.2) | copy-start | bytes 3735556
  2.2 8.4 %collective-permute-start.1 = (f32[10,16,256]{2,1,0:T(8,128)S(1)}, f32[10,16,256]{2,1,0:T(8,128)S(1)}, u32[]{:S(2)}, u32[]{:S(2)}) collective-permute-start(f32[10,16,256]{2,1,0:T(8,128)S(1)} %get-tuple-element.26), channel_id=1, source_target_pairs={{0,28},{4,0},{8,4},{12,8},{16,12},{20,16},{24,20},{28,24},{1,29},{... | collective-permute-start | bytes 491528 | tf_op jit(solution)/shard_map/ppermute | solution.py:593
  5.6 5.6 %collective-permute-start = (f32[10,16,256]{2,1,0:T(8,128)S(1)}, f32[10,16,256]{2,1,0:T(8,128)S(1)}, u32[]{:S(2)}, u32[]{:S(2)}) collective-permute-start(f32[10,16,256]{2,1,0:T(8,128)S(1)} %get-tuple-element.23), channel_id=1, source_target_pairs={{0,4},{4,8},{8,12},{12,16},{16,20},{20,24},{24,28},{28,0},{1,5},{5... | collective-permute-start | bytes 491528 | tf_op jit(solution)/shard_map/ppermute | solution.py:593
  6.7 10.1 %collective-permute-start.2 = (f32[27,4,256]{2,1,0:T(4,128)S(1)}, f32[27,4,256]{2,1,0:T(4,128)S(1)}, u32[]{:S(2)}, u32[]{:S(2)}) collective-permute-start(f32[27,4,256]{2,1,0:T(4,128)S(1)} %get-tuple-element.30.refs_0_), channel_id=1, source_target_pairs={{0,1},{1,2},{2,3},{3,0},{4,5},{5,6},{6,7},{7,4},{8,9},{9,10},{10,1... | collective-permute-start | bytes 331784 | tf_op jit(solution)/shard_map/ppermute | solution.py:593
  8.4 8.5 %collective-permute-start.3 = (f32[27,4,256]{2,1,0:T(4,128)S(1)}, f32[27,4,256]{2,1,0:T(4,128)S(1)}, u32[]{:S(2)}, u32[]{:S(2)}) collective-permute-start(f32[27,4,256]{2,1,0:T(4,128)S(1)} %get-tuple-element.31.refs_1_), channel_id=1, source_target_pairs={{0,3},{1,0},{2,1},{3,2},{4,7},{5,4},{6,5},{7,6},{8,11},{9,8},{10,9... | collective-permute-start | bytes 331784 | tf_op jit(solution)/shard_map/ppermute | solution.py:593
  11.4 5.6 %collective-permute-start.4 = (f32[10,2,256]{2,1,0:T(2,128)S(1)}, f32[10,2,256]{2,1,0:T(2,128)S(1)}, u32[]{:S(2)}, u32[]{:S(2)}) collective-permute-start(f32[10,2,256]{2,1,0:T(2,128)S(1)} %get-tuple-element.32.refs_4_), channel_id=1, source_target_pairs={{0,1},{1,2},{2,3},{3,0},{4,5},{5,6},{6,7},{7,4},{8,9},{9,10},{10,1... | collective-permute-start | bytes 61448 | tf_op jit(solution)/shard_map/ppermute | solution.py:593
  13.0 4.0 %collective-permute-start.5 = (f32[10,2,256]{2,1,0:T(2,128)S(1)}, f32[10,2,256]{2,1,0:T(2,128)S(1)}, u32[]{:S(2)}, u32[]{:S(2)}) collective-permute-start(f32[10,2,256]{2,1,0:T(2,128)S(1)} %get-tuple-element.33.refs_5_), channel_id=1, source_target_pairs={{0,3},{1,0},{2,1},{3,2},{4,7},{5,4},{6,5},{7,6},{8,11},{9,8},{10,9... | collective-permute-start | bytes 61448 | tf_op jit(solution)/shard_map/ppermute | solution.py:593
  17.3 4.8 %collective-permute-start.6 = (f32[5,16,256]{2,1,0:T(8,128)S(1)}, f32[5,16,256]{2,1,0:T(8,128)S(1)}, u32[]{:S(2)}, u32[]{:S(2)}) collective-permute-start(f32[5,16,256]{2,1,0:T(8,128)S(1)} %get-tuple-element.42), channel_id=1, source_target_pairs={{0,4},{4,8},{8,12},{12,16},{16,20},{20,24},{24,28},{28,0},{1,5},{5... | collective-permute-start | bytes 245768 | tf_op jit(solution)/shard_map/ppermute | solution.py:593
  17.4 4.8 %collective-permute-start.7 = (f32[5,16,256]{2,1,0:T(8,128)S(1)}, f32[5,16,256]{2,1,0:T(8,128)S(1)}, u32[]{:S(2)}, u32[]{:S(2)}) collective-permute-start(f32[5,16,256]{2,1,0:T(8,128)S(1)} %get-tuple-element.43), channel_id=1, source_target_pairs={{0,28},{4,0},{8,4},{12,8},{16,12},{20,16},{24,20},{28,24},{1,29},{... | collective-permute-start | bytes 245768 | tf_op jit(solution)/shard_map/ppermute | solution.py:593
